TPU v7x, 128 devices: a whole 4x4x4 slice. The times are simulated.
128 devices in a mesh: space: 16 (over y, x), vel: 8 (over z, core).
Axes of the slice: x: 4, y: 4, z: 4, core: 2. Of those that a mesh axis runs over, the one named last changes fastest.
Arguments:
- space_factor: float32 [32, 64, 16, 128], P(None, 'space'), may hold values from -16 to 16
- core_matrix: float32 [32, 32], replicated, may hold values from -0.5 to 3
- velocity_factor: float32 [32, 110592], P(None, 'vel'), may hold values from -5 to 5
- collision_rates: float32 [64, 16, 128], P('space'), may hold values from 0.05 to 0.5
Outputs:
- space_next: float32 [32, 64, 16, 128], P(None, 'space')
- core_next: float32 [32, 32], replicated
- velocity_next: float32 [32, 110592], P(None, 'vel')
All inputs are finite; a program needn't handle non-finite values.
Results may differ from a plain program's by a relative error of at most 0.0003.
Values sent between devices are 32-bit elements; how exact they have to be, the bound alone decides.
No kernel may reach another device: no remote copies, remote signals or barrier semaphores. Data moves between devices by JAX's collectives and lax.ppermute only.
A program may use at most 128 MiB of HBM per device.

v0:
```python
import jax
import jax.numpy as jnp
import numpy as np
from jax import lax
from jax.experimental import pallas as pl
from jax.experimental.pallas import tpu as pltpu
from jax.sharding import PartitionSpec as P

RANK = 32
NVD = 48
SUB = 3
LOW = SUB + 1
HIGH = SUB
NY = 16
NZ = 128
OWN = 4
Q1 = 6
HALF = NVD * NVD // 2
PLANE = NY * NZ
PAD = PLANE + 2 * NZ
WIDE = LOW + OWN + HIGH
INTERPRET = False

f32 = jnp.float32
bf16 = jnp.bfloat16
highest = lax.Precision.HIGHEST


def tables():
    t = np.float32(0.25) * ((2 * np.arange(NVD) + 1).astype(np.float32) / np.float32(NVD) - np.float32(1.0))
    t = t.astype(np.float32)
    shape = np.exp(-(t.astype(np.float64) ** 2) / (2.0 * 0.125 * 0.125))
    shape = shape / shape.mean()
    plus, minus = np.maximum(t, 0), np.minimum(t, 0)
    u2, u3 = np.repeat(t, NVD), np.tile(t, NVD)
    g23 = np.repeat(shape, NVD) * np.tile(shape, NVD)
    sides = [(1, "p"), (2, "p"), (3, "p"), (1, "m"), (2, "m"), (3, "m")]
    names = [()] + [(s,) for s in sides]
    where = {(): 0}
    for k in range(6):
        where[(k,)] = k + 1
    for j in range(6):
        for k in range(j, 6):
            if k != j and sides[j][0] == sides[k][0]:
                continue
            where[(j, k)] = len(names)
            names.append((sides[j], sides[k]))
    base = np.zeros((2, 32, HALF))
    scale = np.zeros((NVD, 128))
    value = {"p": np.maximum, "m": np.minimum}
    for row, name in enumerate(names):
        b = np.ones(NVD * NVD)
        c = np.ones(NVD)
        for d, sign in name:
            if d == 1:
                c = c * value[sign](t.astype(np.float64), 0)
            elif d == 2:
                b = b * value[sign](u2.astype(np.float64), 0)
            else:
                b = b * value[sign](u3.astype(np.float64), 0)
        base[:, row] = b.reshape(2, HALF)
        scale[:, row] = c
    last = len(names)
    base[:, last] = g23.reshape(2, HALF)
    scale[:, last] = shape
    select = np.zeros((32, 7 * 128), np.float32)
    for j in range(7):
        for k in range(7):
            pair = tuple(sorted([i - 1 for i in (j, k) if i > 0]))
            if pair in where:
                select[where[pair], j * 128 + k] = 1.0
    means = np.zeros((8, 128), np.float32)
    means[:, 0] = 1.0
    means[:, 1:4] = (shape * plus).mean()
    means[:, 4:7] = (shape * minus).mean()
    rows = np.zeros((2, 8, HALF), np.float32)
    rows[:, 0] = u2.reshape(2, HALF)
    rows[:, 1] = np.maximum(u3, 0).reshape(2, HALF)
    rows[:, 2] = np.minimum(u3, 0).reshape(2, HALF)
    rows[:, 3] = g23.reshape(2, HALF)
    speeds = np.concatenate([plus, minus, shape]).astype(np.float32)
    return rows, base.astype(np.float32), scale.astype(np.float32), select, means, speeds, last


ROWS, PHI, PHI_SCALE, SELECT, MEANS, SPEEDS, LAST = tables()


def split(x):
    hi = x.astype(bf16)
    return hi, (x - hi.astype(f32)).astype(bf16)


def dot(a, b):
    return jnp.dot(a, b, preferred_element_type=f32)


def dot_t(a, b):
    return lax.dot_general(a, b, (((1,), (1,)), ((), ())), preferred_element_type=f32)


def mm(a, b):
    return jnp.dot(a, b, precision=highest, preferred_element_type=f32)


def mm_t(a, b):
    return lax.dot_general(a, b, (((1,), (1,)), ((), ())), precision=highest, preferred_element_type=f32)


def lanes(shape):
    return lax.broadcasted_iota(jnp.int32, shape, len(shape) - 1)


def sublanes(shape):
    return lax.broadcasted_iota(jnp.int32, shape, len(shape) - 2)


def eye():
    return (lanes((RANK, RANK)) == sublanes((RANK, RANK))).astype(f32)


def call(kernel, outs, ins, args, scratch=(), name=None):
    spaces = {"v": pltpu.VMEM, "s": pltpu.SMEM}
    return pl.pallas_call(
        kernel,
        out_shape=[jax.ShapeDtypeStruct(s, d) for s, d in outs],
        in_specs=[pl.BlockSpec(memory_space=spaces[c]) for c in ins],
        out_specs=[pl.BlockSpec(memory_space=pltpu.VMEM) for _ in outs],
        scratch_shapes=list(scratch),
        compiler_params=pltpu.CompilerParams(vmem_limit_bytes=58 * 1024 * 1024),
        interpret=INTERPRET,
        name=name,
    )(*args)


def point_tiles(first, second, y, positive, extra):
    lane = lanes((RANK, 128))
    middle = (lane >= 32) & (lane < 64)
    tile_a = first + jnp.where(middle, 0.0, second)
    y = jnp.where(lane < 32, y, 0.0)
    y = jnp.where(positive, pltpu.roll(y, 64, 1) if not INTERPRET else jnp.roll(y, 64, 1), y)
    return tile_a, jnp.where(middle, second, 0.0) + y + extra


def roll_lanes(x, shift):
    return jnp.roll(x, shift, 1) if INTERPRET else pltpu.roll(x, shift % x.shape[1], 1)


def stacked(values, rows, h):
    return jnp.concatenate(
        [values, values * rows[h, 0:1, :], values * rows[h, 1:2, :], values * rows[h, 2:3, :]], axis=0
    )


def point_sums_kernel(v_ref, speeds, rows, phi, scale, values, out):
    q0 = v_ref[0] * Q1
    phi_parts = [split(phi[h]) for h in range(2)]

    def body(b, carry):
        sums, y, moments = list(carry[:2]), carry[2], carry[3]
        u = speeds[q0 + b] + speeds[NVD + q0 + b]
        for h in range(2):
            start = pl.multiple_of(b * (2 * HALF) + h * HALF, 128)
            sh, sl = split(stacked(values[:, pl.ds(start, HALF)], rows, h))
            lh, ll = sh[:RANK], sl[:RANK]
            ph, plo = phi_parts[h]
            both = jnp.concatenate([lh, ll], axis=0)
            t = dot_t(both, sh)
            t = t[:RANK] + t[RANK:] + dot_t(lh, sl)
            m = dot_t(both, ph)
            m = m[:RANK] + m[RANK:] + dot_t(lh, plo)
            sums[h] = sums[h] + t
            y = y + u * t
            moments = moments + m * scale[pl.ds(q0 + b, 1), :RANK]
        return sums[0], sums[1], y, moments

    zero = jnp.zeros((RANK, 128), f32)
    first, second, y, moments = lax.fori_loop(0, Q1, body, (zero, zero, zero, jnp.zeros((RANK, RANK), f32)))
    moments = jnp.concatenate([jnp.zeros((RANK, 96), f32), moments], axis=1)
    tile_a, tile_b = point_tiles(first, second, y, v_ref[0] >= 4, moments)
    out[:, :128] = tile_a
    out[:, 128:] = tile_b


def point_sums(v, values):
    return call(
        point_sums_kernel, [((RANK, 256), f32)], "ssvvvv",
        (v, SPEEDS, ROWS, PHI, PHI_SCALE, values), name="point_sums",
    )[0]


def space_sums_kernel(values, below, rates, out, hi, lo, zh, zl, ch, cl):
    for y in range(NY):
        a, b = split(below[pl.ds(y, RANK, stride=NY), :])
        hi[:, y * NZ : (y + 1) * NZ] = a
        lo[:, y * NZ : (y + 1) * NZ] = b

    def load(p, carry):
        for y in range(NY):
            block = values[pl.ds(p * NY + y, RANK, stride=OWN * NY), :]
            at = pl.multiple_of(p * PLANE + y * NZ, 128)
            a, b = split(block)
            hi[:, pl.ds(at + PLANE, NZ)] = a
            lo[:, pl.ds(at + PLANE, NZ)] = b
            a, b = split(roll_lanes(block, 1))
            zh[:, pl.ds(at, NZ)] = a
            zl[:, pl.ds(at, NZ)] = b
            a, b = split(block * rates[pl.ds(p * NY + y, 1), :])
            ch[:, pl.ds(at, NZ)] = a
            cl[:, pl.ds(at, NZ)] = b
        return carry

    lax.fori_loop(0, OWN, load, 0)

    def body(p, carry):
        t, c = carry
        at = pl.multiple_of(p * PLANE, 128)

        def stack(main, turned):
            here = main[:, pl.ds(at + PLANE, PLANE)]
            wrapped = jnp.concatenate([here[:, PLANE - NZ :], here[:, : PLANE - NZ]], axis=1)
            return jnp.concatenate(
                [here, main[:, pl.ds(at, PLANE)], wrapped, turned[:, pl.ds(at, PLANE)]], axis=0
            )

        sh, sl = stack(hi, zh), stack(lo, zl)
        both = jnp.concatenate([sh[:RANK], sl[:RANK]], axis=0)
        part = dot_t(both, sh)
        t = t + part[:RANK] + part[RANK:] + dot_t(sh[:RANK], sl)
        part = dot_t(both, ch[:, pl.ds(at, PLANE)])
        c = c + part[:RANK] + part[RANK:] + dot_t(sh[:RANK], cl[:, pl.ds(at, PLANE)])
        return t, c

    t, c = lax.fori_loop(0, OWN, body, (jnp.zeros((RANK, 128), f32), jnp.zeros((RANK, RANK), f32)))
    out[:, :128] = t
    out[:, 128:] = jnp.concatenate([c, jnp.zeros((RANK, 96), f32)], axis=1)


def space_sums(values, below, rates):
    own = (RANK, OWN * PLANE)
    return call(
        space_sums_kernel, [((RANK, 256), f32)], "vvv", (values, below, rates),
        [pltpu.VMEM((RANK, (OWN + 1) * PLANE), bf16)] * 2 + [pltpu.VMEM(own, bf16)] * 4, name="space_sums",
    )[0]


def factor_pair(first, second):
    zeros = jnp.zeros((RANK, 64), f32)
    works = [jnp.concatenate([g, eye(), zeros], axis=1) for g in (first, second)]
    row = sublanes((RANK, 128))
    for k in range(RANK):
        for n in range(2):
            w = works[n]
            scale = lax.rsqrt(w[k : k + 1, k : k + 1])
            lead = w[k : k + 1, :] * scale
            column = w[:, k : k + 1] * scale
            works[n] = jnp.where(row > k, w - column * lead, jnp.where(row == k, lead, w))
    return [(w[:, :RANK], w[:, RANK : 2 * RANK]) for w in works]


def transposed(x):
    return mm_t(eye(), x)


def point_blocks(tiles, points_total):
    t = tiles * (1.0 / points_total)
    gram = t[:, 0:32]
    plus = [t[:, 192:224], t[:, 160:192], t[:, 64:96]]
    minus = [t[:, 128:160], t[:, 32:64], t[:, 96:128]]
    return gram, plus, minus, t[:, 224:256]


def congruent(inverse, blocks):
    inverse_t = transposed(inverse)
    half = mm(jnp.concatenate(blocks, axis=0), inverse_t)
    return [mm(inverse, half[k * RANK : (k + 1) * RANK]) for k in range(len(blocks))]


def small_first_kernel(cells_total, points_total, space, point, core, select, means, wk, wl, src):
    s = space[...] * (1.0 / cells_total)
    gram = s[:, 0:32]
    gram_v, plus, minus, raw = point_blocks(point[...], points_total)
    (upper, inverse), (upper_v, inverse_v) = factor_pair(gram, gram_v)
    identity = eye()
    raw_a = [gram - s[:, 32 * (d + 1) : 32 * (d + 2)] for d in range(3)]
    to_spread = mm(upper, core[...])
    to_kinetic_t = mm_t(core[...], upper_v)
    zeros = jnp.zeros((RANK, 32), f32)
    inverse_t = transposed(inverse)
    triple = jnp.concatenate([inverse_t] * 3 + [zeros], axis=1)
    left = (
        [mm(inverse, s[:, 128:160])] + [mm(inverse, a) for a in raw_a] + [mm_t(inverse, a) for a in raw_a]
    )
    turned = mm(jnp.concatenate(left, axis=0), triple)
    one = jnp.concatenate([identity] * 3 + [zeros], axis=1)
    e_wide = turned[:RANK]
    mixers = [one - e_wide] + [-turned[RANK * (d + 1) : RANK * (d + 2)] for d in range(3)]
    mixers = mixers + [turned[RANK * (d + 4) : RANK * (d + 5)] for d in range(3)]
    stack = jnp.concatenate(mixers, axis=0)
    wl[1] = stack
    wl[0] = mm(stack[:, :RANK], jnp.concatenate([to_spread] * 3 + [zeros], axis=1))
    square = [m[:, :RANK] for m in mixers]
    e = e_wide[:, :RANK]
    moved = mm(mm(to_spread, raw), select[...])
    groups = [moved[:, 128 * j : 128 * (j + 1)] for j in range(7)]
    lane = lanes((RANK, 128))
    source = [mm(e, groups[0])[:, 0:1]]
    following = mm(square[0], groups[0]) + source[0] * means[0:1, :]
    for j in range(1, 7):
        following = following + mm(square[j], groups[j])
    source.append(mm(e, following)[:, 0:1])
    third = mm(square[0], jnp.where(lane == 0, following, 0.0))
    for j in range(1, 7):
        third = third + mm(square[j], jnp.where(lane == j, following, 0.0))
    third = jnp.sum(third, axis=1, keepdims=True) + source[1] * means[0:1, 0:1]
    source.append(mm(e, jnp.broadcast_to(third, (RANK, 128)))[:, 0:1])
    for n in range(3):
        src[n] = jnp.where((lane >= 96) & (lane < 99), source[n], 0.0)
    flux = congruent(inverse_v, plus + minus)
    turned_raw = mm(inverse_v, raw)
    weights = turned_raw[:, 0:1]
    moments_row = transposed(turned_raw)[LAST : LAST + 1, :]
    center = identity
    blocks = []
    for d in range(3):
        center = center - flux[d] + flux[d + 3]
        blocks += [flux[d], -flux[d + 3]]
    blocks = [center] + blocks
    relax_t = weights * moments_row - identity
    empty = jnp.zeros((RANK, 6 * RANK), f32)
    for kind in range(2):
        if kind == 0:
            parts = [mm(to_kinetic_t, block) for block in blocks]
            relax = mm(to_kinetic_t, relax_t)
        else:
            parts, relax = blocks, relax_t
        wk[kind, :RANK, :] = transposed(jnp.concatenate(parts, axis=0))
        wk[kind, RANK:, :] = jnp.concatenate([transposed(relax), empty], axis=1)


def small_first(space, point, core, cells_total, points_total):
    def kernel(*refs):
        small_first_kernel(cells_total, points_total, *refs)

    return call(
        kernel, [((2, 64, 224), f32), ((2, 224, 128), f32), ((3, RANK, 128), f32)], "vvvvv",
        (space, point, core, SELECT, MEANS), name="small_first",
    )


def evolve_point_kernel(v_ref, speeds, rows, wl, src, values, new, out):
    q0 = v_ref[0] * Q1
    lane_w = lanes((RANK, 128))
    low_lane = ((lane_w >= 64) & (lane_w < 96)) | (lane_w == 97)

    def weights_of(w):
        hi = w.astype(bf16).astype(f32)
        return jnp.where(low_lane, w - hi, hi).astype(bf16)

    def piece(kind, n):
        return wl[kind, n * RANK : (n + 1) * RANK, :]

    fixed = [
        [jnp.concatenate([weights_of(piece(kind, n)) for n in ((5, 3, 6) if h == 0 else (2, 3, 6))], axis=0) for h in range(2)]
        for kind in range(2)
    ]
    tops = []
    aux = []
    for h in range(2):
        gh, gl = split(rows[h, 3:4, :])
        row = sublanes((16, HALF))
        gh, gl = gh.astype(f32), gl.astype(f32)
        tops.append(jnp.where(row < 2, gh, jnp.where(row == 2, gl, 0.0)).astype(bf16))
        aux.append(jnp.where(row == 0, 1.0, jnp.where(row == 1, gh, jnp.where(row == 2, gl, 0.0))).astype(bf16))

    def body(b, carry):
        sums, y, cross, ones_sum = list(carry[:2]), carry[2], carry[3], carry[4]
        up = speeds[q0 + b]
        um = speeds[NVD + q0 + b]
        g1 = speeds[2 * NVD + q0 + b]
        u = up + um
        moving = [piece(kind, 0) + up * piece(kind, 1) + um * piece(kind, 4) for kind in range(2)]
        heads = [weights_of(moving[min(n, 1)] + g1 * src[n]) for n in range(3)]
        for h in range(2):
            start = pl.multiple_of(b * (2 * HALF) + h * HALF, 128)
            state = values[:, pl.ds(start, HALF)]
            raw_hi, raw_lo = split(state)
            hi, lo = raw_hi, raw_lo
            for n in range(SUB):
                if n > 0:
                    hi, lo = split(state)
                w = jnp.concatenate([heads[n], fixed[min(n, 1)][h]], axis=0)[:, :112]
                mixed = dot(w, jnp.concatenate([hi, lo, hi, tops[h]], axis=0))
                state = (
                    mixed[:RANK]
                    + rows[h, 0:1, :] * mixed[RANK : 2 * RANK]
                    + rows[h, 1:2, :] * mixed[2 * RANK : 3 * RANK]
                    + rows[h, 2:3, :] * mixed[3 * RANK :]
                )
            new[:, pl.ds(start, HALF)] = state
            sh, sl = split(stacked(state, rows, h))
            lh, ll = sh[:RANK], sl[:RANK]
            t = dot_t(jnp.concatenate([lh, ll, aux[h]], axis=0), sh)
            t2 = dot_t(jnp.concatenate([lh, aux[h]], axis=0), sl)
            t_main = t[:RANK] + t[RANK : 2 * RANK] + t2[:RANK]
            cross_part = dot_t(jnp.concatenate([lh, ll], axis=0), raw_hi)
            cross = cross + cross_part[:RANK] + cross_part[RANK:] + dot_t(lh, raw_lo)
            a = t[2 * RANK : 2 * RANK + 8]
            a2 = t2[RANK : RANK + 8]
            row8 = sublanes((8, 128))
            a = a + jnp.where(row8 < 2, a2, 0.0)
            ones_sum = ones_sum + jnp.where(row8 == 0, a, a * g1)
            sums[h] = sums[h] + t_main
            y = y + u * t_main
        return sums[0], sums[1], y, cross, ones_sum

    zero = jnp.zeros((RANK, 128), f32)
    first, second, y, cross, ones_sum = lax.fori_loop(
        0, Q1, body, (zero, zero, zero, jnp.zeros((RANK, RANK), f32), jnp.zeros((8, 128), f32))
    )
    cross = jnp.concatenate([jnp.zeros((RANK, 96), f32), cross], axis=1)
    tile_a, tile_b = point_tiles(first, second, y, v_ref[0] >= 4, cross)
    out[:RANK, :128] = tile_a
    out[:RANK, 128:] = tile_b
    out[RANK:, :128] = ones_sum
    out[RANK:, 128:] = jnp.zeros((8, 128), f32)


def evolve_point(v, wl, src, values):
    return call(
        evolve_point_kernel, [(values.shape, f32), ((RANK + 8, 256), f32)], "ssvvvv",
        (v, SPEEDS, ROWS, wl, src, values), name="evolve_point",
    )


CHUNK = 512


def evolve_space_kernel(wk, values, below3, below1, above3, rates, rates_below, rates_above, new, out, raw_hi, raw_lo, rates_all, ch, cl, *bufs):
    rates_all[: (LOW - 1) * NY, :] = rates_below[...]
    rates_all[(LOW - 1) * NY : (LOW - 1 + OWN) * NY, :] = rates[...]
    rates_all[(LOW - 1 + OWN) * NY :, :] = rates_above[...]
    sets = [bufs[0:6], bufs[6:12]]

    def store(dst, t, y, block, rolled):
        hi, lo, mh, ml, ph, plo = dst
        at = pl.multiple_of(t * PAD + (y + 1) * NZ, 128)
        a, b = split(block)
        hi[:, pl.ds(at, NZ)] = a
        lo[:, pl.ds(at, NZ)] = b
        if y == 0:
            other = pl.multiple_of(t * PAD + (NY + 1) * NZ, 128)
            hi[:, pl.ds(other, NZ)] = a
            lo[:, pl.ds(other, NZ)] = b
        if y == NY - 1:
            other = pl.multiple_of(t * PAD, 128)
            hi[:, pl.ds(other, NZ)] = a
            lo[:, pl.ds(other, NZ)] = b
        if rolled:
            c, d = split(roll_lanes(block, 1))
            mh[:, pl.ds(at, NZ)] = c
            ml[:, pl.ds(at, NZ)] = d
        if rolled == 2:
            c, d = split(roll_lanes(block, -1))
            ph[:, pl.ds(at, NZ)] = c
            plo[:, pl.ds(at, NZ)] = d
        return a, b

    def fill(source, planes, first, keep):
        def load(p, carry):
            for y in range(NY):
                block = source[pl.ds(p * NY + y, RANK, stride=planes * NY), :]
                a, b = store(sets[0], p + first, y, block, 2)
                if keep:
                    at = pl.multiple_of(p * PLANE + y * NZ, 128)
                    raw_hi[:, pl.ds(at, NZ)] = a
                    raw_lo[:, pl.ds(at, NZ)] = b
            return carry

        lax.fori_loop(0, planes, load, 0)

    fill(below3, LOW - 1, 0, False)
    fill(below1, 1, LOW - 1, False)
    fill(values, OWN, LOW, True)
    fill(above3, HIGH, LOW + OWN, False)

    for n in range(SUB):
        whi, wlo = split(wk[min(n, 1)])
        wboth = jnp.concatenate([whi, wlo], axis=0)
        src, dst = sets[n % 2], sets[(n + 1) % 2]
        final = n == SUB - 1

        def step(t, carry, src=src, dst=dst, whi=whi, wboth=wboth, final=final):
            for c in range(PLANE // CHUNK):
                at = pl.multiple_of(t * PAD + NZ + c * CHUNK, 128)

                def stack(main, minus, plus):
                    return jnp.concatenate(
                        [
                            main[:, pl.ds(at, CHUNK)],
                            main[:, pl.ds(pl.multiple_of(at - PAD, 128), CHUNK)],
                            main[:, pl.ds(pl.multiple_of(at + PAD, 128), CHUNK)],
                            main[:, pl.ds(pl.multiple_of(at - NZ, 128), CHUNK)],
                            main[:, pl.ds(pl.multiple_of(at + NZ, 128), CHUNK)],
                            minus[:, pl.ds(at, CHUNK)],
                            plus[:, pl.ds(at, CHUNK)],
                        ],
                        axis=0,
                    )

                mixed = dot(wboth, stack(src[0], src[2], src[4]))
                mixed = mixed[:64] + mixed[64:] + dot(whi, stack(src[1], src[3], src[5]))
                for i in range(CHUNK // NZ):
                    y = c * (CHUNK // NZ) + i
                    cell = slice(i * NZ, (i + 1) * NZ)
                    rate = rates_all[pl.ds((t - 1) * NY + y, 1), :]
                    block = mixed[:RANK, cell] + rate * mixed[RANK:, cell]
                    store(dst, t, y, block, 1 if final else 2)
                    if final:
                        spot = pl.multiple_of((t - LOW + 1) * PLANE + y * NZ, 128)
                        new[:, pl.ds(spot, NZ)] = block
                        a, b = split(block * rate)
                        ch[:, pl.ds(spot, NZ)] = a
                        cl[:, pl.ds(spot, NZ)] = b
            return carry

        lax.fori_loop(1 + n, WIDE - 1 - n, step, 0)

    done = sets[SUB % 2]

    def body(p, carry):
        t, c = carry
        at = pl.multiple_of((p + LOW) * PAD + NZ, 128)
        own = pl.multiple_of(p * PLANE, 128)
        spot = pl.multiple_of((p + 1) * PLANE, 128)

        def stack(main, minus):
            return jnp.concatenate(
                [
                    main[:, pl.ds(at, PLANE)],
                    main[:, pl.ds(pl.multiple_of(at - PAD, 128), PLANE)],
                    main[:, pl.ds(pl.multiple_of(at - NZ, 128), PLANE)],
                    minus[:, pl.ds(at, PLANE)],
                ],
                axis=0,
            )

        sh, sl = stack(done[0], done[2]), stack(done[1], done[3])
        both = jnp.concatenate([sh[:RANK], sl[:RANK]], axis=0)
        part = dot_t(both, sh)
        t = t + part[:RANK] + part[RANK:] + dot_t(sh[:RANK], sl)
        oh = jnp.concatenate([ch[:, pl.ds(spot, PLANE)], raw_hi[:, pl.ds(own, PLANE)]], axis=0)
        ol = jnp.concatenate([cl[:, pl.ds(spot, PLANE)], raw_lo[:, pl.ds(own, PLANE)]], axis=0)
        part = dot_t(both, oh)
        c = c + part[:RANK] + part[RANK:] + dot_t(sh[:RANK], ol)
        return t, c

    t, c = lax.fori_loop(0, OWN, body, (jnp.zeros((RANK, 128), f32), jnp.zeros((RANK, 64), f32)))
    out[:, :128] = t
    out[:, 128:] = jnp.concatenate([c, jnp.zeros((RANK, 64), f32)], axis=1)


def evolve_space(wk, values, below3, below1, above3, rates, rates_below, rates_above):
    return call(
        evolve_space_kernel, [((RANK, (OWN + 1) * PLANE), f32), ((RANK, 256), f32)], "vvvvvvvv",
        (wk, values, below3, below1, above3, rates, rates_below, rates_above),
        [pltpu.VMEM((RANK, OWN * PLANE), bf16)] * 2
        + [pltpu.VMEM(((WIDE - 2) * NY, NZ), f32)]
        + [pltpu.VMEM((RANK, (OWN + 1) * PLANE), bf16)] * 2
        + [pltpu.VMEM((RANK, WIDE * PAD), bf16)] * 12,
        name="evolve_space",
    )


def finish_kernel(cells_total, points_total, space, point, core, kinetic, spread, fresh_space, fresh_core, fresh_point):
    s = space[...] * (1.0 / cells_total)
    gram = s[:, 0:32]
    gram_v, plus, minus, cross_v = point_blocks(point[:RANK, :], points_total)
    (_, inverse), (_, inverse_v) = factor_pair(gram, gram_v)
    zeros = jnp.zeros((RANK, 32), f32)
    lane = lanes((RANK, 128))

    def wide(matrix):
        w = jnp.concatenate([matrix] * 3 + [zeros], axis=1)
        hi = w.astype(bf16).astype(f32)
        return jnp.where((lane >= 64) & (lane < 96), w - hi, hi).astype(bf16)[:, :96]

    w_space, w_point = wide(inverse), wide(inverse_v)

    def out_space(p, carry):
        for half in range(2):
            size = PLANE // 2
            at = pl.multiple_of((p + 1) * PLANE + half * size, 128)
            hi, lo = split(kinetic[:, pl.ds(at, size)])
            made = dot(w_space, jnp.concatenate([hi, lo, hi], axis=0))
            for y in range(NY // 2):
                fresh_space[pl.ds(p * NY + half * (NY // 2) + y, RANK, stride=OWN * NY), :] = made[:, y * NZ : (y + 1) * NZ]
        return carry

    lax.fori_loop(0, OWN, out_space, 0)

    def out_point(i, carry):
        at = pl.multiple_of(i * HALF, 128)
        hi, lo = split(spread[:, pl.ds(at, HALF)])
        fresh_point[:, pl.ds(at, HALF)] = dot(w_point, jnp.concatenate([hi, lo, hi], axis=0))
        return carry

    lax.fori_loop(0, 2 * Q1, out_point, 0)

    inverse_t = transposed(inverse)
    inverse_vt = transposed(inverse_v)
    aux = mm(point[RANK:, 0:32] * (1.0 / points_total), inverse_vt)
    weights_row = aux[0:1, :]
    moments_row = aux[1:2, :] + aux[2:3, :]
    raw_a = [gram - s[:, 32 * (d + 1) : 32 * (d + 2)] for d in range(3)]
    space_half = mm(jnp.concatenate(raw_a + [s[:, 128:160]], axis=0), inverse_t)
    a = [mm(inverse, space_half[d * RANK : (d + 1) * RANK]) for d in range(4)]
    e = a[3]
    a_t = [transposed(a[d]) for d in range(3)]
    flux = congruent(inverse_v, plus + minus)
    left = mm(inverse, s[:, 160:192])
    right = mm(inverse_v, cross_v)
    current = mm_t(mm(left, core[...]), right)
    for _ in range(SUB):
        scaled = mm(e, current)
        change = -scaled + jnp.sum(scaled * weights_row, axis=1, keepdims=True) * moments_row
        for d in range(3):
            change = change - mm(mm(a[d], current), flux[d]) + mm(mm(a_t[d], current), flux[d + 3])
        current = current + change
    fresh_core[...] = current


def finish(space, point, core, kinetic, spread, cells_total, points_total):
    def kernel(*refs):
        finish_kernel(cells_total, points_total, *refs)

    return call(
        kernel, [((RANK * OWN * NY, NZ), f32), ((RANK, RANK), f32), (spread.shape, f32)], "vvvvv",
        (space, point, core, kinetic, spread), name="finish",
    )


def axis_sum(values, axis, routes):
    moved = [lax.ppermute(values, axis, route) for route in routes]
    if len(moved) == 1:
        return values + moved[0]
    return (values + moved[1]) + (moved[0] + moved[2])


def routes_x():
    return [[(4 * y + x, 4 * y + (x + d) % 4) for y in range(4) for x in range(4)] for d in (1, 2, 3)]


def routes_y():
    return [[(4 * y + x, 4 * ((y + d) % 4) + x) for y in range(4) for x in range(4)] for d in (1, 2, 3)]


def routes_z():
    return [[(2 * z + c, 2 * ((z + d) % 4) + c) for z in range(4) for c in range(2)] for d in (1, 2, 3)]


def routes_core():
    return [[(2 * z + c, 2 * z + 1 - c) for z in range(4) for c in range(2)]]


def total(space_part, point_part):
    space_part = axis_sum(space_part, "space", routes_x())
    point_part = axis_sum(point_part, "vel", routes_z())
    space_part = axis_sum(space_part, "space", routes_y())
    point_part = axis_sum(point_part, "vel", routes_core())
    return space_part, point_part


def per_device(space_factor, core_matrix, velocity_factor, collision_rates):
    devices = lax.axis_size("space")
    up = [(i, (i + 1) % devices) for i in range(devices)]
    down = [((i + 1) % devices, i) for i in range(devices)]
    below1 = lax.ppermute(space_factor[:, OWN - 1 :], "space", up).reshape(-1, NZ)
    below3 = lax.ppermute(space_factor[:, : OWN - 1], "space", up).reshape(-1, NZ)
    above3 = lax.ppermute(space_factor[:, :HIGH], "space", down).reshape(-1, NZ)
    rates_below = lax.ppermute(collision_rates[1:], "space", up).reshape(-1, NZ)
    rates_above = lax.ppermute(collision_rates[: HIGH - 1], "space", down).reshape(-1, NZ)
    rates = collision_rates.reshape(-1, NZ)
    values = space_factor.reshape(-1, NZ)
    cells_total = OWN * PLANE * devices
    points_total = velocity_factor.shape[1] * lax.axis_size("vel")
    v = lax.axis_index("vel").astype(jnp.int32).reshape(1)

    point = point_sums(v, velocity_factor)
    space = space_sums(values, below1, rates)
    space, point = total(space, point)
    wk, wl, src = small_first(space, point, core_matrix, cells_total, points_total)
    spread, point = evolve_point(v, wl, src, velocity_factor)
    kinetic, space = evolve_space(wk, values, below3, below1, above3, rates, rates_below, rates_above)
    space, point = total(space, point)
    fresh_space, fresh_core, fresh_point = finish(
        space, point, core_matrix, kinetic, spread, cells_total, points_total
    )
    return fresh_space.reshape(space_factor.shape), fresh_core, fresh_point


def solution(mesh):
    return jax.shard_map(
        per_device,
        mesh=mesh,
        in_specs=(P(None, "space", None, None), P(), P(None, "vel"), P("space", None, None)),
        out_specs=(P(None, "space", None, None), P(), P(None, "vel")),
        check_vma=False,
    )
```

profile of v0, /device:TPU:30, one launch (start us, length us, event | category | flops | bytes accessed | tf_op | source)
XLA Modules:
  0.0 127.0 jit_solution(8500335829671818024)
XLA Ops:
  0.6 0.0 copy-start
  0.6 1.1 slice.13
  1.7 0.1 collective-permute-start
  1.8 6.5 %point_sums.1 = f32[32,256]{1,0:T(8,128)} custom-call(s32[1]{0:T(128)} %bitcast.3.v_ref, f32[144]{0:T(256)} %constant.16.clone.speeds, f32[2,8,1152]{2,1,0:T(8,128)} %constant.17.clone.rows, f32[2,32,1152]{2,1,0:T(8,128)} %constant.18.clone.phi, f32[48,128]{1,0:T(8,128)} %constant.19.clone.scale, f32[32,13824]{1,0:T(8,128)} %values.3), custom_call_target="tpu_custom_call" | custom-call | tf_op jit(solution)/shard_map/point_sums/pallas_call | solution.py:123
  8.3 4.2 %collective-permute-start.9 = (f32[32,256]{1,0:T(8,128)}, f32[32,256]{1,0:T(8,128)S(1)}, u32[]{:S(2)}, u32[]{:S(2)}) collective-permute-start(f32[32,256]{1,0:T(8,128)} %point_sums.1), channel_id=1, source_target_pairs={{0,6},{1,7},{2,0},{3,1},{4,2},{5,3},{6,4},{7,5},{8,14},{9,15},{10,... | collective-permute-start | bytes 98312 | tf_op jit(solution)/shard_map/ppermute | solution.py:643
  12.5 0.0 collective-permute-start.8
  12.5 1.8 %collective-permute-start.7 = (f32[32,256]{1,0:T(8,128)}, f32[32,256]{1,0:T(8,128)S(1)}, u32[]{:S(2)}, u32[]{:S(2)}) collective-permute-start(f32[32,256]{1,0:T(8,128)} %point_sums.1), channel_id=1, source_target_pairs={{0,4},{1,5},{2,6},{3,7},{4,0},{5,1},{6,2},{7,3},{8,12},{9,13},{10,... | collective-permute-start | bytes 98312 | tf_op jit(solution)/shard_map/ppermute | solution.py:643
  14.3 0.1 slice.14
  14.4 2.0 %collective-permute-start.12 = (f32[32,3,16,128]{3,2,1,0:T(8,128)S(1)}, f32[32,3,16,128]{3,2,1,0:T(8,128)S(1)}, u32[]{:S(2)}, u32[]{:S(2)}) collective-permute-start(f32[32,3,16,128]{3,2,1,0:T(8,128)S(1)} %slice.14), channel_id=1, source_target_pairs={{8,0},{16,8},{24,16},{32,24},{40,32},{48,40},{56,48},{64,56},{72,6... | collective-permute-start | bytes 2359304 | tf_op jit(solution)/shard_map/ppermute | solution.py:679
  16.4 0.0 collective-permute-done
  16.4 3.5 %collective-permute-start.11 = (f32[32,3,16,128]{3,2,1,0:T(8,128)S(1)}, f32[32,3,16,128]{3,2,1,0:T(8,128)S(1)}, u32[]{:S(2)}, u32[]{:S(2)}) collective-permute-start(f32[32,3,16,128]{3,2,1,0:T(8,128)S(1)} %slice.14), channel_id=1, source_target_pairs={{0,8},{8,16},{16,24},{24,32},{32,40},{40,48},{48,56},{56,64},{64,7... | collective-permute-start | bytes 2359304 | tf_op jit(solution)/shard_map/ppermute | solution.py:678
  19.8 5.4 %space_sums.1 = f32[32,256]{1,0:T(8,128)} custom-call(f32[2048,128]{1,0:T(8,128)} %bitcast.9, f32[512,128]{1,0:T(8,128)} %bitcast.11, f32[64,128]{1,0:T(8,128)} %bitcast.15), custom_call_target="tpu_custom_call" | custom-call | tf_op jit(solution)/shard_map/space_sums/pallas_call | solution.py:123
  25.3 0.0 collective-permute-done.9
  25.3 0.0 collective-permute-start.3
  25.3 0.0 collective-permute-done.8
  25.3 3.2 %collective-permute-start.2 = (f32[32,256]{1,0:T(8,128)}, f32[32,256]{1,0:T(8,128)S(1)}, u32[]{:S(2)}, u32[]{:S(2)}) collective-permute-start(f32[32,256]{1,0:T(8,128)} %space_sums.1), channel_id=1, source_target_pairs={{0,8},{8,16},{16,24},{24,0},{32,40},{40,48},{48,56},{56,32},{64,72... | collective-permute-start | bytes 98312 | tf_op jit(solution)/shard_map/ppermute | solution.py:643
  28.5 0.0 collective-permute-done.7
  28.5 0.0 collective-permute-start.1
  28.5 8.0 %collective-permute-done.3 = f32[32,256]{1,0:T(8,128)S(1)} collective-permute-done((f32[32,256]{1,0:T(8,128)}, f32[32,256]{1,0:T(8,128)S(1)}, u32[]{:S(2)}, u32[]{:S(2)}) %collective-permute-start.3) | collective-permute-done | bytes 32800 | tf_op jit(solution)/shard_map/ppermute | solution.py:643
  36.5 0.0 collective-permute-start.10
  36.5 0.4 collective-permute-done.2
  36.9 0.0 collective-permute-done.1
  36.9 0.8 add_add_fusion.5
  37.7 0.5 collective-permute-start.6
  38.2 2.8 %collective-permute-start.5 = (f32[32,256]{1,0:T(8,128)S(1)}, f32[32,256]{1,0:T(8,128)S(1)}, u32[]{:S(2)}, u32[]{:S(2)}) collective-permute-start(f32[32,256]{1,0:T(8,128)S(1)} %add_add_fusion.5), channel_id=1, source_target_pairs={{0,32},{8,40},{16,48},{24,56},{32,64},{40,72},{48,80},{56,88},{64,... | collective-permute-start | bytes 98312 | tf_op jit(solution)/shard_map/ppermute | solution.py:643
  41.0 0.0 collective-permute-done.10
  41.0 0.0 collective-permute-start.4
  41.0 0.6 add.69.refs_1_
  41.6 1.2 collective-permute-done.6
  42.9 0.4 collective-permute-start.14
  43.3 0.0 collective-permute-done.5
  43.3 5.8 %collective-permute-start.13 = (f32[3,16,128]{2,1,0:T(8,128)S(1)}, f32[3,16,128]{2,1,0:T(8,128)S(1)}, u32[]{:S(2)}, u32[]{:S(2)}) collective-permute-start(f32[3,16,128]{2,1,0:T(8,128)S(1)} %slice.15), channel_id=1, source_target_pairs={{0,8},{8,16},{16,24},{24,32},{32,40},{40,48},{48,56},{56,64},{64,7... | collective-permute-start | bytes 73736 | tf_op jit(solution)/shard_map/ppermute | solution.py:680
  49.2 0.0 collective-permute-done.4
  49.2 0.6 add_add_fusion.4.refs_0_
  49.8 8.0 %small_first.1 = (f32[2,64,224]{2,1,0:T(8,128)}, f32[2,224,128]{2,1,0:T(8,128)}, f32[3,32,128]{2,1,0:T(8,128)}) custom-call(f32[32,256]{1,0:T(8,128)} %add_add_fusion.4.refs_0_, f32[32,256]{1,0:T(8,128)} %add.69.refs_1_, f32[32,32]{1,0:T(8,128)} %refs_2_.3, f32[32,896]{1,0:T(8,128)} %constant.20.clone.refs_3_, f32[8,128]{1,0:T(8,128)} %constant.21.clone.refs_4_), custom_call_target="tpu_custom_call" | custom-call | tf_op jit(solution)/shard_map/small_first/pallas_call | solution.py:123
  57.8 12.8 %evolve_point.1 = (f32[32,13824]{1,0:T(8,128)}, f32[40,256]{1,0:T(8,128)}) custom-call(s32[1]{0:T(128)} %bitcast.3.v_ref, f32[144]{0:T(256)} %constant.16.clone.speeds, f32[2,8,1152]{2,1,0:T(8,128)} %constant.17.clone.rows, f32[2,224,128]{2,1,0:T(8,128)} %get-tuple-element.15.wl, f32[3,32,128]{2,1,0:T(8,128)} %get-tuple-element.16.src, f32[32,13824]{1,0:T(8,128)} %values.3), custom_call_target="tpu_custom_call" | custom-call | tf_op jit(solution)/shard_map/evolve_point/pallas_call | solution.py:123
  70.6 1.6 %collective-permute-start.23 = (f32[40,256]{1,0:T(8,128)}, f32[40,256]{1,0:T(8,128)S(1)}, u32[]{:S(2)}, u32[]{:S(2)}) collective-permute-start(f32[40,256]{1,0:T(8,128)} %get-tuple-element.17), channel_id=1, source_target_pairs={{0,6},{1,7},{2,0},{3,1},{4,2},{5,3},{6,4},{7,5},{8,14},{9,15},{10,... | collective-permute-start | bytes 122888 | tf_op jit(solution)/shard_map/ppermute | solution.py:643
  72.2 0.0 collective-permute-done.14
  72.2 0.7 collective-permute-start.22
  72.9 0.0 collective-permute-done.13
  72.9 2.3 %collective-permute-start.21 = (f32[40,256]{1,0:T(8,128)}, f32[40,256]{1,0:T(8,128)S(1)}, u32[]{:S(2)}, u32[]{:S(2)}) collective-permute-start(f32[40,256]{1,0:T(8,128)} %get-tuple-element.17), channel_id=1, source_target_pairs={{0,4},{1,5},{2,6},{3,7},{4,0},{5,1},{6,2},{7,3},{8,12},{9,13},{10,... | collective-permute-start | bytes 122888 | tf_op jit(solution)/shard_map/ppermute | solution.py:643
  75.1 0.0 collective-permute-done.12
  75.1 0.0 collective-permute-done.11
  75.1 0.0 copy-start.3
  75.2 0.8 copy-done.2
  76.0 0.3 copy-done.3
  76.3 19.4 %evolve_space.1 = (f32[32,10240]{1,0:T(8,128)}, f32[32,256]{1,0:T(8,128)}) custom-call(f32[2,64,224]{2,1,0:T(8,128)} %get-tuple-element.13.wk, f32[2048,128]{1,0:T(8,128)} %bitcast.10, f32[1536,128]{1,0:T(8,128)} %bitcast.14, f32[512,128]{1,0:T(8,128)} %bitcast.12, f32[1536,128]{1,0:T(8,128)} %bitcast.13, f32[64,128]{1,0:T(8,128)} %bitcast.16, ...), custom_call_target="tpu_custom_call" | custom-call | tf_op jit(solution)/shard_map/evolve_space/pallas_call | solution.py:123
  95.7 0.0 collective-permute-start.17
  95.7 3.2 %collective-permute-start.16 = (f32[32,256]{1,0:T(8,128)}, f32[32,256]{1,0:T(8,128)S(1)}, u32[]{:S(2)}, u32[]{:S(2)}) collective-permute-start(f32[32,256]{1,0:T(8,128)} %get-tuple-element.14), channel_id=1, source_target_pairs={{0,8},{8,16},{16,24},{24,0},{32,40},{40,48},{48,56},{56,32},{64,72... | collective-permute-start | bytes 98312 | tf_op jit(solution)/shard_map/ppermute | solution.py:643
  98.9 0.0 collective-permute-done.23
  98.9 0.0 collective-permute-start.15
  99.0 0.0 collective-permute-done.22
  99.0 0.0 collective-permute-done.21
  99.0 0.1 collective-permute-start.24
  99.1 2.0 %collective-permute-done.17 = f32[32,256]{1,0:T(8,128)S(1)} collective-permute-done((f32[32,256]{1,0:T(8,128)}, f32[32,256]{1,0:T(8,128)S(1)}, u32[]{:S(2)}, u32[]{:S(2)}) %collective-permute-start.17) | collective-permute-done | bytes 32800 | tf_op jit(solution)/shard_map/ppermute | solution.py:643
  101.0 3.5 %collective-permute-done.15 = f32[32,256]{1,0:T(8,128)S(1)} collective-permute-done((f32[32,256]{1,0:T(8,128)}, f32[32,256]{1,0:T(8,128)S(1)}, u32[]{:S(2)}, u32[]{:S(2)}) %collective-permute-start.15) | collective-permute-done | bytes 32800 | tf_op jit(solution)/shard_map/ppermute | solution.py:643
  104.6 0.8 add_add_fusion.2
  105.3 0.1 collective-permute-start.20
  105.4 3.2 %collective-permute-start.19 = (f32[32,256]{1,0:T(8,128)S(1)}, f32[32,256]{1,0:T(8,128)S(1)}, u32[]{:S(2)}, u32[]{:S(2)}) collective-permute-start(f32[32,256]{1,0:T(8,128)S(1)} %add_add_fusion.2), channel_id=1, source_target_pairs={{0,32},{8,40},{16,48},{24,56},{32,64},{40,72},{48,80},{56,88},{64,... | collective-permute-start | bytes 98312 | tf_op jit(solution)/shard_map/ppermute | solution.py:643
  108.7 0.6 add.79.refs_1_
  109.3 1.3 collective-permute-done.20
  110.5 3.5 %collective-permute-done.18 = f32[32,256]{1,0:T(8,128)S(1)} collective-permute-done((f32[32,256]{1,0:T(8,128)S(1)}, f32[32,256]{1,0:T(8,128)S(1)}, u32[]{:S(2)}, u32[]{:S(2)}) %collective-permute-start.18) | collective-permute-done | bytes 32800 | tf_op jit(solution)/shard_map/ppermute | solution.py:643
  114.1 0.6 add_add_fusion.1.refs_0_
  114.7 12.3 %finish.1 = (f32[2048,128]{1,0:T(8,128)}, f32[32,32]{1,0:T(8,128)}, f32[32,13824]{1,0:T(8,128)}) custom-call(f32[32,256]{1,0:T(8,128)} %add_add_fusion.1.refs_0_, f32[40,256]{1,0:T(8,128)} %add.79.refs_1_, f32[32,32]{1,0:T(8,128)} %refs_2_.3, f32[32,10240]{1,0:T(8,128)} %get-tuple-element.18.refs_3_, f32[32,13824]{1,0:T(8,128)} %get-tuple-element.19.refs_4_), custom_call_target="tpu_custom_call" | custom-call | tf_op jit(solution)/shard_map/finish/pallas_call | solution.py:123
  (22 shorter events, 0.1 us)
Async XLA Ops:
  0.6 13.7 %copy-start = (f32[32,4,16,128]{3,2,1,0:T(8,128)S(1)}, f32[32,4,16,128]{3,2,1,0:T(8,128)}, u32[]{:S(2)}) copy-start(f32[32,4,16,128]{3,2,1,0:T(8,128)} %param.10) | copy-start | bytes 3145732
  1.7 14.7 %collective-permute-start = (f32[32,1,16,128]{3,2,1,0:T(8,128)S(1)}, f32[32,1,16,128]{3,2,1,0:T(8,128)S(1)}, u32[]{:S(2)}, u32[]{:S(2)}) collective-permute-start(f32[32,1,16,128]{3,2,1,0:T(8,128)S(1)} %slice.13), channel_id=1, source_target_pairs={{0,8},{8,16},{16,24},{24,32},{32,40},{40,48},{48,56},{56,64},{64,7... | collective-permute-start | bytes 786440 | tf_op jit(solution)/shard_map/ppermute | solution.py:677
  8.3 20.2 %copy-start.5 = (f32[32,256]{1,0:T(8,128)S(1)}, f32[32,256]{1,0:T(8,128)}, u32[]{:S(2)}) copy-start(f32[32,256]{1,0:T(8,128)} %point_sums.1) | copy-start | bytes 98308
  8.3 32.7 %copy-start.4 = (f32[4,16,128]{2,1,0:T(8,128)S(1)}, f32[4,16,128]{2,1,0:T(8,128)}, u32[]{:S(2)}) copy-start(f32[4,16,128]{2,1,0:T(8,128)} %param.13) | copy-start | bytes 98308
  8.3 17.0 %collective-permute-start.9 = (f32[32,256]{1,0:T(8,128)}, f32[32,256]{1,0:T(8,128)S(1)}, u32[]{:S(2)}, u32[]{:S(2)}) collective-permute-start(f32[32,256]{1,0:T(8,128)} %point_sums.1), channel_id=1, source_target_pairs={{0,6},{1,7},{2,0},{3,1},{4,2},{5,3},{6,4},{7,5},{8,14},{9,15},{10,... | collective-permute-start | bytes 98312 | tf_op jit(solution)/shard_map/ppermute | solution.py:643
  12.5 12.8 %collective-permute-start.8 = (f32[32,256]{1,0:T(8,128)}, f32[32,256]{1,0:T(8,128)S(1)}, u32[]{:S(2)}, u32[]{:S(2)}) collective-permute-start(f32[32,256]{1,0:T(8,128)} %point_sums.1), channel_id=1, source_target_pairs={{0,2},{1,3},{2,4},{3,5},{4,6},{5,7},{6,0},{7,1},{8,10},{9,11},{10,... | collective-permute-start | bytes 98312 | tf_op jit(solution)/shard_map/ppermute | solution.py:643
  12.5 16.0 %collective-permute-start.7 = (f32[32,256]{1,0:T(8,128)}, f32[32,256]{1,0:T(8,128)S(1)}, u32[]{:S(2)}, u32[]{:S(2)}) collective-permute-start(f32[32,256]{1,0:T(8,128)} %point_sums.1), channel_id=1, source_target_pairs={{0,4},{1,5},{2,6},{3,7},{4,0},{5,1},{6,2},{7,3},{8,12},{9,13},{10,... | collective-permute-start | bytes 98312 | tf_op jit(solution)/shard_map/ppermute | solution.py:643
  14.4 60.7 %collective-permute-start.12 = (f32[32,3,16,128]{3,2,1,0:T(8,128)S(1)}, f32[32,3,16,128]{3,2,1,0:T(8,128)S(1)}, u32[]{:S(2)}, u32[]{:S(2)}) collective-permute-start(f32[32,3,16,128]{3,2,1,0:T(8,128)S(1)} %slice.14), channel_id=1, source_target_pairs={{8,0},{16,8},{24,16},{32,24},{40,32},{48,40},{56,48},{64,56},{72,6... | collective-permute-start | bytes 2359304 | tf_op jit(solution)/shard_map/ppermute | solution.py:679
  16.4 3.5 %copy-start.1 = (f32[32,1,16,128]{3,2,1,0:T(8,128)}, f32[32,1,16,128]{3,2,1,0:T(8,128)S(1)}, u32[]{:S(2)}) copy-start(f32[32,1,16,128]{3,2,1,0:T(8,128)S(1)} %collective-permute-done) | copy-start | bytes 786436
  16.4 58.8 %collective-permute-start.11 = (f32[32,3,16,128]{3,2,1,0:T(8,128)S(1)}, f32[32,3,16,128]{3,2,1,0:T(8,128)S(1)}, u32[]{:S(2)}, u32[]{:S(2)}) collective-permute-start(f32[32,3,16,128]{3,2,1,0:T(8,128)S(1)} %slice.14), channel_id=1, source_target_pairs={{0,8},{8,16},{16,24},{24,32},{32,40},{40,48},{48,56},{56,64},{64,7... | collective-permute-start | bytes 2359304 | tf_op jit(solution)/shard_map/ppermute | solution.py:678
  25.3 11.2 %collective-permute-start.3 = (f32[32,256]{1,0:T(8,128)}, f32[32,256]{1,0:T(8,128)S(1)}, u32[]{:S(2)}, u32[]{:S(2)}) collective-permute-start(f32[32,256]{1,0:T(8,128)} %space_sums.1), channel_id=1, source_target_pairs={{0,24},{8,0},{16,8},{24,16},{32,56},{40,32},{48,40},{56,48},{64,88... | collective-permute-start | bytes 98312 | tf_op jit(solution)/shard_map/ppermute | solution.py:643
  25.3 11.6 %collective-permute-start.2 = (f32[32,256]{1,0:T(8,128)}, f32[32,256]{1,0:T(8,128)S(1)}, u32[]{:S(2)}, u32[]{:S(2)}) collective-permute-start(f32[32,256]{1,0:T(8,128)} %space_sums.1), channel_id=1, source_target_pairs={{0,8},{8,16},{16,24},{24,0},{32,40},{40,48},{48,56},{56,32},{64,72... | collective-permute-start | bytes 98312 | tf_op jit(solution)/shard_map/ppermute | solution.py:643
  28.5 8.4 %collective-permute-start.1 = (f32[32,256]{1,0:T(8,128)}, f32[32,256]{1,0:T(8,128)S(1)}, u32[]{:S(2)}, u32[]{:S(2)}) collective-permute-start(f32[32,256]{1,0:T(8,128)} %space_sums.1), channel_id=1, source_target_pairs={{0,16},{8,24},{16,0},{24,8},{32,48},{40,56},{48,32},{56,40},{64,80... | collective-permute-start | bytes 98312 | tf_op jit(solution)/shard_map/ppermute | solution.py:643
  36.5 4.5 %collective-permute-start.10 = (f32[32,256]{1,0:T(8,128)S(1)}, f32[32,256]{1,0:T(8,128)S(1)}, u32[]{:S(2)}, u32[]{:S(2)}) collective-permute-start(f32[32,256]{1,0:T(8,128)S(1)} %add_add_fusion.3), channel_id=1, source_target_pairs={{0,1},{1,0},{2,3},{3,2},{4,5},{5,4},{6,7},{7,6},{8,9},{9,8},{10,11... | collective-permute-start | bytes 98312 | tf_op jit(solution)/shard_map/ppermute | solution.py:643
  37.7 5.2 %collective-permute-start.6 = (f32[32,256]{1,0:T(8,128)S(1)}, f32[32,256]{1,0:T(8,128)S(1)}, u32[]{:S(2)}, u32[]{:S(2)}) collective-permute-start(f32[32,256]{1,0:T(8,128)S(1)} %add_add_fusion.5), channel_id=1, source_target_pairs={{0,96},{8,104},{16,112},{24,120},{32,0},{40,8},{48,16},{56,24},{64... | collective-permute-start | bytes 98312 | tf_op jit(solution)/shard_map/ppermute | solution.py:643
  38.2 5.2 %collective-permute-start.5 = (f32[32,256]{1,0:T(8,128)S(1)}, f32[32,256]{1,0:T(8,128)S(1)}, u32[]{:S(2)}, u32[]{:S(2)}) collective-permute-start(f32[32,256]{1,0:T(8,128)S(1)} %add_add_fusion.5), channel_id=1, source_target_pairs={{0,32},{8,40},{16,48},{24,56},{32,64},{40,72},{48,80},{56,88},{64,... | collective-permute-start | bytes 98312 | tf_op jit(solution)/shard_map/ppermute | solution.py:643
  41.0 8.2 %collective-permute-start.4 = (f32[32,256]{1,0:T(8,128)S(1)}, f32[32,256]{1,0:T(8,128)S(1)}, u32[]{:S(2)}, u32[]{:S(2)}) collective-permute-start(f32[32,256]{1,0:T(8,128)S(1)} %add_add_fusion.5), channel_id=1, source_target_pairs={{0,64},{8,72},{16,80},{24,88},{32,96},{40,104},{48,112},{56,120},{... | collective-permute-start | bytes 98312 | tf_op jit(solution)/shard_map/ppermute | solution.py:643
  42.9 29.3 %collective-permute-start.14 = (f32[2,16,128]{2,1,0:T(8,128)S(1)}, f32[2,16,128]{2,1,0:T(8,128)S(1)}, u32[]{:S(2)}, u32[]{:S(2)}) collective-permute-start(f32[2,16,128]{2,1,0:T(8,128)S(1)} %slice.16), channel_id=1, source_target_pairs={{8,0},{16,8},{24,16},{32,24},{40,32},{48,40},{56,48},{64,56},{72,6... | collective-permute-start | bytes 49160 | tf_op jit(solution)/shard_map/ppermute | solution.py:681
  43.3 29.5 %collective-permute-start.13 = (f32[3,16,128]{2,1,0:T(8,128)S(1)}, f32[3,16,128]{2,1,0:T(8,128)S(1)}, u32[]{:S(2)}, u32[]{:S(2)}) collective-permute-start(f32[3,16,128]{2,1,0:T(8,128)S(1)} %slice.15), channel_id=1, source_target_pairs={{0,8},{8,16},{16,24},{24,32},{32,40},{40,48},{48,56},{56,64},{64,7... | collective-permute-start | bytes 73736 | tf_op jit(solution)/shard_map/ppermute | solution.py:680
  70.6 28.4 %copy-start.6 = (f32[40,256]{1,0:T(8,128)S(1)}, f32[40,256]{1,0:T(8,128)}, u32[]{:S(2)}) copy-start(f32[40,256]{1,0:T(8,128)} %get-tuple-element.17) | copy-start | bytes 122884
  70.6 28.4 %collective-permute-start.23 = (f32[40,256]{1,0:T(8,128)}, f32[40,256]{1,0:T(8,128)S(1)}, u32[]{:S(2)}, u32[]{:S(2)}) collective-permute-start(f32[40,256]{1,0:T(8,128)} %get-tuple-element.17), channel_id=1, source_target_pairs={{0,6},{1,7},{2,0},{3,1},{4,2},{5,3},{6,4},{7,5},{8,14},{9,15},{10,... | collective-permute-start | bytes 122888 | tf_op jit(solution)/shard_map/ppermute | solution.py:643
  72.2 3.0 %copy-start.8 = (f32[2,16,128]{2,1,0:T(8,128)}, f32[2,16,128]{2,1,0:T(8,128)S(1)}, u32[]{:S(2)}) copy-start(f32[2,16,128]{2,1,0:T(8,128)S(1)} %collective-permute-done.14) | copy-start | bytes 49156
  72.2 26.7 %collective-permute-start.22 = (f32[40,256]{1,0:T(8,128)}, f32[40,256]{1,0:T(8,128)S(1)}, u32[]{:S(2)}, u32[]{:S(2)}) collective-permute-start(f32[40,256]{1,0:T(8,128)} %get-tuple-element.17), channel_id=1, source_target_pairs={{0,2},{1,3},{2,4},{3,5},{4,6},{5,7},{6,0},{7,1},{8,10},{9,11},{10,... | collective-permute-start | bytes 122888 | tf_op jit(solution)/shard_map/ppermute | solution.py:643
  72.9 2.3 %copy-start.7 = (f32[3,16,128]{2,1,0:T(8,128)}, f32[3,16,128]{2,1,0:T(8,128)S(1)}, u32[]{:S(2)}) copy-start(f32[3,16,128]{2,1,0:T(8,128)S(1)} %collective-permute-done.13) | copy-start | bytes 73732
  72.9 26.1 %collective-permute-start.21 = (f32[40,256]{1,0:T(8,128)}, f32[40,256]{1,0:T(8,128)S(1)}, u32[]{:S(2)}, u32[]{:S(2)}) collective-permute-start(f32[40,256]{1,0:T(8,128)} %get-tuple-element.17), channel_id=1, source_target_pairs={{0,4},{1,5},{2,6},{3,7},{4,0},{5,1},{6,2},{7,3},{8,12},{9,13},{10,... | collective-permute-start | bytes 122888 | tf_op jit(solution)/shard_map/ppermute | solution.py:643
  75.1 0.9 copy-start.2
  75.1 1.1 copy-start.3
  95.7 5.3 %collective-permute-start.17 = (f32[32,256]{1,0:T(8,128)}, f32[32,256]{1,0:T(8,128)S(1)}, u32[]{:S(2)}, u32[]{:S(2)}) collective-permute-start(f32[32,256]{1,0:T(8,128)} %get-tuple-element.14), channel_id=1, source_target_pairs={{0,24},{8,0},{16,8},{24,16},{32,56},{40,32},{48,40},{56,48},{64,88... | collective-permute-start | bytes 98312 | tf_op jit(solution)/shard_map/ppermute | solution.py:643
  95.7 5.3 %collective-permute-start.16 = (f32[32,256]{1,0:T(8,128)}, f32[32,256]{1,0:T(8,128)S(1)}, u32[]{:S(2)}, u32[]{:S(2)}) collective-permute-start(f32[32,256]{1,0:T(8,128)} %get-tuple-element.14), channel_id=1, source_target_pairs={{0,8},{8,16},{16,24},{24,0},{32,40},{40,48},{48,56},{56,32},{64,72... | collective-permute-start | bytes 98312 | tf_op jit(solution)/shard_map/ppermute | solution.py:643
  98.9 5.6 %collective-permute-start.15 = (f32[32,256]{1,0:T(8,128)}, f32[32,256]{1,0:T(8,128)S(1)}, u32[]{:S(2)}, u32[]{:S(2)}) collective-permute-start(f32[32,256]{1,0:T(8,128)} %get-tuple-element.14), channel_id=1, source_target_pairs={{0,16},{8,24},{16,0},{24,8},{32,48},{40,56},{48,32},{56,40},{64,80... | collective-permute-start | bytes 98312 | tf_op jit(solution)/shard_map/ppermute | solution.py:643
  99.0 9.7 %collective-permute-start.24 = (f32[40,256]{1,0:T(8,128)S(1)}, f32[40,256]{1,0:T(8,128)S(1)}, u32[]{:S(2)}, u32[]{:S(2)}) collective-permute-start(f32[40,256]{1,0:T(8,128)S(1)} %add_add_fusion), channel_id=1, source_target_pairs={{0,1},{1,0},{2,3},{3,2},{4,5},{5,4},{6,7},{7,6},{8,9},{9,8},{10,11... | collective-permute-start | bytes 122888 | tf_op jit(solution)/shard_map/ppermute | solution.py:643
  105.3 5.2 %collective-permute-start.20 = (f32[32,256]{1,0:T(8,128)S(1)}, f32[32,256]{1,0:T(8,128)S(1)}, u32[]{:S(2)}, u32[]{:S(2)}) collective-permute-start(f32[32,256]{1,0:T(8,128)S(1)} %add_add_fusion.2), channel_id=1, source_target_pairs={{0,96},{8,104},{16,112},{24,120},{32,0},{40,8},{48,16},{56,24},{64... | collective-permute-start | bytes 98312 | tf_op jit(solution)/shard_map/ppermute | solution.py:643
  105.4 5.1 %collective-permute-start.19 = (f32[32,256]{1,0:T(8,128)S(1)}, f32[32,256]{1,0:T(8,128)S(1)}, u32[]{:S(2)}, u32[]{:S(2)}) collective-permute-start(f32[32,256]{1,0:T(8,128)S(1)} %add_add_fusion.2), channel_id=1, source_target_pairs={{0,32},{8,40},{16,48},{24,56},{32,64},{40,72},{48,80},{56,88},{64,... | collective-permute-start | bytes 98312 | tf_op jit(solution)/shard_map/ppermute | solution.py:643
  108.7 5.4 %collective-permute-start.18 = (f32[32,256]{1,0:T(8,128)S(1)}, f32[32,256]{1,0:T(8,128)S(1)}, u32[]{:S(2)}, u32[]{:S(2)}) collective-permute-start(f32[32,256]{1,0:T(8,128)S(1)} %add_add_fusion.2), channel_id=1, source_target_pairs={{0,64},{8,72},{16,80},{24,88},{32,96},{40,104},{48,112},{56,120},{... | collective-permute-start | bytes 98312 | tf_op jit(solution)/shard_map/ppermute | solution.py:643
where the time goes:
time: 127 us
  Pallas kernels  64.4 us (51%)
  starting transfers between devices  35.5 us (28%)
  waiting for transfers between devices  19.9 us (16%)
  other arithmetic  4.03 us (3%)
  local copies, waits for them, and re-layouts  2.26 us (2%)
    pallas_call x6, Pallas kernels, call(): pl.pallas_call(kernel, out_shape=[jax.ShapeDtypeStruct(s, d) for s, d in...  64.4 us
    ppermute x20, starting transfers between devices, axis_sum(): moved = [lax.ppermute(values, axis, route) for route in routes]  23.7 us
    ppermute x20, waiting for transfers between devices, axis_sum(): moved = [lax.ppermute(values, axis, route) for route in routes]  19.9 us
    ppermute x1, starting transfers between devices, per_device(): rates_below = lax.ppermute(collision_rates[1:], 'space', up).reshape(-1, NZ)  5.82 us
    ppermute x1, starting transfers between devices, per_device(): lax.ppermute(space_factor[:, :OWN - 1], 'space', up).reshape(-1, NZ)  3.45 us
    add x6, other arithmetic, axis_sum(): return values + moved[1] + (moved[0] + moved[2])  2.8 us
  transfers between devices with their start and end apart: 25, of which 7 were waited for; matrix products, arithmetic and copies ran while one was open for 3% of the time, Pallas kernels for 41%

commit v1 on v0

--- a/solution.py
+++ b/solution.py
@@ -119,7 +119,7 @@
 
 
 def call(kernel, outs, ins, args, scratch=(), name=None):
-    spaces = {"v": pltpu.VMEM, "s": pltpu.SMEM}
+    spaces = {"v": pltpu.VMEM, "s": pltpu.SMEM, "a": pl.ANY}
     return pl.pallas_call(
         kernel,
         out_shape=[jax.ShapeDtypeStruct(s, d) for s, d in outs],
@@ -151,7 +151,7 @@
     )
 
 
-def point_sums_kernel(v_ref, speeds, rows, phi, scale, values, out):
+def point_sums_kernel(v_ref, speeds, rows, phi, scale, values, after, out):
     q0 = v_ref[0] * Q1
     phi_parts = [split(phi[h]) for h in range(2)]
 
@@ -181,19 +181,14 @@
     out[:, 128:] = tile_b
 
 
-def point_sums(v, values):
+def point_sums(v, values, after):
     return call(
-        point_sums_kernel, [((RANK, 256), f32)], "ssvvvv",
-        (v, SPEEDS, ROWS, PHI, PHI_SCALE, values), name="point_sums",
+        point_sums_kernel, [((RANK, 256), f32)], "ssvvvva",
+        (v, SPEEDS, ROWS, PHI, PHI_SCALE, values, after), name="point_sums",
     )[0]
 
 
-def space_sums_kernel(values, below, rates, out, hi, lo, zh, zl, ch, cl):
-    for y in range(NY):
-        a, b = split(below[pl.ds(y, RANK, stride=NY), :])
-        hi[:, y * NZ : (y + 1) * NZ] = a
-        lo[:, y * NZ : (y + 1) * NZ] = b
-
+def space_sums_kernel(values, rates, out, hi, lo, zh, zl, ch, cl):
     def load(p, carry):
         for y in range(NY):
             block = values[pl.ds(p * NY + y, RANK, stride=OWN * NY), :]
@@ -209,6 +204,8 @@
             cl[:, pl.ds(at, NZ)] = b
         return carry
 
+    hi[:, :PLANE] = jnp.zeros((RANK, PLANE), bf16)
+    lo[:, :PLANE] = jnp.zeros((RANK, PLANE), bf16)
     lax.fori_loop(0, OWN, load, 0)
 
     def body(p, carry):
@@ -235,26 +232,53 @@
     out[:, 128:] = jnp.concatenate([c, jnp.zeros((RANK, 96), f32)], axis=1)
 
 
-def space_sums(values, below, rates):
+def space_sums(values, rates):
     own = (RANK, OWN * PLANE)
     return call(
-        space_sums_kernel, [((RANK, 256), f32)], "vvv", (values, below, rates),
+        space_sums_kernel, [((RANK, 256), f32)], "vv", (values, rates),
         [pltpu.VMEM((RANK, (OWN + 1) * PLANE), bf16)] * 2 + [pltpu.VMEM(own, bf16)] * 4, name="space_sums",
     )[0]
+
+
+def edge_sums_kernel(values, below, inner, out):
+    t = jnp.zeros((RANK, 64), f32)
+    empty = jnp.zeros((RANK, PLANE), bf16)
+    first = jnp.concatenate([values[pl.ds(y, RANK, stride=OWN * NY), :] for y in range(NY)], axis=1)
+    other = jnp.concatenate([below[pl.ds(y, RANK, stride=NY), :] for y in range(NY)], axis=1)
+    lh, ll = split(first)
+    oh, ol = split(other)
+    part = dot_t(jnp.concatenate([lh, ll], axis=0), jnp.concatenate([empty, oh], axis=0))
+    t = part[:RANK] + part[RANK:] + dot_t(lh, jnp.concatenate([empty, ol], axis=0))
+    out[:, :128] = inner[:, :128] + jnp.concatenate([t, jnp.zeros((RANK, 64), f32)], axis=1)
+    out[:, 128:] = inner[:, 128:]
+
+
+def edge_sums(values, below, inner):
+    return call(edge_sums_kernel, [((RANK, 256), f32)], "vvv", (values, below, inner), name="edge_sums")[0]
 
 
 def factor_pair(first, second):
     zeros = jnp.zeros((RANK, 64), f32)
     works = [jnp.concatenate([g, eye(), zeros], axis=1) for g in (first, second)]
+    pivots = [jnp.ones((RANK, 128), f32)] * 2
     row = sublanes((RANK, 128))
-    for k in range(RANK):
+    for k in range(0, RANK, 2):
         for n in range(2):
             w = works[n]
-            scale = lax.rsqrt(w[k : k + 1, k : k + 1])
-            lead = w[k : k + 1, :] * scale
-            column = w[:, k : k + 1] * scale
-            works[n] = jnp.where(row > k, w - column * lead, jnp.where(row == k, lead, w))
-    return [(w[:, :RANK], w[:, RANK : 2 * RANK]) for w in works]
+            c0 = jnp.broadcast_to(w[:, k : k + 1], (RANK, 128))
+            c1 = jnp.broadcast_to(w[:, k + 1 : k + 2], (RANK, 128))
+            r0, r1 = w[k : k + 1, :], w[k + 1 : k + 2, :]
+            a, b, d = c0[k : k + 1, :], c1[k : k + 1, :], c1[k + 1 : k + 2, :]
+            over = 1.0 / a
+            ratio = b * over
+            d = d - b * ratio
+            r1 = r1 - ratio * r0
+            c1 = c1 - ratio * c0
+            step = w - c0 * (r0 * over) - c1 * (r1 * (1.0 / d))
+            works[n] = jnp.where(row > k + 1, step, jnp.where(row == k + 1, r1, w))
+            pivots[n] = jnp.where(row == k, a, jnp.where(row == k + 1, d, pivots[n]))
+    done = [works[n] * lax.rsqrt(pivots[n]) for n in range(2)]
+    return [(w[:, :RANK], w[:, RANK : 2 * RANK]) for w in done]
 
 
 def transposed(x):
@@ -275,10 +299,15 @@
     return [mm(inverse, half[k * RANK : (k + 1) * RANK]) for k in range(len(blocks))]
 
 
-def small_first_kernel(cells_total, points_total, space, point, core, select, means, wk, wl, src):
-    s = space[...] * (1.0 / cells_total)
+def four(parts):
+    return (parts[0][...] + parts[2][...]) + (parts[1][...] + parts[3][...])
+
+
+def small_first_kernel(cells_total, points_total, p0, p1, p2, p3, core, select, means, after, wk, wl, src):
+    both = four((p0, p1, p2, p3))
+    s = both[:RANK] * (1.0 / cells_total)
     gram = s[:, 0:32]
-    gram_v, plus, minus, raw = point_blocks(point[...], points_total)
+    gram_v, plus, minus, raw = point_blocks(both[RANK:], points_total)
     (upper, inverse), (upper_v, inverse_v) = factor_pair(gram, gram_v)
     identity = eye()
     raw_a = [gram - s[:, 32 * (d + 1) : 32 * (d + 2)] for d in range(3)]
@@ -337,17 +366,17 @@
         wk[kind, RANK:, :] = jnp.concatenate([transposed(relax), empty], axis=1)
 
 
-def small_first(space, point, core, cells_total, points_total):
+def small_first(parts, core, after, cells_total, points_total):
     def kernel(*refs):
         small_first_kernel(cells_total, points_total, *refs)
 
     return call(
-        kernel, [((2, 64, 224), f32), ((2, 224, 128), f32), ((3, RANK, 128), f32)], "vvvvv",
-        (space, point, core, SELECT, MEANS), name="small_first",
-    )
-
-
-def evolve_point_kernel(v_ref, speeds, rows, wl, src, values, new, out):
+        kernel, [((2, 64, 224), f32), ((2, 224, 128), f32), ((3, RANK, 128), f32)], "vvvvvvva",
+        (*parts, core, SELECT, MEANS, after), name="small_first",
+    )
+
+
+def evolve_point_kernel(v_ref, speeds, rows, wl, src, values, after, new, out):
     q0 = v_ref[0] * Q1
     lane_w = lanes((RANK, 128))
     low_lane = ((lane_w >= 64) & (lane_w < 96)) | (lane_w == 97)
@@ -425,68 +454,74 @@
     out[RANK:, 128:] = jnp.zeros((8, 128), f32)
 
 
-def evolve_point(v, wl, src, values):
+def evolve_point(v, wl, src, values, after):
     return call(
-        evolve_point_kernel, [(values.shape, f32), ((RANK + 8, 256), f32)], "ssvvvv",
-        (v, SPEEDS, ROWS, wl, src, values), name="evolve_point",
+        evolve_point_kernel, [(values.shape, f32), ((RANK + 8, 256), f32)], "ssvvvva",
+        (v, SPEEDS, ROWS, wl, src, values, after), name="evolve_point",
     )
 
 
 CHUNK = 512
 
 
-def evolve_space_kernel(wk, values, below3, below1, above3, rates, rates_below, rates_above, new, out, raw_hi, raw_lo, rates_all, ch, cl, *bufs):
-    rates_all[: (LOW - 1) * NY, :] = rates_below[...]
-    rates_all[(LOW - 1) * NY : (LOW - 1 + OWN) * NY, :] = rates[...]
-    rates_all[(LOW - 1 + OWN) * NY :, :] = rates_above[...]
-    sets = [bufs[0:6], bufs[6:12]]
-
-    def store(dst, t, y, block, rolled):
-        hi, lo, mh, ml, ph, plo = dst
-        at = pl.multiple_of(t * PAD + (y + 1) * NZ, 128)
-        a, b = split(block)
-        hi[:, pl.ds(at, NZ)] = a
-        lo[:, pl.ds(at, NZ)] = b
-        if y == 0:
-            other = pl.multiple_of(t * PAD + (NY + 1) * NZ, 128)
-            hi[:, pl.ds(other, NZ)] = a
-            lo[:, pl.ds(other, NZ)] = b
-        if y == NY - 1:
-            other = pl.multiple_of(t * PAD, 128)
-            hi[:, pl.ds(other, NZ)] = a
-            lo[:, pl.ds(other, NZ)] = b
-        if rolled:
-            c, d = split(roll_lanes(block, 1))
-            mh[:, pl.ds(at, NZ)] = c
-            ml[:, pl.ds(at, NZ)] = d
-        if rolled == 2:
-            c, d = split(roll_lanes(block, -1))
-            ph[:, pl.ds(at, NZ)] = c
-            plo[:, pl.ds(at, NZ)] = d
-        return a, b
-
-    def fill(source, planes, first, keep):
+def store(dst, t, y, block, rolled):
+    hi, lo, mh, ml, ph, plo = dst
+    at = pl.multiple_of(t * PAD + (y + 1) * NZ, 128)
+    a, b = split(block)
+    hi[:, pl.ds(at, NZ)] = a
+    lo[:, pl.ds(at, NZ)] = b
+    if y == 0:
+        other = pl.multiple_of(t * PAD + (NY + 1) * NZ, 128)
+        hi[:, pl.ds(other, NZ)] = a
+        lo[:, pl.ds(other, NZ)] = b
+    if y == NY - 1:
+        other = pl.multiple_of(t * PAD, 128)
+        hi[:, pl.ds(other, NZ)] = a
+        lo[:, pl.ds(other, NZ)] = b
+    if rolled:
+        c, d = split(roll_lanes(block, 1))
+        mh[:, pl.ds(at, NZ)] = c
+        ml[:, pl.ds(at, NZ)] = d
+    if rolled == 2:
+        c, d = split(roll_lanes(block, -1))
+        ph[:, pl.ds(at, NZ)] = c
+        plo[:, pl.ds(at, NZ)] = d
+
+
+def fill_kernel(values, below3, below1, above3, after, *dst):
+    def fill(source, planes, first):
         def load(p, carry):
             for y in range(NY):
-                block = source[pl.ds(p * NY + y, RANK, stride=planes * NY), :]
-                a, b = store(sets[0], p + first, y, block, 2)
-                if keep:
-                    at = pl.multiple_of(p * PLANE + y * NZ, 128)
-                    raw_hi[:, pl.ds(at, NZ)] = a
-                    raw_lo[:, pl.ds(at, NZ)] = b
+                store(dst, p + first, y, source[pl.ds(p * NY + y, RANK, stride=planes * NY), :], 2)
             return carry
 
         lax.fori_loop(0, planes, load, 0)
 
-    fill(below3, LOW - 1, 0, False)
-    fill(below1, 1, LOW - 1, False)
-    fill(values, OWN, LOW, True)
-    fill(above3, HIGH, LOW + OWN, False)
+    fill(below3, LOW - 1, 0)
+    fill(below1, 1, LOW - 1)
+    fill(values, OWN, LOW)
+    fill(above3, HIGH, LOW + OWN)
+
+
+def fill_planes(values, below3, below1, above3, after):
+    return call(
+        fill_kernel, [((RANK, WIDE * PAD), bf16)] * 6, "vvvva", (values, below3, below1, above3, after), name="fill_planes",
+    )
+
+
+def evolve_space_kernel(wk, *refs):
+    raw = refs[0:6]
+    rates, rates_below, rates_above, new, out, rates_all, ch, cl = refs[6:14]
+    sets = [raw, refs[14:20], refs[20:26]]
+    order = [0, 1, 2, 1]
+    rates_all[: (LOW - 1) * NY, :] = rates_below[RANK * (LOW - 1) * NY :, :]
+    rates_all[(LOW - 1) * NY : (LOW - 1 + OWN) * NY, :] = rates[...]
+    rates_all[(LOW - 1 + OWN) * NY :, :] = rates_above[RANK * HIGH * NY : RANK * HIGH * NY + (HIGH - 1) * NY, :]
 
     for n in range(SUB):
         whi, wlo = split(wk[min(n, 1)])
         wboth = jnp.concatenate([whi, wlo], axis=0)
-        src, dst = sets[n % 2], sets[(n + 1) % 2]
+        src, dst = sets[order[n]], sets[order[n + 1]]
         final = n == SUB - 1
 
         def step(t, carry, src=src, dst=dst, whi=whi, wboth=wboth, final=final):
@@ -525,12 +560,11 @@
 
         lax.fori_loop(1 + n, WIDE - 1 - n, step, 0)
 
-    done = sets[SUB % 2]
+    done = sets[order[SUB]]
 
     def body(p, carry):
         t, c = carry
         at = pl.multiple_of((p + LOW) * PAD + NZ, 128)
-        own = pl.multiple_of(p * PLANE, 128)
         spot = pl.multiple_of((p + 1) * PLANE, 128)
 
         def stack(main, minus):
@@ -548,8 +582,8 @@
         both = jnp.concatenate([sh[:RANK], sl[:RANK]], axis=0)
         part = dot_t(both, sh)
         t = t + part[:RANK] + part[RANK:] + dot_t(sh[:RANK], sl)
-        oh = jnp.concatenate([ch[:, pl.ds(spot, PLANE)], raw_hi[:, pl.ds(own, PLANE)]], axis=0)
-        ol = jnp.concatenate([cl[:, pl.ds(spot, PLANE)], raw_lo[:, pl.ds(own, PLANE)]], axis=0)
+        oh = jnp.concatenate([ch[:, pl.ds(spot, PLANE)], raw[0][:, pl.ds(at, PLANE)]], axis=0)
+        ol = jnp.concatenate([cl[:, pl.ds(spot, PLANE)], raw[1][:, pl.ds(at, PLANE)]], axis=0)
         part = dot_t(both, oh)
         c = c + part[:RANK] + part[RANK:] + dot_t(sh[:RANK], ol)
         return t, c
@@ -559,22 +593,22 @@
     out[:, 128:] = jnp.concatenate([c, jnp.zeros((RANK, 64), f32)], axis=1)
 
 
-def evolve_space(wk, values, below3, below1, above3, rates, rates_below, rates_above):
+def evolve_space(wk, filled, rates, rates_below, rates_above):
     return call(
-        evolve_space_kernel, [((RANK, (OWN + 1) * PLANE), f32), ((RANK, 256), f32)], "vvvvvvvv",
-        (wk, values, below3, below1, above3, rates, rates_below, rates_above),
-        [pltpu.VMEM((RANK, OWN * PLANE), bf16)] * 2
-        + [pltpu.VMEM(((WIDE - 2) * NY, NZ), f32)]
+        evolve_space_kernel, [((RANK, (OWN + 1) * PLANE), f32), ((RANK, 256), f32)], "v" * 10,
+        (wk, *filled, rates, rates_below, rates_above),
+        [pltpu.VMEM(((WIDE - 2) * NY, NZ), f32)]
         + [pltpu.VMEM((RANK, (OWN + 1) * PLANE), bf16)] * 2
         + [pltpu.VMEM((RANK, WIDE * PAD), bf16)] * 12,
         name="evolve_space",
     )
 
 
-def finish_kernel(cells_total, points_total, space, point, core, kinetic, spread, fresh_space, fresh_core, fresh_point):
-    s = space[...] * (1.0 / cells_total)
+def finish_kernel(cells_total, points_total, p0, p1, p2, p3, core, kinetic, spread, fresh_space, fresh_core, fresh_point):
+    both = four((p0, p1, p2, p3))
+    s = both[:RANK] * (1.0 / cells_total)
     gram = s[:, 0:32]
-    gram_v, plus, minus, cross_v = point_blocks(point[:RANK, :], points_total)
+    gram_v, plus, minus, cross_v = point_blocks(both[RANK : 2 * RANK], points_total)
     (_, inverse), (_, inverse_v) = factor_pair(gram, gram_v)
     zeros = jnp.zeros((RANK, 32), f32)
     lane = lanes((RANK, 128))
@@ -608,7 +642,7 @@
 
     inverse_t = transposed(inverse)
     inverse_vt = transposed(inverse_v)
-    aux = mm(point[RANK:, 0:32] * (1.0 / points_total), inverse_vt)
+    aux = mm(both[2 * RANK :, 0:32] * (1.0 / points_total), inverse_vt)
     weights_row = aux[0:1, :]
     moments_row = aux[1:2, :] + aux[2:3, :]
     raw_a = [gram - s[:, 32 * (d + 1) : 32 * (d + 2)] for d in range(3)]
@@ -629,45 +663,30 @@
     fresh_core[...] = current
 
 
-def finish(space, point, core, kinetic, spread, cells_total, points_total):
+def finish(parts, core, kinetic, spread, cells_total, points_total):
     def kernel(*refs):
         finish_kernel(cells_total, points_total, *refs)
 
     return call(
-        kernel, [((RANK * OWN * NY, NZ), f32), ((RANK, RANK), f32), (spread.shape, f32)], "vvvvv",
-        (space, point, core, kinetic, spread), name="finish",
-    )
-
-
-def axis_sum(values, axis, routes):
-    moved = [lax.ppermute(values, axis, route) for route in routes]
-    if len(moved) == 1:
-        return values + moved[0]
-    return (values + moved[1]) + (moved[0] + moved[2])
-
-
-def routes_x():
-    return [[(4 * y + x, 4 * y + (x + d) % 4) for y in range(4) for x in range(4)] for d in (1, 2, 3)]
-
-
-def routes_y():
-    return [[(4 * y + x, 4 * ((y + d) % 4) + x) for y in range(4) for x in range(4)] for d in (1, 2, 3)]
-
-
-def routes_z():
-    return [[(2 * z + c, 2 * ((z + d) % 4) + c) for z in range(4) for c in range(2)] for d in (1, 2, 3)]
-
-
-def routes_core():
-    return [[(2 * z + c, 2 * z + 1 - c) for z in range(4) for c in range(2)]]
-
-
-def total(space_part, point_part):
-    space_part = axis_sum(space_part, "space", routes_x())
-    point_part = axis_sum(point_part, "vel", routes_z())
-    space_part = axis_sum(space_part, "space", routes_y())
-    point_part = axis_sum(point_part, "vel", routes_core())
-    return space_part, point_part
+        kernel, [((RANK * OWN * NY, NZ), f32), ((RANK, RANK), f32), (spread.shape, f32)], "vvvvvvv",
+        (*parts, core, kinetic, spread), name="finish",
+    )
+
+
+def spread_pairs(space_part):
+    moved = []
+    for k in range(2):
+        route = [((s ^ (2 * v + k)) * 8 + v, s * 8 + v) for s in range(16) for v in range(8)]
+        moved.append(lax.ppermute(space_part, ("space", "vel"), route))
+    return moved
+
+
+def vel_parts(moved, point_part):
+    joint = jnp.concatenate([moved[0] + moved[1], point_part], axis=0)
+    pair = [(2 * z + c, 2 * z + 1 - c) for z in range(4) for c in range(2)]
+    joint = joint + lax.ppermute(joint, "vel", pair)
+    routes = [[(2 * z + c, 2 * ((z + d) % 4) + c) for z in range(4) for c in range(2)] for d in (1, 2, 3)]
+    return [joint] + [lax.ppermute(joint, "vel", route) for route in routes]
 
 
 def per_device(space_factor, core_matrix, velocity_factor, collision_rates):
@@ -675,26 +694,28 @@
     up = [(i, (i + 1) % devices) for i in range(devices)]
     down = [((i + 1) % devices, i) for i in range(devices)]
     below1 = lax.ppermute(space_factor[:, OWN - 1 :], "space", up).reshape(-1, NZ)
-    below3 = lax.ppermute(space_factor[:, : OWN - 1], "space", up).reshape(-1, NZ)
-    above3 = lax.ppermute(space_factor[:, :HIGH], "space", down).reshape(-1, NZ)
-    rates_below = lax.ppermute(collision_rates[1:], "space", up).reshape(-1, NZ)
-    rates_above = lax.ppermute(collision_rates[: HIGH - 1], "space", down).reshape(-1, NZ)
+    lower = jnp.concatenate([space_factor[:, : OWN - 1], collision_rates[None, 1:]], axis=0)
+    upper = jnp.concatenate([space_factor[:, :HIGH], collision_rates[None, :HIGH]], axis=0)
+    lower = lax.ppermute(lower, "space", up).reshape(-1, NZ)
+    upper = lax.ppermute(upper, "space", down).reshape(-1, NZ)
     rates = collision_rates.reshape(-1, NZ)
     values = space_factor.reshape(-1, NZ)
     cells_total = OWN * PLANE * devices
     points_total = velocity_factor.shape[1] * lax.axis_size("vel")
     v = lax.axis_index("vel").astype(jnp.int32).reshape(1)
 
-    point = point_sums(v, velocity_factor)
-    space = space_sums(values, below1, rates)
-    space, point = total(space, point)
-    wk, wl, src = small_first(space, point, core_matrix, cells_total, points_total)
-    spread, point = evolve_point(v, wl, src, velocity_factor)
-    kinetic, space = evolve_space(wk, values, below3, below1, above3, rates, rates_below, rates_above)
-    space, point = total(space, point)
-    fresh_space, fresh_core, fresh_point = finish(
-        space, point, core_matrix, kinetic, spread, cells_total, points_total
-    )
+    inner = space_sums(values, rates)
+    space = edge_sums(values, below1, inner)
+    moved = spread_pairs(space)
+    point = point_sums(v, velocity_factor, space)
+    parts = vel_parts(moved, point)
+    filled = fill_planes(values, lower, below1, upper, parts[0])
+    wk, wl, src = small_first(parts, core_matrix, filled[0], cells_total, points_total)
+    kinetic, space = evolve_space(wk, filled, rates, lower, upper)
+    moved = spread_pairs(space)
+    spread, point = evolve_point(v, wl, src, velocity_factor, space)
+    parts = vel_parts(moved, point)
+    fresh_space, fresh_core, fresh_point = finish(parts, core_matrix, kinetic, spread, cells_total, points_total)
     return fresh_space.reshape(space_factor.shape), fresh_core, fresh_point
 
 

time: 127 us -> 141 us (1.11)
  the two profiles are of different devices: /device:TPU:30 before, /device:TPU:1 now
where the time goes in v1:
time: 141 us; the launch traced here: 140 us
  Pallas kernels  72.6 us (51%)
  waiting for transfers between devices  30.5 us (22%)
  starting transfers between devices  27.9 us (20%)
  other arithmetic  4.39 us (3%)
  local copies, waits for them, and re-layouts  4.29 us (3%)
    pallas_call x8, Pallas kernels, call(): pl.pallas_call(kernel, out_shape=[jax.ShapeDtypeStruct(s, d) for s, d in...  72.6 us
    ppermute x1, waiting for transfers between devices, per_device(): lax.ppermute(space_factor[:, OWN - 1:], 'space', up).reshape(-1, NZ)  22.5 us
    ppermute x6, starting transfers between devices, vel_parts(): return [joint] + [lax.ppermute(joint, 'vel', route) for route in routes]  10.5 us
    ppermute x4, starting transfers between devices, spread_pairs(): moved.append(lax.ppermute(space_part, ('space', 'vel'), route))  10.3 us
    ppermute x6, waiting for transfers between devices, vel_parts(): return [joint] + [lax.ppermute(joint, 'vel', route) for route in routes]  5.86 us
    ppermute x1, starting transfers between devices, per_device(): upper = lax.ppermute(upper, 'space', down).reshape(-1, NZ)  5.75 us
    unnamed x24, local copies, waits for them, and re-layouts  3.12 us
  transfers between devices with their start and end apart: 15, of which 6 were waited for; matrix products, arithmetic and copies ran while one was open for 1% of the time, Pallas kernels for 25%

profile of v1, /device:TPU:1, one launch (start us, length us, event | category | flops | bytes accessed | tf_op | source)
XLA Modules:
  0.0 140.5 jit_solution(7392505364344086130)
XLA Ops:
  0.6 0.0 slice-start
  0.6 0.8 slice_bitcast_fusion
  1.5 0.3 slice-done
  1.8 1.3 pad_maximum_fusion.1
  3.1 5.7 %collective-permute-start.8 = (f32[33,3,16,128]{3,2,1,0:T(8,128)}, f32[33,3,16,128]{3,2,1,0:T(8,128)S(1)}, u32[]{:S(2)}, u32[]{:S(2)}) collective-permute-start(f32[33,3,16,128]{3,2,1,0:T(8,128)} %get-tuple-element.35), channel_id=1, source_target_pairs={{8,0},{16,8},{24,16},{32,24},{40,32},{48,40},{56,48},{64,56},{72,6... | collective-permute-start | bytes 2433032 | tf_op jit(solution)/shard_map/ppermute | solution.py:700
  8.8 0.0 collective-permute-start.7
  8.8 0.0 copy-done
  8.8 0.1 collective-permute-start
  8.9 5.2 %space_sums.1.inner = f32[32,256]{1,0:T(8,128)} custom-call(f32[2048,128]{1,0:T(8,128)} %bitcast.11, f32[64,128]{1,0:T(8,128)} %bitcast.20), custom_call_target="tpu_custom_call" | custom-call | tf_op jit(solution)/shard_map/space_sums/pallas_call | solution.py:123
  14.2 22.5 %collective-permute-done = f32[32,1,16,128]{3,2,1,0:T(8,128)S(1)} collective-permute-done((f32[32,1,16,128]{3,2,1,0:T(8,128)S(1)}, f32[32,1,16,128]{3,2,1,0:T(8,128)S(1)}, u32[]{:S(2)}, u32[]{:S(2)}) %collective-permute-start) | collective-permute-done | bytes 262176 | tf_op jit(solution)/shard_map/ppermute | solution.py:696
  36.6 0.0 copy-start.3
  36.6 0.7 copy-done.3
  37.3 2.3 %edge_sums.1.after = f32[32,256]{1,0:T(8,128)} custom-call(f32[2048,128]{1,0:T(8,128)} %bitcast.12, f32[512,128]{1,0:T(8,128)} %bitcast.18, f32[32,256]{1,0:T(8,128)} %space_sums.1.inner), custom_call_target="tpu_custom_call" | custom-call | tf_op jit(solution)/shard_map/edge_sums/pallas_call | solution.py:123
  39.6 0.0 collective-permute-start.2
  39.6 1.9 %collective-permute-start.1 = (f32[32,256]{1,0:T(8,128)}, f32[32,256]{1,0:T(8,128)S(1)}, u32[]{:S(2)}, u32[]{:S(2)}) collective-permute-start(f32[32,256]{1,0:T(8,128)} %edge_sums.1.after), channel_id=1, source_target_pairs={{0,0},{17,1},{34,2},{51,3},{68,4},{85,5},{102,6},{119,7},{8,8},{25... | collective-permute-start | bytes 98312 | tf_op jit(solution)/shard_map/ppermute | solution.py:680
  41.5 6.5 %point_sums.1 = f32[32,256]{1,0:T(8,128)} custom-call(s32[1]{0:T(128)} %bitcast.3.v_ref, f32[144]{0:T(256)} %constant.16.clone.speeds, f32[2,8,1152]{2,1,0:T(8,128)} %constant.17.clone.rows, f32[2,32,1152]{2,1,0:T(8,128)} %constant.18.clone.phi, f32[48,128]{1,0:T(8,128)} %constant.19.clone.scale, f32[32,13824]{1,0:T(8,128)} %values.3, f32[32,256]{1,0:T(8,128)} %edge_sums.1.after), custom_call_target="tpu_custom_call" | custom-call | tf_op jit(solution)/shard_map/point_sums/pallas_call | solution.py:123
  48.1 0.0 collective-permute-done.2
  48.1 0.0 collective-permute-done.1
  48.1 0.8 pad_maximum_fusion.3
  48.8 1.3 collective-permute-start.3
  50.1 0.9 collective-permute-done.3
  51.0 0.8 fusion.after.refs_0_
  51.8 0.0 copy-start.4
  51.8 4.4 %collective-permute-start.6 = (f32[64,256]{1,0:T(8,128)S(1)}, f32[64,256]{1,0:T(8,128)S(1)}, u32[]{:S(2)}, u32[]{:S(2)}) collective-permute-start(f32[64,256]{1,0:T(8,128)S(1)} %fusion.after.refs_0_), channel_id=1, source_target_pairs={{0,6},{1,7},{2,0},{3,1},{4,2},{5,3},{6,4},{7,5},{8,14},{9,15},{10,... | collective-permute-start | bytes 196616 | tf_op jit(solution)/shard_map/ppermute | solution.py:689
  56.2 0.0 collective-permute-start.5
  56.2 0.7 collective-permute-start.4
  56.8 0.0 collective-permute-done.8
  56.9 0.0 collective-permute-done.7
  56.9 0.0 copy-start.2
  56.9 0.0 copy-done.4
  56.9 0.9 copy-done.1
  57.8 0.2 copy-done.2
  58.0 8.3 %fill_planes.1 = (bf16[32,25344]{1,0:T(8,128)(2,1)}, bf16[32,25344]{1,0:T(8,128)(2,1)}, bf16[32,25344]{1,0:T(8,128)(2,1)}, bf16[32,25344]{1,0:T(8,128)(2,1)}, bf...) custom-call(f32[2048,128]{1,0:T(8,128)} %bitcast.13, f32[1584,128]{1,0:T(8,128)} %bitcast.16, f32[512,128]{1,0:T(8,128)} %bitcast.19, ...), custom_call_target="tpu_custom_call" | custom-call | tf_op jit(solution)/shard_map/fill_planes/pallas_call | solution.py:123
  66.3 0.0 collective-permute-done.6.refs_3_
  66.3 0.0 collective-permute-done.5.refs_2_
  66.3 0.0 copy-start.10
  66.3 0.0 collective-permute-done.4.refs_1_
  66.3 0.0 copy-start.11
  66.3 0.6 copy-done.9
  66.9 0.0 copy-done.10
  67.0 0.0 copy-done.11
  67.0 7.0 %small_first.1 = (f32[2,64,224]{2,1,0:T(8,128)}, f32[2,224,128]{2,1,0:T(8,128)}, f32[3,32,128]{2,1,0:T(8,128)}) custom-call(f32[64,256]{1,0:T(8,128)} %copy-done.4, f32[64,256]{1,0:T(8,128)} %copy-done.11, f32[64,256]{1,0:T(8,128)} %copy-done.10, f32[64,256]{1,0:T(8,128)} %copy-done.9, f32[32,32]{1,0:T(8,128)} %refs_4_.3, f32[32,896]{1,0:T(8,128)} %constant.20.clone.refs_5_, ...), custom_call_target="tpu_custom_call" | custom-call | tf_op jit(solution)/shard_map/small_first/pallas_call | solution.py:123
  74.0 19.1 %evolve_space.1 = (f32[32,10240]{1,0:T(8,128)}, f32[32,256]{1,0:T(8,128)}) custom-call(f32[2,64,224]{2,1,0:T(8,128)} %get-tuple-element.20.wk, bf16[32,25344]{1,0:T(8,128)(2,1)} %get-tuple-element.19.refs_7_.refs_0_, bf16[32,25344]{1,0:T(8,128)(2,1)} %get-tuple-element.21.refs_1_, bf16[32,25344]{1,0:T(8,128)(2,1)} %get-tuple-element.22.refs_2_, ...), custom_call_target="tpu_custom_call" | custom-call | tf_op jit(solution)/shard_map/evolve_space/pallas_call | solution.py:123
  93.1 0.5 collective-permute-start.10
  93.6 7.9 %collective-permute-start.9 = (f32[32,256]{1,0:T(8,128)}, f32[32,256]{1,0:T(8,128)S(1)}, u32[]{:S(2)}, u32[]{:S(2)}) collective-permute-start(f32[32,256]{1,0:T(8,128)} %get-tuple-element.26.after), channel_id=1, source_target_pairs={{0,0},{17,1},{34,2},{51,3},{68,4},{85,5},{102,6},{119,7},{8,8},{25... | collective-permute-start | bytes 98312 | tf_op jit(solution)/shard_map/ppermute | solution.py:680
  101.5 12.8 %evolve_point.1 = (f32[32,13824]{1,0:T(8,128)}, f32[40,256]{1,0:T(8,128)}) custom-call(s32[1]{0:T(128)} %bitcast.3.v_ref, f32[144]{0:T(256)} %constant.16.clone.speeds, f32[2,8,1152]{2,1,0:T(8,128)} %constant.17.clone.rows, f32[2,224,128]{2,1,0:T(8,128)} %get-tuple-element.27.wl, f32[3,32,128]{2,1,0:T(8,128)} %get-tuple-element.28.src, f32[32,13824]{1,0:T(8,128)} %values.3, ...), custom_call_target="tpu_custom_call" | custom-call | tf_op jit(solution)/shard_map/evolve_point/pallas_call | solution.py:123
  114.3 0.0 collective-permute-done.10
  114.3 0.0 collective-permute-done.9
  114.3 0.8 pad_maximum_fusion.2
  115.1 0.0 collective-permute-start.11
  115.1 1.3 collective-permute-done.11
  116.3 0.8 fusion.1.refs_0_
  117.1 0.0 copy-start.5
  117.1 4.3 %collective-permute-start.14 = (f32[72,256]{1,0:T(8,128)S(1)}, f32[72,256]{1,0:T(8,128)S(1)}, u32[]{:S(2)}, u32[]{:S(2)}) collective-permute-start(f32[72,256]{1,0:T(8,128)S(1)} %fusion.1.refs_0_), channel_id=1, source_target_pairs={{0,6},{1,7},{2,0},{3,1},{4,2},{5,3},{6,4},{7,5},{8,14},{9,15},{10,... | collective-permute-start | bytes 221192 | tf_op jit(solution)/shard_map/ppermute | solution.py:689
  121.4 0.4 collective-permute-start.13
  121.9 0.8 collective-permute-start.12
  122.6 0.2 collective-permute-done.14.refs_3_
  122.8 3.4 %collective-permute-done.13.refs_2_ = f32[72,256]{1,0:T(8,128)S(1)} collective-permute-done((f32[72,256]{1,0:T(8,128)S(1)}, f32[72,256]{1,0:T(8,128)S(1)}, u32[]{:S(2)}, u32[]{:S(2)}) %collective-permute-start.13) | collective-permute-done | bytes 73760 | tf_op jit(solution)/shard_map/ppermute | solution.py:689
  126.2 2.3 %collective-permute-done.12.refs_1_ = f32[72,256]{1,0:T(8,128)S(1)} collective-permute-done((f32[72,256]{1,0:T(8,128)S(1)}, f32[72,256]{1,0:T(8,128)S(1)}, u32[]{:S(2)}, u32[]{:S(2)}) %collective-permute-start.12) | collective-permute-done | bytes 73760 | tf_op jit(solution)/shard_map/ppermute | solution.py:689
  128.5 0.0 copy-done.5
  128.5 0.0 copy-done.6
  128.5 0.0 copy-done.7
  128.5 0.6 copy-done.8
  129.1 11.4 %finish.1 = (f32[2048,128]{1,0:T(8,128)}, f32[32,32]{1,0:T(8,128)}, f32[32,13824]{1,0:T(8,128)}) custom-call(f32[72,256]{1,0:T(8,128)} %copy-done.5, f32[72,256]{1,0:T(8,128)} %copy-done.8, f32[72,256]{1,0:T(8,128)} %copy-done.7, f32[72,256]{1,0:T(8,128)} %copy-done.6, f32[32,32]{1,0:T(8,128)} %refs_4_.3, f32[32,10240]{1,0:T(8,128)} %get-tuple-element.30.refs_5_, ...), custom_call_target="tpu_custom_call" | custom-call | tf_op jit(solution)/shard_map/finish/pallas_call | solution.py:123
  (9 shorter events, 0.0 us)
Async XLA Ops:
  0.6 1.2 slice-start
  1.5 7.3 %copy-start = (f32[32,4,16,128]{3,2,1,0:T(8,128)S(1)}, f32[32,4,16,128]{3,2,1,0:T(8,128)}, u32[]{:S(2)}) copy-start(f32[32,4,16,128]{3,2,1,0:T(8,128)} %param.10) | copy-start | bytes 3145732
  3.1 53.8 %collective-permute-start.8 = (f32[33,3,16,128]{3,2,1,0:T(8,128)}, f32[33,3,16,128]{3,2,1,0:T(8,128)S(1)}, u32[]{:S(2)}, u32[]{:S(2)}) collective-permute-start(f32[33,3,16,128]{3,2,1,0:T(8,128)} %get-tuple-element.35), channel_id=1, source_target_pairs={{8,0},{16,8},{24,16},{32,24},{40,32},{48,40},{56,48},{64,56},{72,6... | collective-permute-start | bytes 2433032 | tf_op jit(solution)/shard_map/ppermute | solution.py:700
  8.8 48.0 %collective-permute-start.7 = (f32[33,3,16,128]{3,2,1,0:T(8,128)}, f32[33,3,16,128]{3,2,1,0:T(8,128)S(1)}, u32[]{:S(2)}, u32[]{:S(2)}) collective-permute-start(f32[33,3,16,128]{3,2,1,0:T(8,128)} %get-tuple-element.36), channel_id=1, source_target_pairs={{0,8},{8,16},{16,24},{24,32},{32,40},{40,48},{48,56},{56,64},{64,7... | collective-permute-start | bytes 2433032 | tf_op jit(solution)/shard_map/ppermute | solution.py:699
  8.8 27.8 %collective-permute-start = (f32[32,1,16,128]{3,2,1,0:T(8,128)S(1)}, f32[32,1,16,128]{3,2,1,0:T(8,128)S(1)}, u32[]{:S(2)}, u32[]{:S(2)}) collective-permute-start(f32[32,1,16,128]{3,2,1,0:T(8,128)S(1)} %slice.13), channel_id=1, source_target_pairs={{0,8},{8,16},{16,24},{24,32},{32,40},{40,48},{48,56},{56,64},{64,7... | collective-permute-start | bytes 786440 | tf_op jit(solution)/shard_map/ppermute | solution.py:696
  36.6 0.7 copy-start.3
  39.6 8.4 %collective-permute-start.2 = (f32[32,256]{1,0:T(8,128)}, f32[32,256]{1,0:T(8,128)S(1)}, u32[]{:S(2)}, u32[]{:S(2)}) collective-permute-start(f32[32,256]{1,0:T(8,128)} %edge_sums.1.after), channel_id=1, source_target_pairs={{8,0},{25,1},{42,2},{59,3},{76,4},{93,5},{110,6},{127,7},{0,8},{17... | collective-permute-start | bytes 98312 | tf_op jit(solution)/shard_map/ppermute | solution.py:680
  39.6 8.4 %collective-permute-start.1 = (f32[32,256]{1,0:T(8,128)}, f32[32,256]{1,0:T(8,128)S(1)}, u32[]{:S(2)}, u32[]{:S(2)}) collective-permute-start(f32[32,256]{1,0:T(8,128)} %edge_sums.1.after), channel_id=1, source_target_pairs={{0,0},{17,1},{34,2},{51,3},{68,4},{85,5},{102,6},{119,7},{8,8},{25... | collective-permute-start | bytes 98312 | tf_op jit(solution)/shard_map/ppermute | solution.py:680
  48.8 2.2 %collective-permute-start.3 = (f32[64,256]{1,0:T(8,128)S(1)}, f32[64,256]{1,0:T(8,128)S(1)}, u32[]{:S(2)}, u32[]{:S(2)}) collective-permute-start(f32[64,256]{1,0:T(8,128)S(1)} %pad_maximum_fusion.3), channel_id=1, source_target_pairs={{0,1},{1,0},{2,3},{3,2},{4,5},{5,4},{6,7},{7,6},{8,9},{9,8},{10,11... | collective-permute-start | bytes 196616 | tf_op jit(solution)/shard_map/ppermute | solution.py:687
  51.8 5.1 %copy-start.4 = (f32[64,256]{1,0:T(8,128)}, f32[64,256]{1,0:T(8,128)S(1)}, u32[]{:S(2)}) copy-start(f32[64,256]{1,0:T(8,128)S(1)} %fusion.after.refs_0_) | copy-start | bytes 196612
  51.8 14.5 %collective-permute-start.6 = (f32[64,256]{1,0:T(8,128)S(1)}, f32[64,256]{1,0:T(8,128)S(1)}, u32[]{:S(2)}, u32[]{:S(2)}) collective-permute-start(f32[64,256]{1,0:T(8,128)S(1)} %fusion.after.refs_0_), channel_id=1, source_target_pairs={{0,6},{1,7},{2,0},{3,1},{4,2},{5,3},{6,4},{7,5},{8,14},{9,15},{10,... | collective-permute-start | bytes 196616 | tf_op jit(solution)/shard_map/ppermute | solution.py:689
  56.2 10.2 %collective-permute-start.5 = (f32[64,256]{1,0:T(8,128)S(1)}, f32[64,256]{1,0:T(8,128)S(1)}, u32[]{:S(2)}, u32[]{:S(2)}) collective-permute-start(f32[64,256]{1,0:T(8,128)S(1)} %fusion.after.refs_0_), channel_id=1, source_target_pairs={{0,4},{1,5},{2,6},{3,7},{4,0},{5,1},{6,2},{7,3},{8,12},{9,13},{10,... | collective-permute-start | bytes 196616 | tf_op jit(solution)/shard_map/ppermute | solution.py:689
  56.2 10.2 %collective-permute-start.4 = (f32[64,256]{1,0:T(8,128)S(1)}, f32[64,256]{1,0:T(8,128)S(1)}, u32[]{:S(2)}, u32[]{:S(2)}) collective-permute-start(f32[64,256]{1,0:T(8,128)S(1)} %fusion.after.refs_0_), channel_id=1, source_target_pairs={{0,2},{1,3},{2,4},{3,5},{4,6},{5,7},{6,0},{7,1},{8,10},{9,11},{10,... | collective-permute-start | bytes 196616 | tf_op jit(solution)/shard_map/ppermute | solution.py:689
  56.9 0.9 copy-start.1
  56.9 1.1 copy-start.2
  66.3 0.6 copy-start.9
  66.3 0.6 copy-start.10
  66.3 0.6 copy-start.11
  93.1 21.2 %collective-permute-start.10 = (f32[32,256]{1,0:T(8,128)}, f32[32,256]{1,0:T(8,128)S(1)}, u32[]{:S(2)}, u32[]{:S(2)}) collective-permute-start(f32[32,256]{1,0:T(8,128)} %get-tuple-element.26.after), channel_id=1, source_target_pairs={{8,0},{25,1},{42,2},{59,3},{76,4},{93,5},{110,6},{127,7},{0,8},{17... | collective-permute-start | bytes 98312 | tf_op jit(solution)/shard_map/ppermute | solution.py:680
  93.6 20.7 %collective-permute-start.9 = (f32[32,256]{1,0:T(8,128)}, f32[32,256]{1,0:T(8,128)S(1)}, u32[]{:S(2)}, u32[]{:S(2)}) collective-permute-start(f32[32,256]{1,0:T(8,128)} %get-tuple-element.26.after), channel_id=1, source_target_pairs={{0,0},{17,1},{34,2},{51,3},{68,4},{85,5},{102,6},{119,7},{8,8},{25... | collective-permute-start | bytes 98312 | tf_op jit(solution)/shard_map/ppermute | solution.py:680
  115.1 1.3 collective-permute-start.11
  117.1 11.4 %copy-start.5 = (f32[72,256]{1,0:T(8,128)}, f32[72,256]{1,0:T(8,128)S(1)}, u32[]{:S(2)}) copy-start(f32[72,256]{1,0:T(8,128)S(1)} %fusion.1.refs_0_) | copy-start | bytes 221188
  117.1 5.7 %collective-permute-start.14 = (f32[72,256]{1,0:T(8,128)S(1)}, f32[72,256]{1,0:T(8,128)S(1)}, u32[]{:S(2)}, u32[]{:S(2)}) collective-permute-start(f32[72,256]{1,0:T(8,128)S(1)} %fusion.1.refs_0_), channel_id=1, source_target_pairs={{0,6},{1,7},{2,0},{3,1},{4,2},{5,3},{6,4},{7,5},{8,14},{9,15},{10,... | collective-permute-start | bytes 221192 | tf_op jit(solution)/shard_map/ppermute | solution.py:689
  121.4 4.8 %collective-permute-start.13 = (f32[72,256]{1,0:T(8,128)S(1)}, f32[72,256]{1,0:T(8,128)S(1)}, u32[]{:S(2)}, u32[]{:S(2)}) collective-permute-start(f32[72,256]{1,0:T(8,128)S(1)} %fusion.1.refs_0_), channel_id=1, source_target_pairs={{0,4},{1,5},{2,6},{3,7},{4,0},{5,1},{6,2},{7,3},{8,12},{9,13},{10,... | collective-permute-start | bytes 221192 | tf_op jit(solution)/shard_map/ppermute | solution.py:689
  121.9 6.6 %collective-permute-start.12 = (f32[72,256]{1,0:T(8,128)S(1)}, f32[72,256]{1,0:T(8,128)S(1)}, u32[]{:S(2)}, u32[]{:S(2)}) collective-permute-start(f32[72,256]{1,0:T(8,128)S(1)} %fusion.1.refs_0_), channel_id=1, source_target_pairs={{0,2},{1,3},{2,4},{3,5},{4,6},{5,7},{6,0},{7,1},{8,10},{9,11},{10,... | collective-permute-start | bytes 221192 | tf_op jit(solution)/shard_map/ppermute | solution.py:689
  122.8 5.7 %copy-start.6 = (f32[72,256]{1,0:T(8,128)}, f32[72,256]{1,0:T(8,128)S(1)}, u32[]{:S(2)}) copy-start(f32[72,256]{1,0:T(8,128)S(1)} %collective-permute-done.14.refs_3_) | copy-start | bytes 221188
  126.2 2.3 %copy-start.7 = (f32[72,256]{1,0:T(8,128)}, f32[72,256]{1,0:T(8,128)S(1)}, u32[]{:S(2)}) copy-start(f32[72,256]{1,0:T(8,128)S(1)} %collective-permute-done.13.refs_2_) | copy-start | bytes 221188
  128.5 0.6 copy-start.8

commit v2 on v1

--- a/solution.py
+++ b/solution.py
@@ -5,6 +5,7 @@
 from jax.experimental import pallas as pl
 from jax.experimental.pallas import tpu as pltpu
 from jax.sharding import PartitionSpec as P
+
 
 RANK = 32
 NVD = 48
@@ -17,7 +18,6 @@
 Q1 = 6
 HALF = NVD * NVD // 2
 PLANE = NY * NZ
-PAD = PLANE + 2 * NZ
 WIDE = LOW + OWN + HIGH
 INTERPRET = False
 
@@ -118,7 +118,7 @@
     return (lanes((RANK, RANK)) == sublanes((RANK, RANK))).astype(f32)
 
 
-def call(kernel, outs, ins, args, scratch=(), name=None):
+def call(kernel, outs, ins, args, scratch=(), mib=8):
     spaces = {"v": pltpu.VMEM, "s": pltpu.SMEM, "a": pl.ANY}
     return pl.pallas_call(
         kernel,
@@ -126,9 +126,8 @@
         in_specs=[pl.BlockSpec(memory_space=spaces[c]) for c in ins],
         out_specs=[pl.BlockSpec(memory_space=pltpu.VMEM) for _ in outs],
         scratch_shapes=list(scratch),
-        compiler_params=pltpu.CompilerParams(vmem_limit_bytes=58 * 1024 * 1024),
+        compiler_params=pltpu.CompilerParams(vmem_limit_bytes=mib * 1024 * 1024),
         interpret=INTERPRET,
-        name=name,
     )(*args)
 
 
@@ -184,11 +183,11 @@
 def point_sums(v, values, after):
     return call(
         point_sums_kernel, [((RANK, 256), f32)], "ssvvvva",
-        (v, SPEEDS, ROWS, PHI, PHI_SCALE, values, after), name="point_sums",
+        (v, SPEEDS, ROWS, PHI, PHI_SCALE, values, after), mib=12,
     )[0]
 
 
-def space_sums_kernel(values, rates, out, hi, lo, zh, zl, ch, cl):
+def space_sums_kernel(values, rates, out, own_hi, own_lo, hi, lo, zh, zl, ch, cl):
     def load(p, carry):
         for y in range(NY):
             block = values[pl.ds(p * NY + y, RANK, stride=OWN * NY), :]
@@ -196,6 +195,8 @@
             a, b = split(block)
             hi[:, pl.ds(at + PLANE, NZ)] = a
             lo[:, pl.ds(at + PLANE, NZ)] = b
+            own_hi[:, pl.ds(at, NZ)] = a
+            own_lo[:, pl.ds(at, NZ)] = b
             a, b = split(roll_lanes(block, 1))
             zh[:, pl.ds(at, NZ)] = a
             zl[:, pl.ds(at, NZ)] = b
@@ -235,26 +236,26 @@
 def space_sums(values, rates):
     own = (RANK, OWN * PLANE)
     return call(
-        space_sums_kernel, [((RANK, 256), f32)], "vv", (values, rates),
-        [pltpu.VMEM((RANK, (OWN + 1) * PLANE), bf16)] * 2 + [pltpu.VMEM(own, bf16)] * 4, name="space_sums",
-    )[0]
-
-
-def edge_sums_kernel(values, below, inner, out):
-    t = jnp.zeros((RANK, 64), f32)
+        space_sums_kernel, [((RANK, 256), f32), (own, bf16), (own, bf16)], "vv", (values, rates),
+        [pltpu.VMEM((RANK, (OWN + 1) * PLANE), bf16)] * 2 + [pltpu.VMEM(own, bf16)] * 4, mib=12,
+    )
+
+
+def edge_sums_kernel(own_hi, own_lo, below, inner, out, edge_hi, edge_lo):
     empty = jnp.zeros((RANK, PLANE), bf16)
-    first = jnp.concatenate([values[pl.ds(y, RANK, stride=OWN * NY), :] for y in range(NY)], axis=1)
-    other = jnp.concatenate([below[pl.ds(y, RANK, stride=NY), :] for y in range(NY)], axis=1)
-    lh, ll = split(first)
-    oh, ol = split(other)
+    oh, ol = split(jnp.concatenate([below[pl.ds(y, RANK, stride=NY), :] for y in range(NY)], axis=1))
+    edge_hi[...] = oh
+    edge_lo[...] = ol
+    lh, ll = own_hi[:, :PLANE], own_lo[:, :PLANE]
     part = dot_t(jnp.concatenate([lh, ll], axis=0), jnp.concatenate([empty, oh], axis=0))
     t = part[:RANK] + part[RANK:] + dot_t(lh, jnp.concatenate([empty, ol], axis=0))
     out[:, :128] = inner[:, :128] + jnp.concatenate([t, jnp.zeros((RANK, 64), f32)], axis=1)
     out[:, 128:] = inner[:, 128:]
 
 
-def edge_sums(values, below, inner):
-    return call(edge_sums_kernel, [((RANK, 256), f32)], "vvv", (values, below, inner), name="edge_sums")[0]
+def edge_sums(own_hi, own_lo, below, inner):
+    plane = ((RANK, PLANE), bf16)
+    return call(edge_sums_kernel, [((RANK, 256), f32), plane, plane], "vvvv", (own_hi, own_lo, below, inner))
 
 
 def factor_pair(first, second):
@@ -307,7 +308,7 @@
     both = four((p0, p1, p2, p3))
     s = both[:RANK] * (1.0 / cells_total)
     gram = s[:, 0:32]
-    gram_v, plus, minus, raw = point_blocks(both[RANK:], points_total)
+    gram_v, _, _, raw = point_blocks(both[RANK:], points_total)
     (upper, inverse), (upper_v, inverse_v) = factor_pair(gram, gram_v)
     identity = eye()
     raw_a = [gram - s[:, 32 * (d + 1) : 32 * (d + 2)] for d in range(3)]
@@ -344,26 +345,20 @@
     source.append(mm(e, jnp.broadcast_to(third, (RANK, 128)))[:, 0:1])
     for n in range(3):
         src[n] = jnp.where((lane >= 96) & (lane < 99), source[n], 0.0)
-    flux = congruent(inverse_v, plus + minus)
-    turned_raw = mm(inverse_v, raw)
-    weights = turned_raw[:, 0:1]
-    moments_row = transposed(turned_raw)[LAST : LAST + 1, :]
+    half = mm(inverse_v, both[RANK:, :] * (1.0 / points_total))
+    turned_raw = half[:, 224:256]
+    weights_row = transposed(turned_raw)[0:1, :]
+    blocks = [half[:, 192:224], half[:, 128:160], half[:, 160:192], half[:, 32:64], half[:, 64:96], half[:, 96:128]]
+    flux = mm(jnp.concatenate(blocks, axis=0), transposed(inverse_v))
+    flux = [flux[k * RANK : (k + 1) * RANK] * (1.0 if k % 2 == 0 else -1.0) for k in range(6)]
     center = identity
-    blocks = []
-    for d in range(3):
-        center = center - flux[d] + flux[d + 3]
-        blocks += [flux[d], -flux[d + 3]]
-    blocks = [center] + blocks
-    relax_t = weights * moments_row - identity
-    empty = jnp.zeros((RANK, 6 * RANK), f32)
-    for kind in range(2):
-        if kind == 0:
-            parts = [mm(to_kinetic_t, block) for block in blocks]
-            relax = mm(to_kinetic_t, relax_t)
-        else:
-            parts, relax = blocks, relax_t
-        wk[kind, :RANK, :] = transposed(jnp.concatenate(parts, axis=0))
-        wk[kind, RANK:, :] = jnp.concatenate([transposed(relax), empty], axis=1)
+    for block in flux:
+        center = center - block
+    relax = turned_raw[:, LAST : LAST + 1] * weights_row - identity
+    column = jnp.concatenate([center, relax] + flux, axis=0)
+    to_kinetic = transposed(to_kinetic_t)
+    wk[0] = mm(column, jnp.concatenate([to_kinetic] * 3 + [zeros], axis=1))
+    wk[1] = jnp.concatenate([column] * 3 + [jnp.zeros((8 * RANK, 32), f32)], axis=1)
 
 
 def small_first(parts, core, after, cells_total, points_total):
@@ -371,8 +366,8 @@
         small_first_kernel(cells_total, points_total, *refs)
 
     return call(
-        kernel, [((2, 64, 224), f32), ((2, 224, 128), f32), ((3, RANK, 128), f32)], "vvvvvvva",
-        (*parts, core, SELECT, MEANS, after), name="small_first",
+        kernel, [((2, 8 * RANK, 128), f32), ((2, 224, 128), f32), ((3, RANK, 128), f32)], "vvvvvvva",
+        (*parts, core, SELECT, MEANS, after),
     )
 
 
@@ -457,133 +452,133 @@
 def evolve_point(v, wl, src, values, after):
     return call(
         evolve_point_kernel, [(values.shape, f32), ((RANK + 8, 256), f32)], "ssvvvva",
-        (v, SPEEDS, ROWS, wl, src, values, after), name="evolve_point",
-    )
-
-
-CHUNK = 512
-
-
-def store(dst, t, y, block, rolled):
-    hi, lo, mh, ml, ph, plo = dst
-    at = pl.multiple_of(t * PAD + (y + 1) * NZ, 128)
-    a, b = split(block)
-    hi[:, pl.ds(at, NZ)] = a
-    lo[:, pl.ds(at, NZ)] = b
-    if y == 0:
-        other = pl.multiple_of(t * PAD + (NY + 1) * NZ, 128)
-        hi[:, pl.ds(other, NZ)] = a
-        lo[:, pl.ds(other, NZ)] = b
-    if y == NY - 1:
-        other = pl.multiple_of(t * PAD, 128)
-        hi[:, pl.ds(other, NZ)] = a
-        lo[:, pl.ds(other, NZ)] = b
-    if rolled:
-        c, d = split(roll_lanes(block, 1))
-        mh[:, pl.ds(at, NZ)] = c
-        ml[:, pl.ds(at, NZ)] = d
-    if rolled == 2:
-        c, d = split(roll_lanes(block, -1))
-        ph[:, pl.ds(at, NZ)] = c
-        plo[:, pl.ds(at, NZ)] = d
-
-
-def fill_kernel(values, below3, below1, above3, after, *dst):
-    def fill(source, planes, first):
-        def load(p, carry):
+        (v, SPEEDS, ROWS, wl, src, values, after), mib=16,
+    )
+
+
+RATES = (LOW - 1 + OWN + HIGH - 1) * NY
+HALO = RANK * HIGH * NY
+
+
+def fill_kernel(v_ref, own_hi, own_lo, edge_hi, edge_lo, mine, other, after, hi, lo, rates_low, rates_high):
+    core = v_ref[0] % 2
+    hi[:, LOW * PLANE : (LOW + OWN) * PLANE] = own_hi[...]
+    lo[:, LOW * PLANE : (LOW + OWN) * PLANE] = own_lo[...]
+    hi[:, (LOW - 1) * PLANE : LOW * PLANE] = edge_hi[...]
+    lo[:, (LOW - 1) * PLANE : LOW * PLANE] = edge_lo[...]
+    for source, place in ((mine, core), (other, 1 - core)):
+
+        def load(p, carry, source=source, place=place):
             for y in range(NY):
-                store(dst, p + first, y, source[pl.ds(p * NY + y, RANK, stride=planes * NY), :], 2)
+                a, b = split(source[pl.ds(p * NY + y, RANK, stride=HIGH * NY), :])
+                at = pl.multiple_of((p + place * (LOW + OWN)) * PLANE + y * NZ, 128)
+                hi[:, pl.ds(at, NZ)] = a
+                lo[:, pl.ds(at, NZ)] = b
             return carry
 
-        lax.fori_loop(0, planes, load, 0)
-
-    fill(below3, LOW - 1, 0)
-    fill(below1, 1, LOW - 1)
-    fill(values, OWN, LOW)
-    fill(above3, HIGH, LOW + OWN)
-
-
-def fill_planes(values, below3, below1, above3, after):
-    return call(
-        fill_kernel, [((RANK, WIDE * PAD), bf16)] * 6, "vvvva", (values, below3, below1, above3, after), name="fill_planes",
-    )
-
-
-def evolve_space_kernel(wk, *refs):
-    raw = refs[0:6]
-    rates, rates_below, rates_above, new, out, rates_all, ch, cl = refs[6:14]
-    sets = [raw, refs[14:20], refs[20:26]]
+        lax.fori_loop(0, HIGH, load, 0)
+    first, second = mine[HALO:, :], other[HALO:, :]
+    rates_low[...] = jnp.where(core == 0, first, second)
+    rates_high[...] = jnp.where(core == 0, second, first)
+
+
+def fill_planes(v, own, edge, mine, other, after):
+    wide = ((RANK, WIDE * PLANE), bf16)
+    part = ((HIGH * NY, NZ), f32)
+    return call(fill_kernel, [wide, wide, part, part], "svvvvvva", (v, *own, *edge, mine, other, after), mib=12)
+
+
+def evolve_space_kernel(wk, raw_hi, raw_lo, rates, rates_low, rates_high, new, out, rates_all, partial, passed, *bufs):
+    sets = [(raw_hi, raw_lo), bufs[0:2], bufs[2:4]]
     order = [0, 1, 2, 1]
-    rates_all[: (LOW - 1) * NY, :] = rates_below[RANK * (LOW - 1) * NY :, :]
-    rates_all[(LOW - 1) * NY : (LOW - 1 + OWN) * NY, :] = rates[...]
-    rates_all[(LOW - 1 + OWN) * NY :, :] = rates_above[RANK * HIGH * NY : RANK * HIGH * NY + (HIGH - 1) * NY, :]
+    low, own = (LOW - 1) * NY, OWN * NY
+    rates_all[:low, :] = rates_low[...]
+    rates_all[low : low + own, :] = rates[...]
+    rates_all[low + own :, :] = rates_high[: (HIGH - 1) * NY, :]
+    lane = lanes((8 * RANK, 128))
+    low_lane = (lane >= 64) & (lane < 96)
 
     for n in range(SUB):
-        whi, wlo = split(wk[min(n, 1)])
-        wboth = jnp.concatenate([whi, wlo], axis=0)
+        w = wk[min(n, 1)]
+        w_hi = w.astype(bf16).astype(f32)
+        w = jnp.where(low_lane, w - w_hi, w_hi).astype(bf16)[:, :96]
         src, dst = sets[order[n]], sets[order[n + 1]]
         final = n == SUB - 1
-
-        def step(t, carry, src=src, dst=dst, whi=whi, wboth=wboth, final=final):
-            for c in range(PLANE // CHUNK):
-                at = pl.multiple_of(t * PAD + NZ + c * CHUNK, 128)
-
-                def stack(main, minus, plus):
-                    return jnp.concatenate(
-                        [
-                            main[:, pl.ds(at, CHUNK)],
-                            main[:, pl.ds(pl.multiple_of(at - PAD, 128), CHUNK)],
-                            main[:, pl.ds(pl.multiple_of(at + PAD, 128), CHUNK)],
-                            main[:, pl.ds(pl.multiple_of(at - NZ, 128), CHUNK)],
-                            main[:, pl.ds(pl.multiple_of(at + NZ, 128), CHUNK)],
-                            minus[:, pl.ds(at, CHUNK)],
-                            plus[:, pl.ds(at, CHUNK)],
-                        ],
-                        axis=0,
-                    )
-
-                mixed = dot(wboth, stack(src[0], src[2], src[4]))
-                mixed = mixed[:64] + mixed[64:] + dot(whi, stack(src[1], src[3], src[5]))
-                for i in range(CHUNK // NZ):
-                    y = c * (CHUNK // NZ) + i
-                    cell = slice(i * NZ, (i + 1) * NZ)
-                    rate = rates_all[pl.ds((t - 1) * NY + y, 1), :]
-                    block = mixed[:RANK, cell] + rate * mixed[RANK:, cell]
-                    store(dst, t, y, block, 1 if final else 2)
-                    if final:
-                        spot = pl.multiple_of((t - LOW + 1) * PLANE + y * NZ, 128)
-                        new[:, pl.ds(spot, NZ)] = block
-                        a, b = split(block * rate)
-                        ch[:, pl.ds(spot, NZ)] = a
-                        cl[:, pl.ds(spot, NZ)] = b
+        begin, end = 1 + n, WIDE - 1 - n
+
+        def tile(t, j, src=src):
+            at = pl.multiple_of(t * PLANE + j * 256, 256)
+            a, b = src[0][:, pl.ds(at, 256)], src[1][:, pl.ds(at, 256)]
+            return jnp.concatenate([a, b, a], axis=0)
+
+        def put(t, y, block, dst=dst, final=final):
+            at = pl.multiple_of(t * PLANE + y * NZ, 128)
+            a, b = split(block)
+            dst[0][:, pl.ds(at, NZ)] = a
+            dst[1][:, pl.ds(at, NZ)] = b
+            if final:
+                new[:, pl.ds(pl.multiple_of((t - 2) * PLANE + y * NZ, 128), NZ)] = block
+
+        def step(t, carry, w=w, tile=tile, put=put):
+            held = None
+            first = None
+            for j in range(NY // 2):
+                mixed = dot(w, tile(t, j))
+                for i in range(2):
+                    y = 2 * j + i
+                    cell = slice(y * NZ, (y + 1) * NZ)
+                    part = [mixed[k * RANK : (k + 1) * RANK, i * NZ : (i + 1) * NZ] for k in range(8)]
+                    put(t - 1, y, partial[:, cell] + part[3])
+                    base = part[0] + rates_all[pl.ds((t - 1) * NY + y, 1), :] * part[1] + passed[:, cell]
+                    passed[:, cell] = part[2]
+                    base = base + roll_lanes(part[6], 1) + roll_lanes(part[7], -1)
+                    if y == 0:
+                        first = (base, part[5])
+                    elif y == 1:
+                        held_base = base + held[1]
+                    else:
+                        partial[:, (y - 1) * NZ : y * NZ] = held[0] + part[5]
+                        held_base = base + held[1]
+                    if y == 1:
+                        first = (first[0] + part[5], first[1])
+                    held = (held_base if y > 0 else base, part[4])
+            partial[:, (NY - 1) * NZ :] = held[0] + first[1]
+            partial[:, :NZ] = first[0] + held[1]
             return carry
 
-        lax.fori_loop(1 + n, WIDE - 1 - n, step, 0)
+        for j in range(NY // 2):
+            passed[:, j * 256 : (j + 1) * 256] = dot(w[2 * RANK : 3 * RANK], tile(begin - 1, j))
+        lax.fori_loop(begin, end, step, 0)
+        for j in range(NY // 2):
+            mixed = dot(w[3 * RANK : 4 * RANK], tile(end, j))
+            for i in range(2):
+                y = 2 * j + i
+                put(end - 1, y, partial[:, y * NZ : (y + 1) * NZ] + mixed[:, i * NZ : (i + 1) * NZ])
 
     done = sets[order[SUB]]
 
     def body(p, carry):
         t, c = carry
-        at = pl.multiple_of((p + LOW) * PAD + NZ, 128)
-        spot = pl.multiple_of((p + 1) * PLANE, 128)
-
-        def stack(main, minus):
-            return jnp.concatenate(
-                [
-                    main[:, pl.ds(at, PLANE)],
-                    main[:, pl.ds(pl.multiple_of(at - PAD, 128), PLANE)],
-                    main[:, pl.ds(pl.multiple_of(at - NZ, 128), PLANE)],
-                    minus[:, pl.ds(at, PLANE)],
-                ],
-                axis=0,
-            )
-
-        sh, sl = stack(done[0], done[2]), stack(done[1], done[3])
+        at = pl.multiple_of((p + LOW) * PLANE, 128)
+        turned, relaxed = [], []
+        for y in range(NY):
+            block = new[:, pl.ds(pl.multiple_of((p + 2) * PLANE + y * NZ, 128), NZ)]
+            turned.append(split(roll_lanes(block, 1)))
+            relaxed.append(split(block * rates[pl.ds(p * NY + y, 1), :]))
+
+        def stacks(k):
+            here = done[k][:, pl.ds(at, PLANE)]
+            wrapped = jnp.concatenate([here[:, PLANE - NZ :], here[:, : PLANE - NZ]], axis=1)
+            behind = done[k][:, pl.ds(pl.multiple_of(at - PLANE, 128), PLANE)]
+            rolled = jnp.concatenate([block[k] for block in turned], axis=1)
+            scaled = jnp.concatenate([block[k] for block in relaxed], axis=1)
+            old = (raw_hi, raw_lo)[k][:, pl.ds(at, PLANE)]
+            return jnp.concatenate([here, behind, wrapped, rolled], axis=0), jnp.concatenate([scaled, old], axis=0)
+
+        (sh, oh), (sl, ol) = stacks(0), stacks(1)
         both = jnp.concatenate([sh[:RANK], sl[:RANK]], axis=0)
         part = dot_t(both, sh)
         t = t + part[:RANK] + part[RANK:] + dot_t(sh[:RANK], sl)
-        oh = jnp.concatenate([ch[:, pl.ds(spot, PLANE)], raw[0][:, pl.ds(at, PLANE)]], axis=0)
-        ol = jnp.concatenate([cl[:, pl.ds(spot, PLANE)], raw[1][:, pl.ds(at, PLANE)]], axis=0)
         part = dot_t(both, oh)
         c = c + part[:RANK] + part[RANK:] + dot_t(sh[:RANK], ol)
         return t, c
@@ -593,14 +588,14 @@
     out[:, 128:] = jnp.concatenate([c, jnp.zeros((RANK, 64), f32)], axis=1)
 
 
-def evolve_space(wk, filled, rates, rates_below, rates_above):
+def evolve_space(wk, filled, rates):
     return call(
-        evolve_space_kernel, [((RANK, (OWN + 1) * PLANE), f32), ((RANK, 256), f32)], "v" * 10,
-        (wk, *filled, rates, rates_below, rates_above),
-        [pltpu.VMEM(((WIDE - 2) * NY, NZ), f32)]
-        + [pltpu.VMEM((RANK, (OWN + 1) * PLANE), bf16)] * 2
-        + [pltpu.VMEM((RANK, WIDE * PAD), bf16)] * 12,
-        name="evolve_space",
+        evolve_space_kernel, [((RANK, (OWN + 2) * PLANE), f32), ((RANK, 256), f32)], "v" * 6,
+        (wk, filled[0], filled[1], rates, filled[2], filled[3]),
+        [pltpu.VMEM((RATES, NZ), f32)]
+        + [pltpu.VMEM((RANK, PLANE), f32)] * 2
+        + [pltpu.VMEM((RANK, WIDE * PLANE), bf16)] * 4,
+        mib=16,
     )
 
 
@@ -623,7 +618,7 @@
     def out_space(p, carry):
         for half in range(2):
             size = PLANE // 2
-            at = pl.multiple_of((p + 1) * PLANE + half * size, 128)
+            at = pl.multiple_of((p + 2) * PLANE + half * size, 128)
             hi, lo = split(kinetic[:, pl.ds(at, size)])
             made = dot(w_space, jnp.concatenate([hi, lo, hi], axis=0))
             for y in range(NY // 2):
@@ -669,7 +664,7 @@
 
     return call(
         kernel, [((RANK * OWN * NY, NZ), f32), ((RANK, RANK), f32), (spread.shape, f32)], "vvvvvvv",
-        (*parts, core, kinetic, spread), name="finish",
+        (*parts, core, kinetic, spread), mib=12,
     )
 
 
@@ -692,26 +687,31 @@
 def per_device(space_factor, core_matrix, velocity_factor, collision_rates):
     devices = lax.axis_size("space")
     up = [(i, (i + 1) % devices) for i in range(devices)]
-    down = [((i + 1) % devices, i) for i in range(devices)]
     below1 = lax.ppermute(space_factor[:, OWN - 1 :], "space", up).reshape(-1, NZ)
-    lower = jnp.concatenate([space_factor[:, : OWN - 1], collision_rates[None, 1:]], axis=0)
-    upper = jnp.concatenate([space_factor[:, :HIGH], collision_rates[None, :HIGH]], axis=0)
-    lower = lax.ppermute(lower, "space", up).reshape(-1, NZ)
-    upper = lax.ppermute(upper, "space", down).reshape(-1, NZ)
     rates = collision_rates.reshape(-1, NZ)
     values = space_factor.reshape(-1, NZ)
     cells_total = OWN * PLANE * devices
     points_total = velocity_factor.shape[1] * lax.axis_size("vel")
-    v = lax.axis_index("vel").astype(jnp.int32).reshape(1)
-
-    inner = space_sums(values, rates)
-    space = edge_sums(values, below1, inner)
+    place = lax.axis_index("vel").astype(jnp.int32)
+    v = place.reshape(1)
+    planes = jnp.where(place % 2 == 0, space_factor[:, : OWN - 1], space_factor[:, :HIGH])
+    lines = jnp.where(place % 2 == 0, collision_rates[1:], collision_rates[:HIGH])
+    halo = jnp.concatenate([planes, lines[None]], axis=0)
+    route = [(s * 8 + w, (s + 1 - 2 * (w % 2)) % devices * 8 + w) for s in range(devices) for w in range(8)]
+    pair = [(w, w ^ 1) for w in range(8)]
+
+    inner, own_hi, own_lo = space_sums(values, rates)
+    halo, inner = lax.optimization_barrier((halo, inner))
+    mine = lax.ppermute(halo, ("space", "vel"), route)
+    space, *edge = edge_sums(own_hi, own_lo, below1, inner)
     moved = spread_pairs(space)
     point = point_sums(v, velocity_factor, space)
+    mine, point = lax.optimization_barrier((mine, point))
+    other = lax.ppermute(mine, "vel", pair)
     parts = vel_parts(moved, point)
-    filled = fill_planes(values, lower, below1, upper, parts[0])
+    filled = fill_planes(v, (own_hi, own_lo), edge, mine.reshape(-1, NZ), other.reshape(-1, NZ), parts[0])
     wk, wl, src = small_first(parts, core_matrix, filled[0], cells_total, points_total)
-    kinetic, space = evolve_space(wk, filled, rates, lower, upper)
+    kinetic, space = evolve_space(wk, filled, rates)
     moved = spread_pairs(space)
     spread, point = evolve_point(v, wl, src, velocity_factor, space)
     parts = vel_parts(moved, point)

time: 141 us -> 109 us (0.77)
  the two profiles are of different devices: /device:TPU:1 before, /device:TPU:4 now
where the time goes in v2:
time: 109 us
  Pallas kernels  48.6 us (45%)
  starting transfers between devices  30.2 us (28%)
  waiting for transfers between devices  27.6 us (25%)
    pallas_call x8, Pallas kernels, call(): pl.pallas_call(kernel, out_shape=[jax.ShapeDtypeStruct(s, d) for s, d in...  48.6 us
    ppermute x6, starting transfers between devices, vel_parts(): return [joint] + [lax.ppermute(joint, 'vel', route) for route in routes]  14.5 us
    ppermute x1, waiting for transfers between devices, per_device(): lax.ppermute(space_factor[:, OWN - 1:], 'space', up).reshape(-1, NZ)  14.3 us
    ppermute x6, waiting for transfers between devices, vel_parts(): return [joint] + [lax.ppermute(joint, 'vel', route) for route in routes]  9.65 us
    ppermute x2, starting transfers between devices, vel_parts(): joint = joint + lax.ppermute(joint, 'vel', pair)  6.67 us
    ppermute x4, starting transfers between devices, spread_pairs(): moved.append(lax.ppermute(space_part, ('space', 'vel'), route))  6.18 us
  transfers between devices with their start and end apart: 15, of which 10 were waited for; matrix products, arithmetic and copies ran while one was open for 0% of the time, Pallas kernels for 15%

profile of v2, /device:TPU:4, one launch (start us, length us, event | category | flops | bytes accessed | tf_op | source)
XLA Modules:
  0.0 108.8 jit_solution(1436122684371400027)
XLA Ops:
  0.6 0.0 slice-start
  0.6 0.0 copy-start.1
  0.7 0.0 copy-start.2
  0.7 0.9 select_bitcast_fusion
  1.6 0.2 slice-done
  1.8 0.1 pad_maximum_fusion
  1.9 0.0 copy-start
  1.9 0.0 copy-start.3
  1.9 0.0 copy-start.4
  1.9 0.0 copy-start.7
  1.9 0.0 copy-start.9
  1.9 0.2 copy-done.1
  2.1 0.0 copy-done.2
  2.1 3.7 %shard_map.121 = (f32[32,256]{1,0:T(8,128)S(1)}, bf16[32,8192]{1,0:T(8,128)(2,1)S(1)}, bf16[32,8192]{1,0:T(8,128)(2,1)S(1)}) custom-call(f32[2048,128]{1,0:T(8,128)S(1)} %bitcast.9, f32[64,128]{1,0:T(8,128)S(1)} %bitcast.12), custom_call_target="tpu_custom_call" | custom-call | tf_op jit(solution)/shard_map/pallas_call | solution.py:123
  5.8 1.2 %collective-permute-start.3 = (f32[33,3,16,128]{3,2,1,0:T(8,128)S(1)}, f32[33,3,16,128]{3,2,1,0:T(8,128)S(1)}, u32[]{:S(2)}, u32[]{:S(2)}) collective-permute-start(f32[33,3,16,128]{3,2,1,0:T(8,128)S(1)} %pad_maximum_fusion), channel_id=1, source_target_pairs={{0,8},{1,121},{2,10},{3,123},{4,12},{5,125},{6,14},{7,127},{8,16},... | collective-permute-start | bytes 2433032 | tf_op jit(solution)/shard_map/ppermute | solution.py:705
  7.0 1.6 %collective-permute-start = (f32[32,1,16,128]{3,2,1,0:T(8,128)S(1)}, f32[32,1,16,128]{3,2,1,0:T(8,128)S(1)}, u32[]{:S(2)}, u32[]{:S(2)}) collective-permute-start(f32[32,1,16,128]{3,2,1,0:T(8,128)S(1)} %slice.13), channel_id=1, source_target_pairs={{0,8},{8,16},{16,24},{24,32},{32,40},{40,48},{48,56},{56,64},{64,7... | collective-permute-start | bytes 786440 | tf_op jit(solution)/shard_map/ppermute | solution.py:690
  8.6 14.3 %collective-permute-done = f32[32,1,16,128]{3,2,1,0:T(8,128)S(1)} collective-permute-done((f32[32,1,16,128]{3,2,1,0:T(8,128)S(1)}, f32[32,1,16,128]{3,2,1,0:T(8,128)S(1)}, u32[]{:S(2)}, u32[]{:S(2)}) %collective-permute-start) | collective-permute-done | bytes 262176 | tf_op jit(solution)/shard_map/ppermute | solution.py:690
  22.9 0.3 shard_map.122
  23.2 0.0 copy-done
  23.2 0.0 copy-done.3
  23.2 0.0 copy-done.4
  23.2 0.0 copy-done.7
  23.2 0.0 copy-done.9
  23.3 4.8 %shard_map.123 = f32[32,256]{1,0:T(8,128)S(1)} custom-call(s32[1]{0:T(128)} %bitcast.4.v_ref, f32[144]{0:T(256)S(1)} %copy-done.9, f32[2,8,1152]{2,1,0:T(8,128)S(1)} %copy-done.4, f32[2,32,1152]{2,1,0:T(8,128)S(1)} %copy-done.3, f32[48,128]{1,0:T(8,128)S(1)} %copy-done.7, f32[32,13824]{1,0:T(8,128)S(1)} %copy-done, f32[32,256]{1,0:T(8,128)S(1)} %get-tuple-element.31.after), custom_call_target="tpu_custom_call" | custom-call | tf_op jit(solution)/shard_map/pallas_call | solution.py:123
  28.1 0.0 copy-start.5
  28.1 0.0 copy-start.6
  28.1 0.0 copy-start.8
  28.1 0.0 collective-permute-done.3
  28.1 0.1 collective-permute-start.8
  28.2 1.6 %collective-permute-start.2 = (f32[32,256]{1,0:T(8,128)S(1)}, f32[32,256]{1,0:T(8,128)S(1)}, u32[]{:S(2)}, u32[]{:S(2)}) collective-permute-start(f32[32,256]{1,0:T(8,128)S(1)} %get-tuple-element.31.after), channel_id=1, source_target_pairs={{8,0},{25,1},{42,2},{59,3},{76,4},{93,5},{110,6},{127,7},{0,8},{17... | collective-permute-start | bytes 98312 | tf_op jit(solution)/shard_map/ppermute | solution.py:675
  29.8 0.7 collective-permute-start.1
  30.4 1.8 %collective-permute-done.2 = f32[32,256]{1,0:T(8,128)S(1)} collective-permute-done((f32[32,256]{1,0:T(8,128)S(1)}, f32[32,256]{1,0:T(8,128)S(1)}, u32[]{:S(2)}, u32[]{:S(2)}) %collective-permute-start.2) | collective-permute-done | bytes 32800 | tf_op jit(solution)/shard_map/ppermute | solution.py:675
  32.2 0.0 collective-permute-done.1
  32.2 4.0 %collective-permute-start.4 = (f32[64,256]{1,0:T(8,128)S(1)}, f32[64,256]{1,0:T(8,128)S(1)}, u32[]{:S(2)}, u32[]{:S(2)}) collective-permute-start(f32[64,256]{1,0:T(8,128)S(1)} %pad_maximum_fusion.2), channel_id=1, source_target_pairs={{0,1},{1,0},{2,3},{3,2},{4,5},{5,4},{6,7},{7,6},{8,9},{9,8},{10,11... | collective-permute-start | bytes 196616 | tf_op jit(solution)/shard_map/ppermute | solution.py:682
  36.2 0.9 collective-permute-done.4
  37.1 8.4 %collective-permute-start.7 = (f32[64,256]{1,0:T(8,128)S(1)}, f32[64,256]{1,0:T(8,128)S(1)}, u32[]{:S(2)}, u32[]{:S(2)}) collective-permute-start(f32[64,256]{1,0:T(8,128)S(1)} %fusion.after.refs_0_), channel_id=1, source_target_pairs={{0,6},{1,7},{2,0},{3,1},{4,2},{5,3},{6,4},{7,5},{8,14},{9,15},{10,... | collective-permute-start | bytes 196616 | tf_op jit(solution)/shard_map/ppermute | solution.py:684
  45.6 0.4 collective-permute-start.6
  46.0 1.3 %collective-permute-start.5 = (f32[64,256]{1,0:T(8,128)S(1)}, f32[64,256]{1,0:T(8,128)S(1)}, u32[]{:S(2)}, u32[]{:S(2)}) collective-permute-start(f32[64,256]{1,0:T(8,128)S(1)} %fusion.after.refs_0_), channel_id=1, source_target_pairs={{0,2},{1,3},{2,4},{3,5},{4,6},{5,7},{6,0},{7,1},{8,10},{9,11},{10,... | collective-permute-start | bytes 196616 | tf_op jit(solution)/shard_map/ppermute | solution.py:684
  47.3 0.0 collective-permute-done.8
  47.3 0.7 shard_map.124
  48.0 0.9 collective-permute-done.7.refs_3_
  48.9 3.0 %collective-permute-done.6.refs_2_ = f32[64,256]{1,0:T(8,128)S(1)} collective-permute-done((f32[64,256]{1,0:T(8,128)S(1)}, f32[64,256]{1,0:T(8,128)S(1)}, u32[]{:S(2)}, u32[]{:S(2)}) %collective-permute-start.6) | collective-permute-done | bytes 65568 | tf_op jit(solution)/shard_map/ppermute | solution.py:684
  51.9 0.7 collective-permute-done.5.refs_1_
  52.6 0.0 copy-done.5
  52.6 0.0 copy-done.6
  52.6 0.0 copy-done.8
  52.6 4.5 %shard_map.125 = (f32[2,256,128]{2,1,0:T(8,128)S(1)}, f32[2,224,128]{2,1,0:T(8,128)S(1)}, f32[3,32,128]{2,1,0:T(8,128)S(1)}) custom-call(f32[64,256]{1,0:T(8,128)S(1)} %fusion.after.refs_0_, f32[64,256]{1,0:T(8,128)S(1)} %collective-permute-done.5.refs_1_, f32[64,256]{1,0:T(8,128)S(1)} %collective-permute-done.6.refs_2_, ...), custom_call_target="tpu_custom_call" | custom-call | tf_op jit(solution)/shard_map/pallas_call | solution.py:123
  57.1 14.4 %shard_map.126 = (f32[32,12288]{1,0:T(8,128)S(1)}, f32[32,256]{1,0:T(8,128)S(1)}) custom-call(f32[2,256,128]{2,1,0:T(8,128)S(1)} %get-tuple-element.38.wk, bf16[32,22528]{1,0:T(8,128)(2,1)S(1)} %get-tuple-element.37.refs_7_.raw_hi, bf16[32,22528]{1,0:T(8,128)(2,1)S(1)} %get-tuple-element.39.raw_lo, f32[64,128]{1,0:T(8,128)S(1)} %bitcast.13, ...), custom_call_target="tpu_custom_call" | custom-call | tf_op jit(solution)/shard_map/pallas_call | solution.py:123
  71.5 3.3 %collective-permute-start.10 = (f32[32,256]{1,0:T(8,128)S(1)}, f32[32,256]{1,0:T(8,128)S(1)}, u32[]{:S(2)}, u32[]{:S(2)}) collective-permute-start(f32[32,256]{1,0:T(8,128)S(1)} %get-tuple-element.42.after), channel_id=1, source_target_pairs={{8,0},{25,1},{42,2},{59,3},{76,4},{93,5},{110,6},{127,7},{0,8},{17... | collective-permute-start | bytes 98312 | tf_op jit(solution)/shard_map/ppermute | solution.py:675
  74.8 0.7 collective-permute-start.9
  75.5 10.8 %shard_map.127 = (f32[32,13824]{1,0:T(8,128)S(1)}, f32[40,256]{1,0:T(8,128)S(1)}) custom-call(s32[1]{0:T(128)} %bitcast.4.v_ref, f32[144]{0:T(256)S(1)} %copy-done.9, f32[2,8,1152]{2,1,0:T(8,128)S(1)} %copy-done.4, f32[2,224,128]{2,1,0:T(8,128)S(1)} %get-tuple-element.43.wl, f32[3,32,128]{2,1,0:T(8,128)S(1)} %get-tuple-element.44.src, ...), custom_call_target="tpu_custom_call" | custom-call | tf_op jit(solution)/shard_map/pallas_call | solution.py:123
  86.4 0.0 collective-permute-done.10
  86.4 0.0 collective-permute-done.9
  86.4 2.7 %collective-permute-start.11 = (f32[72,256]{1,0:T(8,128)S(1)}, f32[72,256]{1,0:T(8,128)S(1)}, u32[]{:S(2)}, u32[]{:S(2)}) collective-permute-start(f32[72,256]{1,0:T(8,128)S(1)} %pad_maximum_fusion.1), channel_id=1, source_target_pairs={{0,1},{1,0},{2,3},{3,2},{4,5},{5,4},{6,7},{7,6},{8,9},{9,8},{10,11... | collective-permute-start | bytes 221192 | tf_op jit(solution)/shard_map/ppermute | solution.py:682
  89.1 0.9 collective-permute-done.11
  90.0 2.3 %collective-permute-start.14 = (f32[72,256]{1,0:T(8,128)S(1)}, f32[72,256]{1,0:T(8,128)S(1)}, u32[]{:S(2)}, u32[]{:S(2)}) collective-permute-start(f32[72,256]{1,0:T(8,128)S(1)} %fusion.1.refs_0_), channel_id=1, source_target_pairs={{0,6},{1,7},{2,0},{3,1},{4,2},{5,3},{6,4},{7,5},{8,14},{9,15},{10,... | collective-permute-start | bytes 221192 | tf_op jit(solution)/shard_map/ppermute | solution.py:684
  92.3 0.7 collective-permute-start.13
  93.0 1.3 %collective-permute-start.12 = (f32[72,256]{1,0:T(8,128)S(1)}, f32[72,256]{1,0:T(8,128)S(1)}, u32[]{:S(2)}, u32[]{:S(2)}) collective-permute-start(f32[72,256]{1,0:T(8,128)S(1)} %fusion.1.refs_0_), channel_id=1, source_target_pairs={{0,2},{1,3},{2,4},{3,5},{4,6},{5,7},{6,0},{7,1},{8,10},{9,11},{10,... | collective-permute-start | bytes 221192 | tf_op jit(solution)/shard_map/ppermute | solution.py:684
  94.3 0.3 collective-permute-done.14.refs_3_
  94.6 4.1 %collective-permute-done.13.refs_2_ = f32[72,256]{1,0:T(8,128)S(1)} collective-permute-done((f32[72,256]{1,0:T(8,128)S(1)}, f32[72,256]{1,0:T(8,128)S(1)}, u32[]{:S(2)}, u32[]{:S(2)}) %collective-permute-start.13) | collective-permute-done | bytes 73760 | tf_op jit(solution)/shard_map/ppermute | solution.py:684
  98.7 0.8 collective-permute-done.12.refs_1_
  99.4 9.4 %shard_map.128 = (f32[2048,128]{1,0:T(8,128)}, f32[32,32]{1,0:T(8,128)}, f32[32,13824]{1,0:T(8,128)}) custom-call(f32[72,256]{1,0:T(8,128)S(1)} %fusion.1.refs_0_, f32[72,256]{1,0:T(8,128)S(1)} %collective-permute-done.12.refs_1_, f32[72,256]{1,0:T(8,128)S(1)} %collective-permute-done.13.refs_2_, f32[72,256]{1,0:T(8,128)S(1)} %collective-permute-done.14.refs_3_, ...), custom_call_target="tpu_custom_call" | custom-call | tf_op jit(solution)/shard_map/pallas_call | solution.py:123
  (7 shorter events, 0.1 us)
Async XLA Ops:
  0.6 1.2 %slice-start = ((f32[32,4,16,128]{3,2,1,0:T(8,128)}), f32[32,3,16,128]{3,2,1,0:T(8,128)S(1)}, s32[]{:S(2)}) async-start(f32[32,4,16,128]{3,2,1,0:T(8,128)} %param.10), calls=%async_computation | async-start | bytes 1572864 | tf_op jit(solution)/shard_map/slice | solution.py:697
  0.6 1.5 %copy-start.1 = (f32[32,4,16,128]{3,2,1,0:T(8,128)S(1)}, f32[32,4,16,128]{3,2,1,0:T(8,128)}, u32[]{:S(2)}) copy-start(f32[32,4,16,128]{3,2,1,0:T(8,128)} %param.10) | copy-start | bytes 3145732
  0.7 1.5 %copy-start.2 = (f32[4,16,128]{2,1,0:T(8,128)S(1)}, f32[4,16,128]{2,1,0:T(8,128)}, u32[]{:S(2)}) copy-start(f32[4,16,128]{2,1,0:T(8,128)} %param.13) | copy-start | bytes 98308
  1.9 21.4 %copy-start = (f32[32,13824]{1,0:T(8,128)S(1)}, f32[32,13824]{1,0:T(8,128)}, u32[]{:S(2)}) copy-start(f32[32,13824]{1,0:T(8,128)} %values.3) | copy-start | bytes 5308420
  1.9 21.4 %copy-start.3 = (f32[2,32,1152]{2,1,0:T(8,128)S(1)}, f32[2,32,1152]{2,1,0:T(8,128)}, u32[]{:S(2)}) copy-start(f32[2,32,1152]{2,1,0:T(8,128)} %constant.34.clone.phi) | copy-start | bytes 884740
  1.9 21.3 %copy-start.4 = (f32[2,8,1152]{2,1,0:T(8,128)S(1)}, f32[2,8,1152]{2,1,0:T(8,128)}, u32[]{:S(2)}) copy-start(f32[2,8,1152]{2,1,0:T(8,128)} %constant.33.clone.rows) | copy-start | bytes 221188
  1.9 21.3 %copy-start.7 = (f32[48,128]{1,0:T(8,128)S(1)}, f32[48,128]{1,0:T(8,128)}, u32[]{:S(2)}) copy-start(f32[48,128]{1,0:T(8,128)} %constant.35.clone.scale) | copy-start | bytes 73732
  1.9 21.3 %copy-start.9 = (f32[144]{0:T(256)S(1)}, f32[144]{0:T(256)}, u32[]{:S(2)}) copy-start(f32[144]{0:T(256)} %constant.32.clone.speeds) | copy-start | bytes 1732
  5.8 22.3 %collective-permute-start.3 = (f32[33,3,16,128]{3,2,1,0:T(8,128)S(1)}, f32[33,3,16,128]{3,2,1,0:T(8,128)S(1)}, u32[]{:S(2)}, u32[]{:S(2)}) collective-permute-start(f32[33,3,16,128]{3,2,1,0:T(8,128)S(1)} %pad_maximum_fusion), channel_id=1, source_target_pairs={{0,8},{1,121},{2,10},{3,123},{4,12},{5,125},{6,14},{7,127},{8,16},... | collective-permute-start | bytes 2433032 | tf_op jit(solution)/shard_map/ppermute | solution.py:705
  7.0 15.9 %collective-permute-start = (f32[32,1,16,128]{3,2,1,0:T(8,128)S(1)}, f32[32,1,16,128]{3,2,1,0:T(8,128)S(1)}, u32[]{:S(2)}, u32[]{:S(2)}) collective-permute-start(f32[32,1,16,128]{3,2,1,0:T(8,128)S(1)} %slice.13), channel_id=1, source_target_pairs={{0,8},{8,16},{16,24},{24,32},{32,40},{40,48},{48,56},{56,64},{64,7... | collective-permute-start | bytes 786440 | tf_op jit(solution)/shard_map/ppermute | solution.py:690
  28.1 24.5 %copy-start.5 = (f32[32,896]{1,0:T(8,128)S(1)}, f32[32,896]{1,0:T(8,128)}, u32[]{:S(2)}) copy-start(f32[32,896]{1,0:T(8,128)} %constant.36.clone.refs_5_) | copy-start | bytes 344068
  28.1 24.5 %copy-start.6 = (f32[32,32]{1,0:T(8,128)S(1)}, f32[32,32]{1,0:T(8,128)}, u32[]{:S(2)}) copy-start(f32[32,32]{1,0:T(8,128)} %refs_4_.3) | copy-start | bytes 12292
  28.1 24.5 %copy-start.8 = (f32[8,128]{1,0:T(8,128)S(1)}, f32[8,128]{1,0:T(8,128)}, u32[]{:S(2)}) copy-start(f32[8,128]{1,0:T(8,128)} %constant.37.clone.refs_6_) | copy-start | bytes 12292
  28.1 19.2 %collective-permute-start.8 = (f32[33,3,16,128]{3,2,1,0:T(8,128)S(1)}, f32[33,3,16,128]{3,2,1,0:T(8,128)S(1)}, u32[]{:S(2)}, u32[]{:S(2)}) collective-permute-start(f32[33,3,16,128]{3,2,1,0:T(8,128)S(1)} %collective-permute-done.3), channel_id=1, source_target_pairs={{0,1},{1,0},{2,3},{3,2},{4,5},{5,4},{6,7},{7,6},{8,9},{9,8},{10,11... | collective-permute-start | bytes 2433032 | tf_op jit(solution)/shard_map/ppermute | solution.py:710
  28.2 4.0 %collective-permute-start.2 = (f32[32,256]{1,0:T(8,128)S(1)}, f32[32,256]{1,0:T(8,128)S(1)}, u32[]{:S(2)}, u32[]{:S(2)}) collective-permute-start(f32[32,256]{1,0:T(8,128)S(1)} %get-tuple-element.31.after), channel_id=1, source_target_pairs={{8,0},{25,1},{42,2},{59,3},{76,4},{93,5},{110,6},{127,7},{0,8},{17... | collective-permute-start | bytes 98312 | tf_op jit(solution)/shard_map/ppermute | solution.py:675
  29.8 2.4 %collective-permute-start.1 = (f32[32,256]{1,0:T(8,128)S(1)}, f32[32,256]{1,0:T(8,128)S(1)}, u32[]{:S(2)}, u32[]{:S(2)}) collective-permute-start(f32[32,256]{1,0:T(8,128)S(1)} %get-tuple-element.31.after), channel_id=1, source_target_pairs={{0,0},{17,1},{34,2},{51,3},{68,4},{85,5},{102,6},{119,7},{8,8},{25... | collective-permute-start | bytes 98312 | tf_op jit(solution)/shard_map/ppermute | solution.py:675
  32.2 4.9 %collective-permute-start.4 = (f32[64,256]{1,0:T(8,128)S(1)}, f32[64,256]{1,0:T(8,128)S(1)}, u32[]{:S(2)}, u32[]{:S(2)}) collective-permute-start(f32[64,256]{1,0:T(8,128)S(1)} %pad_maximum_fusion.2), channel_id=1, source_target_pairs={{0,1},{1,0},{2,3},{3,2},{4,5},{5,4},{6,7},{7,6},{8,9},{9,8},{10,11... | collective-permute-start | bytes 196616 | tf_op jit(solution)/shard_map/ppermute | solution.py:682
  37.1 11.7 %collective-permute-start.7 = (f32[64,256]{1,0:T(8,128)S(1)}, f32[64,256]{1,0:T(8,128)S(1)}, u32[]{:S(2)}, u32[]{:S(2)}) collective-permute-start(f32[64,256]{1,0:T(8,128)S(1)} %fusion.after.refs_0_), channel_id=1, source_target_pairs={{0,6},{1,7},{2,0},{3,1},{4,2},{5,3},{6,4},{7,5},{8,14},{9,15},{10,... | collective-permute-start | bytes 196616 | tf_op jit(solution)/shard_map/ppermute | solution.py:684
  45.6 6.3 %collective-permute-start.6 = (f32[64,256]{1,0:T(8,128)S(1)}, f32[64,256]{1,0:T(8,128)S(1)}, u32[]{:S(2)}, u32[]{:S(2)}) collective-permute-start(f32[64,256]{1,0:T(8,128)S(1)} %fusion.after.refs_0_), channel_id=1, source_target_pairs={{0,4},{1,5},{2,6},{3,7},{4,0},{5,1},{6,2},{7,3},{8,12},{9,13},{10,... | collective-permute-start | bytes 196616 | tf_op jit(solution)/shard_map/ppermute | solution.py:684
  46.0 6.6 %collective-permute-start.5 = (f32[64,256]{1,0:T(8,128)S(1)}, f32[64,256]{1,0:T(8,128)S(1)}, u32[]{:S(2)}, u32[]{:S(2)}) collective-permute-start(f32[64,256]{1,0:T(8,128)S(1)} %fusion.after.refs_0_), channel_id=1, source_target_pairs={{0,2},{1,3},{2,4},{3,5},{4,6},{5,7},{6,0},{7,1},{8,10},{9,11},{10,... | collective-permute-start | bytes 196616 | tf_op jit(solution)/shard_map/ppermute | solution.py:684
  71.5 14.8 %collective-permute-start.10 = (f32[32,256]{1,0:T(8,128)S(1)}, f32[32,256]{1,0:T(8,128)S(1)}, u32[]{:S(2)}, u32[]{:S(2)}) collective-permute-start(f32[32,256]{1,0:T(8,128)S(1)} %get-tuple-element.42.after), channel_id=1, source_target_pairs={{8,0},{25,1},{42,2},{59,3},{76,4},{93,5},{110,6},{127,7},{0,8},{17... | collective-permute-start | bytes 98312 | tf_op jit(solution)/shard_map/ppermute | solution.py:675
  74.8 11.5 %collective-permute-start.9 = (f32[32,256]{1,0:T(8,128)S(1)}, f32[32,256]{1,0:T(8,128)S(1)}, u32[]{:S(2)}, u32[]{:S(2)}) collective-permute-start(f32[32,256]{1,0:T(8,128)S(1)} %get-tuple-element.42.after), channel_id=1, source_target_pairs={{0,0},{17,1},{34,2},{51,3},{68,4},{85,5},{102,6},{119,7},{8,8},{25... | collective-permute-start | bytes 98312 | tf_op jit(solution)/shard_map/ppermute | solution.py:675
  86.4 3.6 %collective-permute-start.11 = (f32[72,256]{1,0:T(8,128)S(1)}, f32[72,256]{1,0:T(8,128)S(1)}, u32[]{:S(2)}, u32[]{:S(2)}) collective-permute-start(f32[72,256]{1,0:T(8,128)S(1)} %pad_maximum_fusion.1), channel_id=1, source_target_pairs={{0,1},{1,0},{2,3},{3,2},{4,5},{5,4},{6,7},{7,6},{8,9},{9,8},{10,11... | collective-permute-start | bytes 221192 | tf_op jit(solution)/shard_map/ppermute | solution.py:682
  90.0 4.6 %collective-permute-start.14 = (f32[72,256]{1,0:T(8,128)S(1)}, f32[72,256]{1,0:T(8,128)S(1)}, u32[]{:S(2)}, u32[]{:S(2)}) collective-permute-start(f32[72,256]{1,0:T(8,128)S(1)} %fusion.1.refs_0_), channel_id=1, source_target_pairs={{0,6},{1,7},{2,0},{3,1},{4,2},{5,3},{6,4},{7,5},{8,14},{9,15},{10,... | collective-permute-start | bytes 221192 | tf_op jit(solution)/shard_map/ppermute | solution.py:684
  92.3 6.3 %collective-permute-start.13 = (f32[72,256]{1,0:T(8,128)S(1)}, f32[72,256]{1,0:T(8,128)S(1)}, u32[]{:S(2)}, u32[]{:S(2)}) collective-permute-start(f32[72,256]{1,0:T(8,128)S(1)} %fusion.1.refs_0_), channel_id=1, source_target_pairs={{0,4},{1,5},{2,6},{3,7},{4,0},{5,1},{6,2},{7,3},{8,12},{9,13},{10,... | collective-permute-start | bytes 221192 | tf_op jit(solution)/shard_map/ppermute | solution.py:684
  93.0 6.5 %collective-permute-start.12 = (f32[72,256]{1,0:T(8,128)S(1)}, f32[72,256]{1,0:T(8,128)S(1)}, u32[]{:S(2)}, u32[]{:S(2)}) collective-permute-start(f32[72,256]{1,0:T(8,128)S(1)} %fusion.1.refs_0_), channel_id=1, source_target_pairs={{0,2},{1,3},{2,4},{3,5},{4,6},{5,7},{6,0},{7,1},{8,10},{9,11},{10,... | collective-permute-start | bytes 221192 | tf_op jit(solution)/shard_map/ppermute | solution.py:684

commit v3 on v2

--- a/solution.py
+++ b/solution.py
@@ -19,11 +19,11 @@
 HALF = NVD * NVD // 2
 PLANE = NY * NZ
 WIDE = LOW + OWN + HIGH
+ROWS_K = 7 * RANK + 16
 INTERPRET = False
 
 f32 = jnp.float32
 bf16 = jnp.bfloat16
-highest = lax.Precision.HIGHEST
 
 
 def tables():
@@ -98,12 +98,16 @@
     return lax.dot_general(a, b, (((1,), (1,)), ((), ())), preferred_element_type=f32)
 
 
-def mm(a, b):
-    return jnp.dot(a, b, precision=highest, preferred_element_type=f32)
+def mm(a, b, form=dot):
+    rows = a.shape[0]
+    ah, al = split(a)
+    bh, bl = split(b)
+    main = form(jnp.concatenate([ah, al], axis=0), bh)
+    return main[:rows] + main[rows:] + form(ah, bl)
 
 
 def mm_t(a, b):
-    return lax.dot_general(a, b, (((1,), (1,)), ((), ())), precision=highest, preferred_element_type=f32)
+    return mm(a, b, dot_t)
 
 
 def lanes(shape):
@@ -118,13 +122,14 @@
     return (lanes((RANK, RANK)) == sublanes((RANK, RANK))).astype(f32)
 
 
-def call(kernel, outs, ins, args, scratch=(), mib=8):
+def call(kernel, outs, ins, args, scratch=(), mib=8, out_spaces=None):
     spaces = {"v": pltpu.VMEM, "s": pltpu.SMEM, "a": pl.ANY}
+    out_spaces = out_spaces or "v" * len(outs)
     return pl.pallas_call(
         kernel,
         out_shape=[jax.ShapeDtypeStruct(s, d) for s, d in outs],
         in_specs=[pl.BlockSpec(memory_space=spaces[c]) for c in ins],
-        out_specs=[pl.BlockSpec(memory_space=pltpu.VMEM) for _ in outs],
+        out_specs=[pl.BlockSpec(memory_space=spaces[c]) for c in out_spaces],
         scratch_shapes=list(scratch),
         compiler_params=pltpu.CompilerParams(vmem_limit_bytes=mib * 1024 * 1024),
         interpret=INTERPRET,
@@ -163,10 +168,9 @@
             lh, ll = sh[:RANK], sl[:RANK]
             ph, plo = phi_parts[h]
             both = jnp.concatenate([lh, ll], axis=0)
-            t = dot_t(both, sh)
-            t = t[:RANK] + t[RANK:] + dot_t(lh, sl)
-            m = dot_t(both, ph)
-            m = m[:RANK] + m[RANK:] + dot_t(lh, plo)
+            t = dot_t(both, jnp.concatenate([sh, ph], axis=0))
+            t = t[:RANK] + t[RANK:] + dot_t(lh, jnp.concatenate([sl, plo], axis=0))
+            t, m = t[:, :128], t[:, 128:]
             sums[h] = sums[h] + t
             y = y + u * t
             moments = moments + m * scale[pl.ds(q0 + b, 1), :RANK]
@@ -187,7 +191,7 @@
     )[0]
 
 
-def space_sums_kernel(values, rates, out, own_hi, own_lo, hi, lo, zh, zl, ch, cl):
+def space_sums_kernel(values, rates, out, own, hi, lo, zh, zl, ch, cl):
     def load(p, carry):
         for y in range(NY):
             block = values[pl.ds(p * NY + y, RANK, stride=OWN * NY), :]
@@ -195,8 +199,7 @@
             a, b = split(block)
             hi[:, pl.ds(at + PLANE, NZ)] = a
             lo[:, pl.ds(at + PLANE, NZ)] = b
-            own_hi[:, pl.ds(at, NZ)] = a
-            own_lo[:, pl.ds(at, NZ)] = b
+            own[:, pl.ds(at, NZ)] = block
             a, b = split(roll_lanes(block, 1))
             zh[:, pl.ds(at, NZ)] = a
             zl[:, pl.ds(at, NZ)] = b
@@ -222,11 +225,9 @@
 
         sh, sl = stack(hi, zh), stack(lo, zl)
         both = jnp.concatenate([sh[:RANK], sl[:RANK]], axis=0)
-        part = dot_t(both, sh)
-        t = t + part[:RANK] + part[RANK:] + dot_t(sh[:RANK], sl)
-        part = dot_t(both, ch[:, pl.ds(at, PLANE)])
-        c = c + part[:RANK] + part[RANK:] + dot_t(sh[:RANK], cl[:, pl.ds(at, PLANE)])
-        return t, c
+        part = dot_t(both, jnp.concatenate([sh, ch[:, pl.ds(at, PLANE)]], axis=0))
+        part = part[:RANK] + part[RANK:] + dot_t(sh[:RANK], jnp.concatenate([sl, cl[:, pl.ds(at, PLANE)]], axis=0))
+        return t + part[:, :128], c + part[:, 128:]
 
     t, c = lax.fori_loop(0, OWN, body, (jnp.zeros((RANK, 128), f32), jnp.zeros((RANK, RANK), f32)))
     out[:, :128] = t
@@ -236,26 +237,25 @@
 def space_sums(values, rates):
     own = (RANK, OWN * PLANE)
     return call(
-        space_sums_kernel, [((RANK, 256), f32), (own, bf16), (own, bf16)], "vv", (values, rates),
+        space_sums_kernel, [((RANK, 256), f32), (own, f32)], "vv", (values, rates),
         [pltpu.VMEM((RANK, (OWN + 1) * PLANE), bf16)] * 2 + [pltpu.VMEM(own, bf16)] * 4, mib=12,
     )
 
 
-def edge_sums_kernel(own_hi, own_lo, below, inner, out, edge_hi, edge_lo):
+def edge_sums_kernel(own, below, inner, out, edge):
     empty = jnp.zeros((RANK, PLANE), bf16)
-    oh, ol = split(jnp.concatenate([below[pl.ds(y, RANK, stride=NY), :] for y in range(NY)], axis=1))
-    edge_hi[...] = oh
-    edge_lo[...] = ol
-    lh, ll = own_hi[:, :PLANE], own_lo[:, :PLANE]
+    other = jnp.concatenate([below[pl.ds(y, RANK, stride=NY), :] for y in range(NY)], axis=1)
+    edge[...] = other
+    oh, ol = split(other)
+    lh, ll = split(own[:, :PLANE])
     part = dot_t(jnp.concatenate([lh, ll], axis=0), jnp.concatenate([empty, oh], axis=0))
     t = part[:RANK] + part[RANK:] + dot_t(lh, jnp.concatenate([empty, ol], axis=0))
     out[:, :128] = inner[:, :128] + jnp.concatenate([t, jnp.zeros((RANK, 64), f32)], axis=1)
     out[:, 128:] = inner[:, 128:]
 
 
-def edge_sums(own_hi, own_lo, below, inner):
-    plane = ((RANK, PLANE), bf16)
-    return call(edge_sums_kernel, [((RANK, 256), f32), plane, plane], "vvvv", (own_hi, own_lo, below, inner))
+def edge_sums(own, below, inner):
+    return call(edge_sums_kernel, [((RANK, 256), f32), ((RANK, PLANE), f32)], "vvv", (own, below, inner))
 
 
 def factor_pair(first, second):
@@ -294,17 +294,11 @@
     return gram, plus, minus, t[:, 224:256]
 
 
-def congruent(inverse, blocks):
-    inverse_t = transposed(inverse)
-    half = mm(jnp.concatenate(blocks, axis=0), inverse_t)
-    return [mm(inverse, half[k * RANK : (k + 1) * RANK]) for k in range(len(blocks))]
-
-
 def four(parts):
     return (parts[0][...] + parts[2][...]) + (parts[1][...] + parts[3][...])
 
 
-def small_first_kernel(cells_total, points_total, p0, p1, p2, p3, core, select, means, after, wk, wl, src):
+def small_first_kernel(cells_total, points_total, p0, p1, p2, p3, core, select, means, after, wk, wl, src, moment):
     both = four((p0, p1, p2, p3))
     s = both[:RANK] * (1.0 / cells_total)
     gram = s[:, 0:32]
@@ -351,14 +345,12 @@
     blocks = [half[:, 192:224], half[:, 128:160], half[:, 160:192], half[:, 32:64], half[:, 64:96], half[:, 96:128]]
     flux = mm(jnp.concatenate(blocks, axis=0), transposed(inverse_v))
     flux = [flux[k * RANK : (k + 1) * RANK] * (1.0 if k % 2 == 0 else -1.0) for k in range(6)]
-    center = identity
-    for block in flux:
-        center = center - block
-    relax = turned_raw[:, LAST : LAST + 1] * weights_row - identity
-    column = jnp.concatenate([center, relax] + flux, axis=0)
+    row = sublanes((16, RANK))
+    column = jnp.concatenate([identity] + flux + [jnp.where(row == 0, weights_row, 0.0)], axis=0)
     to_kinetic = transposed(to_kinetic_t)
     wk[0] = mm(column, jnp.concatenate([to_kinetic] * 3 + [zeros], axis=1))
-    wk[1] = jnp.concatenate([column] * 3 + [jnp.zeros((8 * RANK, 32), f32)], axis=1)
+    wk[1] = jnp.concatenate([column] * 3 + [jnp.zeros((ROWS_K, 32), f32)], axis=1)
+    moment[...] = jnp.broadcast_to(turned_raw[:, LAST : LAST + 1], (RANK, 128))
 
 
 def small_first(parts, core, after, cells_total, points_total):
@@ -366,7 +358,7 @@
         small_first_kernel(cells_total, points_total, *refs)
 
     return call(
-        kernel, [((2, 8 * RANK, 128), f32), ((2, 224, 128), f32), ((3, RANK, 128), f32)], "vvvvvvva",
+        kernel, [((2, ROWS_K, 128), f32), ((2, 224, 128), f32), ((3, RANK, 128), f32), ((RANK, 128), f32)], "vvvvvvva",
         (*parts, core, SELECT, MEANS, after),
     )
 
@@ -423,13 +415,13 @@
             new[:, pl.ds(start, HALF)] = state
             sh, sl = split(stacked(state, rows, h))
             lh, ll = sh[:RANK], sl[:RANK]
-            t = dot_t(jnp.concatenate([lh, ll, aux[h]], axis=0), sh)
-            t2 = dot_t(jnp.concatenate([lh, aux[h]], axis=0), sl)
+            t = dot_t(jnp.concatenate([lh, ll, aux[h]], axis=0), jnp.concatenate([sh, raw_hi], axis=0))
+            t2 = dot_t(jnp.concatenate([lh, aux[h]], axis=0), jnp.concatenate([sl, raw_lo], axis=0))
             t_main = t[:RANK] + t[RANK : 2 * RANK] + t2[:RANK]
-            cross_part = dot_t(jnp.concatenate([lh, ll], axis=0), raw_hi)
-            cross = cross + cross_part[:RANK] + cross_part[RANK:] + dot_t(lh, raw_lo)
-            a = t[2 * RANK : 2 * RANK + 8]
-            a2 = t2[RANK : RANK + 8]
+            cross = cross + t_main[:, 128:]
+            t_main = t_main[:, :128]
+            a = t[2 * RANK : 2 * RANK + 8, :128]
+            a2 = t2[RANK : RANK + 8, :128]
             row8 = sublanes((8, 128))
             a = a + jnp.where(row8 < 2, a2, 0.0)
             ones_sum = ones_sum + jnp.where(row8 == 0, a, a * g1)
@@ -460,20 +452,16 @@
 HALO = RANK * HIGH * NY
 
 
-def fill_kernel(v_ref, own_hi, own_lo, edge_hi, edge_lo, mine, other, after, hi, lo, rates_low, rates_high):
+def fill_kernel(v_ref, own, edge, mine, other, after, state, rates_low, rates_high):
     core = v_ref[0] % 2
-    hi[:, LOW * PLANE : (LOW + OWN) * PLANE] = own_hi[...]
-    lo[:, LOW * PLANE : (LOW + OWN) * PLANE] = own_lo[...]
-    hi[:, (LOW - 1) * PLANE : LOW * PLANE] = edge_hi[...]
-    lo[:, (LOW - 1) * PLANE : LOW * PLANE] = edge_lo[...]
+    state[:, LOW * PLANE : (LOW + OWN) * PLANE] = own[...]
+    state[:, (LOW - 1) * PLANE : LOW * PLANE] = edge[...]
     for source, place in ((mine, core), (other, 1 - core)):
 
         def load(p, carry, source=source, place=place):
             for y in range(NY):
-                a, b = split(source[pl.ds(p * NY + y, RANK, stride=HIGH * NY), :])
                 at = pl.multiple_of((p + place * (LOW + OWN)) * PLANE + y * NZ, 128)
-                hi[:, pl.ds(at, NZ)] = a
-                lo[:, pl.ds(at, NZ)] = b
+                state[:, pl.ds(at, NZ)] = source[pl.ds(p * NY + y, RANK, stride=HIGH * NY), :]
             return carry
 
         lax.fori_loop(0, HIGH, load, 0)
@@ -483,127 +471,121 @@
 
 
 def fill_planes(v, own, edge, mine, other, after):
-    wide = ((RANK, WIDE * PLANE), bf16)
     part = ((HIGH * NY, NZ), f32)
-    return call(fill_kernel, [wide, wide, part, part], "svvvvvva", (v, *own, *edge, mine, other, after), mib=12)
-
-
-def evolve_space_kernel(wk, raw_hi, raw_lo, rates, rates_low, rates_high, new, out, rates_all, partial, passed, *bufs):
-    sets = [(raw_hi, raw_lo), bufs[0:2], bufs[2:4]]
-    order = [0, 1, 2, 1]
+    return call(
+        fill_kernel, [((RANK, WIDE * PLANE), f32), part, part], "svvvva", (v, own, edge, mine, other, after),
+        mib=12,
+    )
+
+
+def evolve_space_kernel(wk, moment, raw, rates, rates_low, rates_high, new, out, rates_all, partial, passed, *bufs):
+    sources, targets = [raw, bufs[0], bufs[1]], [bufs[0], bufs[1], new]
     low, own = (LOW - 1) * NY, OWN * NY
     rates_all[:low, :] = rates_low[...]
     rates_all[low : low + own, :] = rates[...]
     rates_all[low + own :, :] = rates_high[: (HIGH - 1) * NY, :]
-    lane = lanes((8 * RANK, 128))
+    lane = lanes((ROWS_K, 128))
     low_lane = (lane >= 64) & (lane < 96)
 
     for n in range(SUB):
         w = wk[min(n, 1)]
         w_hi = w.astype(bf16).astype(f32)
         w = jnp.where(low_lane, w - w_hi, w_hi).astype(bf16)[:, :96]
-        src, dst = sets[order[n]], sets[order[n + 1]]
-        final = n == SUB - 1
+        if n > 0:
+            w = w[RANK:]
+        skip = w.shape[0] - ROWS_K + RANK
+        src, dst = sources[n], targets[n]
+        shift = 2 if n == SUB - 1 else 0
         begin, end = 1 + n, WIDE - 1 - n
 
         def tile(t, j, src=src):
-            at = pl.multiple_of(t * PLANE + j * 256, 256)
-            a, b = src[0][:, pl.ds(at, 256)], src[1][:, pl.ds(at, 256)]
-            return jnp.concatenate([a, b, a], axis=0)
-
-        def put(t, y, block, dst=dst, final=final):
-            at = pl.multiple_of(t * PLANE + y * NZ, 128)
-            a, b = split(block)
-            dst[0][:, pl.ds(at, NZ)] = a
-            dst[1][:, pl.ds(at, NZ)] = b
-            if final:
-                new[:, pl.ds(pl.multiple_of((t - 2) * PLANE + y * NZ, 128), NZ)] = block
-
-        def step(t, carry, w=w, tile=tile, put=put):
-            held = None
-            first = None
+            cells = src[:, pl.ds(pl.multiple_of(t * PLANE + j * 256, 256), 256)]
+            a, b = split(cells)
+            return cells, jnp.concatenate([a, b, a], axis=0)
+
+        def put(t, y, block, dst=dst, shift=shift):
+            dst[:, pl.ds(pl.multiple_of((t - shift) * PLANE + y * NZ, 128), NZ)] = block
+
+        def step(t, carry, w=w, tile=tile, put=put, skip=skip):
+            scale = moment[...]
+            bases, ups, downs = [], [], []
             for j in range(NY // 2):
-                mixed = dot(w, tile(t, j))
+                cells, operand = tile(t, j)
+                mixed = dot(w, operand)
                 for i in range(2):
                     y = 2 * j + i
                     cell = slice(y * NZ, (y + 1) * NZ)
-                    part = [mixed[k * RANK : (k + 1) * RANK, i * NZ : (i + 1) * NZ] for k in range(8)]
-                    put(t - 1, y, partial[:, cell] + part[3])
-                    base = part[0] + rates_all[pl.ds((t - 1) * NY + y, 1), :] * part[1] + passed[:, cell]
-                    passed[:, cell] = part[2]
-                    base = base + roll_lanes(part[6], 1) + roll_lanes(part[7], -1)
-                    if y == 0:
-                        first = (base, part[5])
-                    elif y == 1:
-                        held_base = base + held[1]
-                    else:
-                        partial[:, (y - 1) * NZ : y * NZ] = held[0] + part[5]
-                        held_base = base + held[1]
-                    if y == 1:
-                        first = (first[0] + part[5], first[1])
-                    held = (held_base if y > 0 else base, part[4])
-            partial[:, (NY - 1) * NZ :] = held[0] + first[1]
-            partial[:, :NZ] = first[0] + held[1]
+                    half = slice(i * NZ, (i + 1) * NZ)
+                    part = [mixed[skip + k * RANK : skip + (k + 1) * RANK, half] for k in range(6)]
+                    here = mixed[:RANK, half] if skip else cells[:, half]
+                    density = mixed[skip + 6 * RANK : skip + 6 * RANK + 1, half]
+                    put(t - 1, y, partial[:, cell] + part[1])
+                    rate = rates_all[pl.ds((t - 1) * NY + y, 1), :]
+                    base = here + rate * (scale * density - here) + passed[:, cell]
+                    passed[:, cell] = part[0]
+                    base = base - ((part[0] + part[1]) + (part[2] + part[3]) + (part[4] + part[5]))
+                    bases.append(base + roll_lanes(part[4], 1) + roll_lanes(part[5], -1))
+                    ups.append(part[2])
+                    downs.append(part[3])
+                    if y >= 2:
+                        partial[:, (y - 1) * NZ : y * NZ] = bases[y - 1] + ups[y - 2] + downs[y]
+            partial[:, (NY - 1) * NZ :] = bases[NY - 1] + ups[NY - 2] + downs[0]
+            partial[:, :NZ] = bases[0] + ups[NY - 1] + downs[1]
             return carry
 
         for j in range(NY // 2):
-            passed[:, j * 256 : (j + 1) * 256] = dot(w[2 * RANK : 3 * RANK], tile(begin - 1, j))
+            passed[:, j * 256 : (j + 1) * 256] = dot(w[skip : skip + RANK], tile(begin - 1, j)[1])
         lax.fori_loop(begin, end, step, 0)
         for j in range(NY // 2):
-            mixed = dot(w[3 * RANK : 4 * RANK], tile(end, j))
+            mixed = dot(w[skip + RANK : skip + 2 * RANK], tile(end, j)[1])
             for i in range(2):
                 y = 2 * j + i
                 put(end - 1, y, partial[:, y * NZ : (y + 1) * NZ] + mixed[:, i * NZ : (i + 1) * NZ])
 
-    done = sets[order[SUB]]
-
     def body(p, carry):
         t, c = carry
-        at = pl.multiple_of((p + LOW) * PLANE, 128)
         turned, relaxed = [], []
         for y in range(NY):
             block = new[:, pl.ds(pl.multiple_of((p + 2) * PLANE + y * NZ, 128), NZ)]
             turned.append(split(roll_lanes(block, 1)))
             relaxed.append(split(block * rates[pl.ds(p * NY + y, 1), :]))
-
-        def stacks(k):
-            here = done[k][:, pl.ds(at, PLANE)]
-            wrapped = jnp.concatenate([here[:, PLANE - NZ :], here[:, : PLANE - NZ]], axis=1)
-            behind = done[k][:, pl.ds(pl.multiple_of(at - PLANE, 128), PLANE)]
+        here = split(new[:, pl.ds(pl.multiple_of((p + 2) * PLANE, 128), PLANE)])
+        behind = split(new[:, pl.ds(pl.multiple_of((p + 1) * PLANE, 128), PLANE)])
+        old = split(raw[:, pl.ds(pl.multiple_of((p + LOW) * PLANE, 128), PLANE)])
+
+        def stack(k):
+            wrapped = jnp.concatenate([here[k][:, PLANE - NZ :], here[k][:, : PLANE - NZ]], axis=1)
             rolled = jnp.concatenate([block[k] for block in turned], axis=1)
             scaled = jnp.concatenate([block[k] for block in relaxed], axis=1)
-            old = (raw_hi, raw_lo)[k][:, pl.ds(at, PLANE)]
-            return jnp.concatenate([here, behind, wrapped, rolled], axis=0), jnp.concatenate([scaled, old], axis=0)
-
-        (sh, oh), (sl, ol) = stacks(0), stacks(1)
-        both = jnp.concatenate([sh[:RANK], sl[:RANK]], axis=0)
-        part = dot_t(both, sh)
-        t = t + part[:RANK] + part[RANK:] + dot_t(sh[:RANK], sl)
-        part = dot_t(both, oh)
-        c = c + part[:RANK] + part[RANK:] + dot_t(sh[:RANK], ol)
-        return t, c
+            return jnp.concatenate([here[k], behind[k], wrapped, rolled, scaled, old[k]], axis=0)
+
+        part = dot_t(jnp.concatenate(here, axis=0), stack(0))
+        part = part[:RANK] + part[RANK:] + dot_t(here[0], stack(1))
+        return t + part[:, :128], c + part[:, 128:]
 
     t, c = lax.fori_loop(0, OWN, body, (jnp.zeros((RANK, 128), f32), jnp.zeros((RANK, 64), f32)))
     out[:, :128] = t
     out[:, 128:] = jnp.concatenate([c, jnp.zeros((RANK, 64), f32)], axis=1)
 
 
-def evolve_space(wk, filled, rates):
+def evolve_space(wk, moment, filled, rates):
     return call(
         evolve_space_kernel, [((RANK, (OWN + 2) * PLANE), f32), ((RANK, 256), f32)], "v" * 6,
-        (wk, filled[0], filled[1], rates, filled[2], filled[3]),
+        (wk, moment, filled[0], rates, filled[1], filled[2]),
         [pltpu.VMEM((RATES, NZ), f32)]
         + [pltpu.VMEM((RANK, PLANE), f32)] * 2
-        + [pltpu.VMEM((RANK, WIDE * PLANE), bf16)] * 4,
+        + [pltpu.VMEM((RANK, WIDE * PLANE), f32)] * 2,
         mib=16,
     )
 
 
-def finish_kernel(cells_total, points_total, p0, p1, p2, p3, core, kinetic, spread, fresh_space, fresh_core, fresh_point):
+def finish_kernel(
+    cells_total, points_total, p0, p1, p2, p3, core, kinetic, spread, space_out, fresh_core, point_out, fresh_space, fresh_point, sems
+):
     both = four((p0, p1, p2, p3))
     s = both[:RANK] * (1.0 / cells_total)
-    gram = s[:, 0:32]
-    gram_v, plus, minus, cross_v = point_blocks(both[RANK : 2 * RANK], points_total)
+    q = both[RANK:] * (1.0 / points_total)
+    gram, gram_v = s[:, 0:32], q[:RANK, 0:32]
     (_, inverse), (_, inverse_v) = factor_pair(gram, gram_v)
     zeros = jnp.zeros((RANK, 32), f32)
     lane = lanes((RANK, 128))
@@ -626,45 +608,60 @@
         return carry
 
     lax.fori_loop(0, OWN, out_space, 0)
+    copies = [pltpu.make_async_copy(fresh_space, space_out, sems.at[0])]
+    copies[0].start()
+    third = 2 * Q1 * HALF // 3
 
     def out_point(i, carry):
-        at = pl.multiple_of(i * HALF, 128)
-        hi, lo = split(spread[:, pl.ds(at, HALF)])
-        fresh_point[:, pl.ds(at, HALF)] = dot(w_point, jnp.concatenate([hi, lo, hi], axis=0))
+        at = pl.multiple_of(i * 1536, 512)
+        hi, lo = split(spread[:, pl.ds(at, 1536)])
+        fresh_point[:, pl.ds(at, 1536)] = dot(w_point, jnp.concatenate([hi, lo, hi], axis=0))
         return carry
 
-    lax.fori_loop(0, 2 * Q1, out_point, 0)
+    for k in range(3):
+        lax.fori_loop(3 * k, 3 * k + 3, out_point, 0)
+        cells = pl.ds(k * third, third)
+        copies.append(pltpu.make_async_copy(fresh_point.at[:, cells], point_out.at[:, cells], sems.at[k + 1]))
+        copies[-1].start()
 
     inverse_t = transposed(inverse)
     inverse_vt = transposed(inverse_v)
-    aux = mm(both[2 * RANK :, 0:32] * (1.0 / points_total), inverse_vt)
+    turned = mm(inverse, s)
+    turned_v = mm(inverse_v, q[:RANK])
+    aux = mm(q[RANK:, 0:32], inverse_vt)
     weights_row = aux[0:1, :]
     moments_row = aux[1:2, :] + aux[2:3, :]
-    raw_a = [gram - s[:, 32 * (d + 1) : 32 * (d + 2)] for d in range(3)]
-    space_half = mm(jnp.concatenate(raw_a + [s[:, 128:160]], axis=0), inverse_t)
-    a = [mm(inverse, space_half[d * RANK : (d + 1) * RANK]) for d in range(4)]
-    e = a[3]
-    a_t = [transposed(a[d]) for d in range(3)]
-    flux = congruent(inverse_v, plus + minus)
-    left = mm(inverse, s[:, 160:192])
-    right = mm(inverse_v, cross_v)
-    current = mm_t(mm(left, core[...]), right)
+    left = [turned[:, 128:160]]
+    for d in range(3):
+        left.append(turned[:, 0:32] - turned[:, 32 * (d + 1) : 32 * (d + 2)])
+    for d in range(3):
+        left.append(mm_t(inverse, gram - s[:, 32 * (d + 1) : 32 * (d + 2)]))
+    stack = mm(jnp.concatenate(left, axis=0), inverse_t)
+    lines = [turned_v[:, 192:224], turned_v[:, 160:192], turned_v[:, 64:96]]
+    lines += [-turned_v[:, 128:160], -turned_v[:, 32:64], -turned_v[:, 96:128]]
+    flux = mm(jnp.concatenate(lines, axis=0), inverse_vt)
+    current = mm_t(mm(turned[:, 160:192], core[...]), turned_v[:, 224:256])
     for _ in range(SUB):
-        scaled = mm(e, current)
+        moved = mm(stack, current)
+        scaled = moved[:RANK]
         change = -scaled + jnp.sum(scaled * weights_row, axis=1, keepdims=True) * moments_row
-        for d in range(3):
-            change = change - mm(mm(a[d], current), flux[d]) + mm(mm(a_t[d], current), flux[d + 3])
-        current = current + change
+        across = jnp.concatenate([moved[(k + 1) * RANK : (k + 2) * RANK] for k in range(6)], axis=1)
+        current = current + (change - mm(across, flux))
     fresh_core[...] = current
+    for copy in copies:
+        copy.wait()
 
 
 def finish(parts, core, kinetic, spread, cells_total, points_total):
     def kernel(*refs):
         finish_kernel(cells_total, points_total, *refs)
 
+    flat = (RANK * OWN * NY, NZ)
     return call(
-        kernel, [((RANK * OWN * NY, NZ), f32), ((RANK, RANK), f32), (spread.shape, f32)], "vvvvvvv",
-        (*parts, core, kinetic, spread), mib=12,
+        kernel, [(flat, f32), ((RANK, RANK), f32), (spread.shape, f32)], "vvvvvvv",
+        (*parts, core, kinetic, spread),
+        [pltpu.VMEM(flat, f32), pltpu.VMEM(spread.shape, f32), pltpu.SemaphoreType.DMA((4,))],
+        mib=12, out_spaces="ava",
     )
 
 
@@ -681,7 +678,10 @@
     pair = [(2 * z + c, 2 * z + 1 - c) for z in range(4) for c in range(2)]
     joint = joint + lax.ppermute(joint, "vel", pair)
     routes = [[(2 * z + c, 2 * ((z + d) % 4) + c) for z in range(4) for c in range(2)] for d in (1, 2, 3)]
-    return [joint] + [lax.ppermute(joint, "vel", route) for route in routes]
+    parts = [joint]
+    for route in routes:
+        parts.append(lax.ppermute(joint, "vel", route))
+    return parts
 
 
 def per_device(space_factor, core_matrix, velocity_factor, collision_rates):
@@ -700,18 +700,18 @@
     route = [(s * 8 + w, (s + 1 - 2 * (w % 2)) % devices * 8 + w) for s in range(devices) for w in range(8)]
     pair = [(w, w ^ 1) for w in range(8)]
 
-    inner, own_hi, own_lo = space_sums(values, rates)
-    halo, inner = lax.optimization_barrier((halo, inner))
+    inner, own = space_sums(values, rates)
+    point = point_sums(v, velocity_factor, inner)
+    halo, point = lax.optimization_barrier((halo, point))
     mine = lax.ppermute(halo, ("space", "vel"), route)
-    space, *edge = edge_sums(own_hi, own_lo, below1, inner)
+    space, edge = edge_sums(own, below1, inner)
     moved = spread_pairs(space)
-    point = point_sums(v, velocity_factor, space)
-    mine, point = lax.optimization_barrier((mine, point))
+    parts = vel_parts(moved, point)
+    mine, parts[0] = lax.optimization_barrier((mine, parts[0]))
     other = lax.ppermute(mine, "vel", pair)
-    parts = vel_parts(moved, point)
-    filled = fill_planes(v, (own_hi, own_lo), edge, mine.reshape(-1, NZ), other.reshape(-1, NZ), parts[0])
-    wk, wl, src = small_first(parts, core_matrix, filled[0], cells_total, points_total)
-    kinetic, space = evolve_space(wk, filled, rates)
+    filled = fill_planes(v, own, edge, mine.reshape(-1, NZ), other.reshape(-1, NZ), parts[0])
+    wk, wl, src, moment = small_first(parts, core_matrix, filled[0], cells_total, points_total)
+    kinetic, space = evolve_space(wk, moment, filled, rates)
     moved = spread_pairs(space)
     spread, point = evolve_point(v, wl, src, velocity_factor, space)
     parts = vel_parts(moved, point)

time: 109 us -> 106 us (0.972)
  the two profiles are of different devices: /device:TPU:4 before, /device:TPU:1 now
where the time goes in v3:
time: 106 us
  Pallas kernels  45.1 us (43%)
  starting transfers between devices  30.1 us (28%)
  waiting for transfers between devices  28.5 us (27%)
    pallas_call x8, Pallas kernels, call(): pl.pallas_call(kernel, out_shape=[jax.ShapeDtypeStruct(s, d) for s, d in...  45.1 us
    ppermute x6, starting transfers between devices, vel_parts(): parts.append(lax.ppermute(joint, 'vel', route))  11.7 us
    ppermute x1, waiting for transfers between devices, per_device(): lax.ppermute(space_factor[:, OWN - 1:], 'space', up).reshape(-1, NZ)  11.6 us
    ppermute x6, waiting for transfers between devices, vel_parts(): parts.append(lax.ppermute(joint, 'vel', route))  10.5 us
    ppermute x4, starting transfers between devices, spread_pairs(): moved.append(lax.ppermute(space_part, ('space', 'vel'), route))  8.75 us
    ppermute x1, starting transfers between devices, per_device(): mine = lax.ppermute(halo, ('space', 'vel'), route)  5.76 us
    ppermute x4, waiting for transfers between devices, spread_pairs(): moved.append(lax.ppermute(space_part, ('space', 'vel'), route))  4.24 us
    ppermute x2, starting transfers between devices, vel_parts(): joint = joint + lax.ppermute(joint, 'vel', pair)  3.36 us
  transfers between devices with their start and end apart: 15, of which 10 were waited for; matrix products, arithmetic and copies ran while one was open for 0% of the time, Pallas kernels for 11%

profile of v3, /device:TPU:1, one launch (start us, length us, event | category | flops | bytes accessed | tf_op | source)
XLA Modules:
  0.0 106.1 jit_solution(10631918579576537773)
XLA Ops:
  0.6 0.0 slice-start
  0.6 0.0 copy-start.1
  0.7 0.0 copy-start.2
  0.7 0.0 copy-start
  0.7 0.0 copy-start.3
  0.7 0.0 copy-start.4
  0.7 0.0 copy-start.7
  0.7 0.0 copy-start.9
  0.7 0.9 select_bitcast_fusion
  1.6 0.1 slice-done
  1.8 0.1 pad_maximum_fusion
  1.8 0.3 copy-done.1
  2.1 0.0 copy-done.2
  2.1 3.4 %shard_map.121 = (f32[32,256]{1,0:T(8,128)S(1)}, f32[32,8192]{1,0:T(8,128)S(1)}) custom-call(f32[2048,128]{1,0:T(8,128)S(1)} %bitcast.9, f32[64,128]{1,0:T(8,128)S(1)} %bitcast.12), custom_call_target="tpu_custom_call" | custom-call | tf_op jit(solution)/shard_map/pallas_call | solution.py:128
  5.5 0.0 copy-done
  5.5 0.0 copy-done.3
  5.5 0.0 copy-done.4
  5.6 0.0 copy-done.7
  5.6 0.0 copy-done.9
  5.6 4.6 %shard_map.122 = f32[32,256]{1,0:T(8,128)S(1)} custom-call(s32[1]{0:T(128)} %bitcast.1.v_ref, f32[144]{0:T(256)S(1)} %copy-done.9, f32[2,8,1152]{2,1,0:T(8,128)S(1)} %copy-done.4, f32[2,32,1152]{2,1,0:T(8,128)S(1)} %copy-done.3, f32[48,128]{1,0:T(8,128)S(1)} %copy-done.7, f32[32,13824]{1,0:T(8,128)S(1)} %copy-done, f32[32,256]{1,0:T(8,128)S(1)} %get-tuple-element.25.after.inner), custom_call_target="tpu_custom_call" | custom-call | tf_op jit(solution)/shard_map/pallas_call | solution.py:128
  10.1 5.8 %collective-permute-start = (f32[33,3,16,128]{3,2,1,0:T(8,128)S(1)}, f32[33,3,16,128]{3,2,1,0:T(8,128)S(1)}, u32[]{:S(2)}, u32[]{:S(2)}) collective-permute-start(f32[33,3,16,128]{3,2,1,0:T(8,128)S(1)} %pad_maximum_fusion), channel_id=1, source_target_pairs={{0,8},{1,121},{2,10},{3,123},{4,12},{5,125},{6,14},{7,127},{8,16},... | collective-permute-start | bytes 2433032 | tf_op jit(solution)/shard_map/ppermute | solution.py:706
  15.9 0.1 collective-permute-start.1
  16.0 11.6 %collective-permute-done.1 = f32[32,1,16,128]{3,2,1,0:T(8,128)S(1)} collective-permute-done((f32[32,1,16,128]{3,2,1,0:T(8,128)S(1)}, f32[32,1,16,128]{3,2,1,0:T(8,128)S(1)}, u32[]{:S(2)}, u32[]{:S(2)}) %collective-permute-start.1) | collective-permute-done | bytes 262176 | tf_op jit(solution)/shard_map/ppermute | solution.py:690
  27.6 0.3 shard_map.123
  27.9 0.0 copy-start.5
  27.9 0.0 copy-start.6
  28.0 0.0 copy-start.8
  28.0 0.1 collective-permute-start.3
  28.1 1.9 %collective-permute-start.2 = (f32[32,256]{1,0:T(8,128)S(1)}, f32[32,256]{1,0:T(8,128)S(1)}, u32[]{:S(2)}, u32[]{:S(2)}) collective-permute-start(f32[32,256]{1,0:T(8,128)S(1)} %get-tuple-element.28), channel_id=1, source_target_pairs={{0,0},{17,1},{34,2},{51,3},{68,4},{85,5},{102,6},{119,7},{8,8},{25... | collective-permute-start | bytes 98312 | tf_op jit(solution)/shard_map/ppermute | solution.py:672
  30.0 2.3 %collective-permute-done.3 = f32[32,256]{1,0:T(8,128)S(1)} collective-permute-done((f32[32,256]{1,0:T(8,128)S(1)}, f32[32,256]{1,0:T(8,128)S(1)}, u32[]{:S(2)}, u32[]{:S(2)}) %collective-permute-start.3) | collective-permute-done | bytes 32800 | tf_op jit(solution)/shard_map/ppermute | solution.py:672
  32.3 1.9 %collective-permute-done.2 = f32[32,256]{1,0:T(8,128)S(1)} collective-permute-done((f32[32,256]{1,0:T(8,128)S(1)}, f32[32,256]{1,0:T(8,128)S(1)}, u32[]{:S(2)}, u32[]{:S(2)}) %collective-permute-start.2) | collective-permute-done | bytes 32800 | tf_op jit(solution)/shard_map/ppermute | solution.py:672
  34.2 3.3 %collective-permute-start.4 = (f32[64,256]{1,0:T(8,128)S(1)}, f32[64,256]{1,0:T(8,128)S(1)}, u32[]{:S(2)}, u32[]{:S(2)}) collective-permute-start(f32[64,256]{1,0:T(8,128)S(1)} %pad_maximum_fusion.2), channel_id=1, source_target_pairs={{0,1},{1,0},{2,3},{3,2},{4,5},{5,4},{6,7},{7,6},{8,9},{9,8},{10,11... | collective-permute-start | bytes 196616 | tf_op jit(solution)/shard_map/ppermute | solution.py:679
  37.5 0.9 collective-permute-done.4
  38.4 0.0 collective-permute-done
  38.4 0.4 collective-permute-start.8
  38.9 7.2 %collective-permute-start.7 = (f32[64,256]{1,0:T(8,128)S(1)}, f32[64,256]{1,0:T(8,128)S(1)}, u32[]{:S(2)}, u32[]{:S(2)}) collective-permute-start(f32[64,256]{1,0:T(8,128)S(1)} %fusion.after.refs_0_), channel_id=1, source_target_pairs={{0,6},{1,7},{2,0},{3,1},{4,2},{5,3},{6,4},{7,5},{8,14},{9,15},{10,... | collective-permute-start | bytes 196616 | tf_op jit(solution)/shard_map/ppermute | solution.py:683
  46.1 0.3 collective-permute-start.6
  46.4 0.9 collective-permute-start.5
  47.3 0.0 collective-permute-done.8
  47.3 0.6 shard_map.124
  47.9 0.0 collective-permute-done.7.refs_3_
  47.9 2.9 %collective-permute-done.6.refs_2_ = f32[64,256]{1,0:T(8,128)S(1)} collective-permute-done((f32[64,256]{1,0:T(8,128)S(1)}, f32[64,256]{1,0:T(8,128)S(1)}, u32[]{:S(2)}, u32[]{:S(2)}) %collective-permute-start.6) | collective-permute-done | bytes 65568 | tf_op jit(solution)/shard_map/ppermute | solution.py:683
  50.8 2.1 %collective-permute-done.5.refs_1_ = f32[64,256]{1,0:T(8,128)S(1)} collective-permute-done((f32[64,256]{1,0:T(8,128)S(1)}, f32[64,256]{1,0:T(8,128)S(1)}, u32[]{:S(2)}, u32[]{:S(2)}) %collective-permute-start.5) | collective-permute-done | bytes 65568 | tf_op jit(solution)/shard_map/ppermute | solution.py:683
  52.9 0.0 copy-done.5
  52.9 0.0 copy-done.6
  52.9 0.0 copy-done.8
  52.9 3.8 %shard_map.125 = (f32[2,240,128]{2,1,0:T(8,128)S(1)}, f32[2,224,128]{2,1,0:T(8,128)S(1)}, f32[3,32,128]{2,1,0:T(8,128)S(1)}, f32[32,128]{1,0:T(8,128)S(1)}) custom-call(f32[64,256]{1,0:T(8,128)S(1)} %fusion.after.refs_0_, f32[64,256]{1,0:T(8,128)S(1)} %collective-permute-done.5.refs_1_, f32[64,256]{1,0:T(8,128)S(1)} %collective-permute-done.6.refs_2_, ...), custom_call_target="tpu_custom_call" | custom-call | tf_op jit(solution)/shard_map/pallas_call | solution.py:128
  56.7 13.7 %shard_map.126 = (f32[32,12288]{1,0:T(8,128)S(1)}, f32[32,256]{1,0:T(8,128)S(1)}) custom-call(f32[2,240,128]{2,1,0:T(8,128)S(1)} %get-tuple-element.34.wk, f32[32,128]{1,0:T(8,128)S(1)} %get-tuple-element.35.moment, f32[32,22528]{1,0:T(8,128)S(1)} %get-tuple-element.33.refs_7_.raw, f32[64,128]{1,0:T(8,128)S(1)} %bitcast.13, ...), custom_call_target="tpu_custom_call" | custom-call | tf_op jit(solution)/shard_map/pallas_call | solution.py:128
  70.3 1.5 %collective-permute-start.10 = (f32[32,256]{1,0:T(8,128)S(1)}, f32[32,256]{1,0:T(8,128)S(1)}, u32[]{:S(2)}, u32[]{:S(2)}) collective-permute-start(f32[32,256]{1,0:T(8,128)S(1)} %get-tuple-element.38.after), channel_id=1, source_target_pairs={{8,0},{25,1},{42,2},{59,3},{76,4},{93,5},{110,6},{127,7},{0,8},{17... | collective-permute-start | bytes 98312 | tf_op jit(solution)/shard_map/ppermute | solution.py:672
  71.8 5.3 %collective-permute-start.9 = (f32[32,256]{1,0:T(8,128)S(1)}, f32[32,256]{1,0:T(8,128)S(1)}, u32[]{:S(2)}, u32[]{:S(2)}) collective-permute-start(f32[32,256]{1,0:T(8,128)S(1)} %get-tuple-element.38.after), channel_id=1, source_target_pairs={{0,0},{17,1},{34,2},{51,3},{68,4},{85,5},{102,6},{119,7},{8,8},{25... | collective-permute-start | bytes 98312 | tf_op jit(solution)/shard_map/ppermute | solution.py:672
  77.1 11.2 %shard_map.127 = (f32[32,13824]{1,0:T(8,128)S(1)}, f32[40,256]{1,0:T(8,128)S(1)}) custom-call(s32[1]{0:T(128)} %bitcast.1.v_ref, f32[144]{0:T(256)S(1)} %copy-done.9, f32[2,8,1152]{2,1,0:T(8,128)S(1)} %copy-done.4, f32[2,224,128]{2,1,0:T(8,128)S(1)} %get-tuple-element.39.wl, f32[3,32,128]{2,1,0:T(8,128)S(1)} %get-tuple-element.40.src, ...), custom_call_target="tpu_custom_call" | custom-call | tf_op jit(solution)/shard_map/pallas_call | solution.py:128
  88.3 0.0 collective-permute-done.10
  88.3 0.0 collective-permute-done.9
  88.3 0.1 collective-permute-start.11
  88.4 1.3 %collective-permute-done.11 = f32[72,256]{1,0:T(8,128)S(1)} collective-permute-done((f32[72,256]{1,0:T(8,128)S(1)}, f32[72,256]{1,0:T(8,128)S(1)}, u32[]{:S(2)}, u32[]{:S(2)}) %collective-permute-start.11) | collective-permute-done | bytes 73760 | tf_op jit(solution)/shard_map/ppermute | solution.py:679
  89.7 1.9 %collective-permute-start.14 = (f32[72,256]{1,0:T(8,128)S(1)}, f32[72,256]{1,0:T(8,128)S(1)}, u32[]{:S(2)}, u32[]{:S(2)}) collective-permute-start(f32[72,256]{1,0:T(8,128)S(1)} %fusion.1.refs_0_), channel_id=1, source_target_pairs={{0,6},{1,7},{2,0},{3,1},{4,2},{5,3},{6,4},{7,5},{8,14},{9,15},{10,... | collective-permute-start | bytes 221192 | tf_op jit(solution)/shard_map/ppermute | solution.py:683
  91.6 0.6 collective-permute-start.13
  92.2 0.8 collective-permute-start.12
  93.0 0.5 collective-permute-done.14.refs_3_
  93.4 2.9 %collective-permute-done.13.refs_2_ = f32[72,256]{1,0:T(8,128)S(1)} collective-permute-done((f32[72,256]{1,0:T(8,128)S(1)}, f32[72,256]{1,0:T(8,128)S(1)}, u32[]{:S(2)}, u32[]{:S(2)}) %collective-permute-start.13) | collective-permute-done | bytes 73760 | tf_op jit(solution)/shard_map/ppermute | solution.py:683
  96.3 2.1 %collective-permute-done.12.refs_1_ = f32[72,256]{1,0:T(8,128)S(1)} collective-permute-done((f32[72,256]{1,0:T(8,128)S(1)}, f32[72,256]{1,0:T(8,128)S(1)}, u32[]{:S(2)}, u32[]{:S(2)}) %collective-permute-start.12) | collective-permute-done | bytes 73760 | tf_op jit(solution)/shard_map/ppermute | solution.py:683
  98.5 7.6 %shard_map.128 = (f32[2048,128]{1,0:T(8,128)}, f32[32,32]{1,0:T(8,128)}, f32[32,13824]{1,0:T(8,128)}) custom-call(f32[72,256]{1,0:T(8,128)S(1)} %fusion.1.refs_0_, f32[72,256]{1,0:T(8,128)S(1)} %collective-permute-done.12.refs_1_, f32[72,256]{1,0:T(8,128)S(1)} %collective-permute-done.13.refs_2_, f32[72,256]{1,0:T(8,128)S(1)} %collective-permute-done.14.refs_3_, ...), custom_call_target="tpu_custom_call" | custom-call | tf_op jit(solution)/shard_map/pallas_call | solution.py:128
  (7 shorter events, 0.1 us)
Async XLA Ops:
  0.6 1.1 %slice-start = ((f32[32,4,16,128]{3,2,1,0:T(8,128)}), f32[32,3,16,128]{3,2,1,0:T(8,128)S(1)}, s32[]{:S(2)}) async-start(f32[32,4,16,128]{3,2,1,0:T(8,128)} %param.10), calls=%async_computation | async-start | bytes 1572864 | tf_op jit(solution)/shard_map/slice | solution.py:697
  0.6 1.5 %copy-start.1 = (f32[32,4,16,128]{3,2,1,0:T(8,128)S(1)}, f32[32,4,16,128]{3,2,1,0:T(8,128)}, u32[]{:S(2)}) copy-start(f32[32,4,16,128]{3,2,1,0:T(8,128)} %param.10) | copy-start | bytes 3145732
  0.7 1.5 %copy-start.2 = (f32[4,16,128]{2,1,0:T(8,128)S(1)}, f32[4,16,128]{2,1,0:T(8,128)}, u32[]{:S(2)}) copy-start(f32[4,16,128]{2,1,0:T(8,128)} %param.13) | copy-start | bytes 98308
  0.7 4.9 %copy-start = (f32[32,13824]{1,0:T(8,128)S(1)}, f32[32,13824]{1,0:T(8,128)}, u32[]{:S(2)}) copy-start(f32[32,13824]{1,0:T(8,128)} %values.3) | copy-start | bytes 5308420
  0.7 4.9 %copy-start.3 = (f32[2,32,1152]{2,1,0:T(8,128)S(1)}, f32[2,32,1152]{2,1,0:T(8,128)}, u32[]{:S(2)}) copy-start(f32[2,32,1152]{2,1,0:T(8,128)} %constant.34.clone.phi) | copy-start | bytes 884740
  0.7 4.9 %copy-start.4 = (f32[2,8,1152]{2,1,0:T(8,128)S(1)}, f32[2,8,1152]{2,1,0:T(8,128)}, u32[]{:S(2)}) copy-start(f32[2,8,1152]{2,1,0:T(8,128)} %constant.33.clone.rows) | copy-start | bytes 221188
  0.7 4.9 %copy-start.7 = (f32[48,128]{1,0:T(8,128)S(1)}, f32[48,128]{1,0:T(8,128)}, u32[]{:S(2)}) copy-start(f32[48,128]{1,0:T(8,128)} %constant.35.clone.scale) | copy-start | bytes 73732
  0.7 4.8 %copy-start.9 = (f32[144]{0:T(256)S(1)}, f32[144]{0:T(256)}, u32[]{:S(2)}) copy-start(f32[144]{0:T(256)} %constant.32.clone.speeds) | copy-start | bytes 1732
  10.1 28.3 %collective-permute-start = (f32[33,3,16,128]{3,2,1,0:T(8,128)S(1)}, f32[33,3,16,128]{3,2,1,0:T(8,128)S(1)}, u32[]{:S(2)}, u32[]{:S(2)}) collective-permute-start(f32[33,3,16,128]{3,2,1,0:T(8,128)S(1)} %pad_maximum_fusion), channel_id=1, source_target_pairs={{0,8},{1,121},{2,10},{3,123},{4,12},{5,125},{6,14},{7,127},{8,16},... | collective-permute-start | bytes 2433032 | tf_op jit(solution)/shard_map/ppermute | solution.py:706
  15.9 11.7 %collective-permute-start.1 = (f32[32,1,16,128]{3,2,1,0:T(8,128)S(1)}, f32[32,1,16,128]{3,2,1,0:T(8,128)S(1)}, u32[]{:S(2)}, u32[]{:S(2)}) collective-permute-start(f32[32,1,16,128]{3,2,1,0:T(8,128)S(1)} %slice.16), channel_id=1, source_target_pairs={{0,8},{8,16},{16,24},{24,32},{32,40},{40,48},{48,56},{56,64},{64,7... | collective-permute-start | bytes 786440 | tf_op jit(solution)/shard_map/ppermute | solution.py:690
  27.9 25.0 %copy-start.5 = (f32[32,896]{1,0:T(8,128)S(1)}, f32[32,896]{1,0:T(8,128)}, u32[]{:S(2)}) copy-start(f32[32,896]{1,0:T(8,128)} %constant.36.clone.refs_5_) | copy-start | bytes 344068
  27.9 25.0 %copy-start.6 = (f32[32,32]{1,0:T(8,128)S(1)}, f32[32,32]{1,0:T(8,128)}, u32[]{:S(2)}) copy-start(f32[32,32]{1,0:T(8,128)} %refs_4_.3) | copy-start | bytes 12292
  28.0 25.0 %copy-start.8 = (f32[8,128]{1,0:T(8,128)S(1)}, f32[8,128]{1,0:T(8,128)}, u32[]{:S(2)}) copy-start(f32[8,128]{1,0:T(8,128)} %constant.37.clone.refs_6_) | copy-start | bytes 12292
  28.0 4.3 %collective-permute-start.3 = (f32[32,256]{1,0:T(8,128)S(1)}, f32[32,256]{1,0:T(8,128)S(1)}, u32[]{:S(2)}, u32[]{:S(2)}) collective-permute-start(f32[32,256]{1,0:T(8,128)S(1)} %get-tuple-element.28), channel_id=1, source_target_pairs={{8,0},{25,1},{42,2},{59,3},{76,4},{93,5},{110,6},{127,7},{0,8},{17... | collective-permute-start | bytes 98312 | tf_op jit(solution)/shard_map/ppermute | solution.py:672
  28.1 6.2 %collective-permute-start.2 = (f32[32,256]{1,0:T(8,128)S(1)}, f32[32,256]{1,0:T(8,128)S(1)}, u32[]{:S(2)}, u32[]{:S(2)}) collective-permute-start(f32[32,256]{1,0:T(8,128)S(1)} %get-tuple-element.28), channel_id=1, source_target_pairs={{0,0},{17,1},{34,2},{51,3},{68,4},{85,5},{102,6},{119,7},{8,8},{25... | collective-permute-start | bytes 98312 | tf_op jit(solution)/shard_map/ppermute | solution.py:672
  34.2 4.2 %collective-permute-start.4 = (f32[64,256]{1,0:T(8,128)S(1)}, f32[64,256]{1,0:T(8,128)S(1)}, u32[]{:S(2)}, u32[]{:S(2)}) collective-permute-start(f32[64,256]{1,0:T(8,128)S(1)} %pad_maximum_fusion.2), channel_id=1, source_target_pairs={{0,1},{1,0},{2,3},{3,2},{4,5},{5,4},{6,7},{7,6},{8,9},{9,8},{10,11... | collective-permute-start | bytes 196616 | tf_op jit(solution)/shard_map/ppermute | solution.py:679
  38.4 8.8 %collective-permute-start.8 = (f32[33,3,16,128]{3,2,1,0:T(8,128)S(1)}, f32[33,3,16,128]{3,2,1,0:T(8,128)S(1)}, u32[]{:S(2)}, u32[]{:S(2)}) collective-permute-start(f32[33,3,16,128]{3,2,1,0:T(8,128)S(1)} %collective-permute-done), channel_id=1, source_target_pairs={{0,1},{1,0},{2,3},{3,2},{4,5},{5,4},{6,7},{7,6},{8,9},{9,8},{10,11... | collective-permute-start | bytes 2433032 | tf_op jit(solution)/shard_map/ppermute | solution.py:711
  38.9 9.0 %collective-permute-start.7 = (f32[64,256]{1,0:T(8,128)S(1)}, f32[64,256]{1,0:T(8,128)S(1)}, u32[]{:S(2)}, u32[]{:S(2)}) collective-permute-start(f32[64,256]{1,0:T(8,128)S(1)} %fusion.after.refs_0_), channel_id=1, source_target_pairs={{0,6},{1,7},{2,0},{3,1},{4,2},{5,3},{6,4},{7,5},{8,14},{9,15},{10,... | collective-permute-start | bytes 196616 | tf_op jit(solution)/shard_map/ppermute | solution.py:683
  46.1 4.7 %collective-permute-start.6 = (f32[64,256]{1,0:T(8,128)S(1)}, f32[64,256]{1,0:T(8,128)S(1)}, u32[]{:S(2)}, u32[]{:S(2)}) collective-permute-start(f32[64,256]{1,0:T(8,128)S(1)} %fusion.after.refs_0_), channel_id=1, source_target_pairs={{0,4},{1,5},{2,6},{3,7},{4,0},{5,1},{6,2},{7,3},{8,12},{9,13},{10,... | collective-permute-start | bytes 196616 | tf_op jit(solution)/shard_map/ppermute | solution.py:683
  46.4 6.5 %collective-permute-start.5 = (f32[64,256]{1,0:T(8,128)S(1)}, f32[64,256]{1,0:T(8,128)S(1)}, u32[]{:S(2)}, u32[]{:S(2)}) collective-permute-start(f32[64,256]{1,0:T(8,128)S(1)} %fusion.after.refs_0_), channel_id=1, source_target_pairs={{0,2},{1,3},{2,4},{3,5},{4,6},{5,7},{6,0},{7,1},{8,10},{9,11},{10,... | collective-permute-start | bytes 196616 | tf_op jit(solution)/shard_map/ppermute | solution.py:683
  70.3 18.0 %collective-permute-start.10 = (f32[32,256]{1,0:T(8,128)S(1)}, f32[32,256]{1,0:T(8,128)S(1)}, u32[]{:S(2)}, u32[]{:S(2)}) collective-permute-start(f32[32,256]{1,0:T(8,128)S(1)} %get-tuple-element.38.after), channel_id=1, source_target_pairs={{8,0},{25,1},{42,2},{59,3},{76,4},{93,5},{110,6},{127,7},{0,8},{17... | collective-permute-start | bytes 98312 | tf_op jit(solution)/shard_map/ppermute | solution.py:672
  71.8 16.5 %collective-permute-start.9 = (f32[32,256]{1,0:T(8,128)S(1)}, f32[32,256]{1,0:T(8,128)S(1)}, u32[]{:S(2)}, u32[]{:S(2)}) collective-permute-start(f32[32,256]{1,0:T(8,128)S(1)} %get-tuple-element.38.after), channel_id=1, source_target_pairs={{0,0},{17,1},{34,2},{51,3},{68,4},{85,5},{102,6},{119,7},{8,8},{25... | collective-permute-start | bytes 98312 | tf_op jit(solution)/shard_map/ppermute | solution.py:672
  88.3 1.3 %collective-permute-start.11 = (f32[72,256]{1,0:T(8,128)S(1)}, f32[72,256]{1,0:T(8,128)S(1)}, u32[]{:S(2)}, u32[]{:S(2)}) collective-permute-start(f32[72,256]{1,0:T(8,128)S(1)} %pad_maximum_fusion.1), channel_id=1, source_target_pairs={{0,1},{1,0},{2,3},{3,2},{4,5},{5,4},{6,7},{7,6},{8,9},{9,8},{10,11... | collective-permute-start | bytes 221192 | tf_op jit(solution)/shard_map/ppermute | solution.py:679
  89.7 3.7 %collective-permute-start.14 = (f32[72,256]{1,0:T(8,128)S(1)}, f32[72,256]{1,0:T(8,128)S(1)}, u32[]{:S(2)}, u32[]{:S(2)}) collective-permute-start(f32[72,256]{1,0:T(8,128)S(1)} %fusion.1.refs_0_), channel_id=1, source_target_pairs={{0,6},{1,7},{2,0},{3,1},{4,2},{5,3},{6,4},{7,5},{8,14},{9,15},{10,... | collective-permute-start | bytes 221192 | tf_op jit(solution)/shard_map/ppermute | solution.py:683
  91.6 4.8 %collective-permute-start.13 = (f32[72,256]{1,0:T(8,128)S(1)}, f32[72,256]{1,0:T(8,128)S(1)}, u32[]{:S(2)}, u32[]{:S(2)}) collective-permute-start(f32[72,256]{1,0:T(8,128)S(1)} %fusion.1.refs_0_), channel_id=1, source_target_pairs={{0,4},{1,5},{2,6},{3,7},{4,0},{5,1},{6,2},{7,3},{8,12},{9,13},{10,... | collective-permute-start | bytes 221192 | tf_op jit(solution)/shard_map/ppermute | solution.py:683
  92.2 6.2 %collective-permute-start.12 = (f32[72,256]{1,0:T(8,128)S(1)}, f32[72,256]{1,0:T(8,128)S(1)}, u32[]{:S(2)}, u32[]{:S(2)}) collective-permute-start(f32[72,256]{1,0:T(8,128)S(1)} %fusion.1.refs_0_), channel_id=1, source_target_pairs={{0,2},{1,3},{2,4},{3,5},{4,6},{5,7},{6,0},{7,1},{8,10},{9,11},{10,... | collective-permute-start | bytes 221192 | tf_op jit(solution)/shard_map/ppermute | solution.py:683

commit v4 on v3

--- a/solution.py
+++ b/solution.py
@@ -298,7 +298,7 @@
     return (parts[0][...] + parts[2][...]) + (parts[1][...] + parts[3][...])
 
 
-def small_first_kernel(cells_total, points_total, p0, p1, p2, p3, core, select, means, after, wk, wl, src, moment):
+def small_first_kernel(cells_total, points_total, p0, p1, p2, p3, core, select, means, wk, wl, src, moment):
     both = four((p0, p1, p2, p3))
     s = both[:RANK] * (1.0 / cells_total)
     gram = s[:, 0:32]
@@ -338,7 +338,7 @@
     third = jnp.sum(third, axis=1, keepdims=True) + source[1] * means[0:1, 0:1]
     source.append(mm(e, jnp.broadcast_to(third, (RANK, 128)))[:, 0:1])
     for n in range(3):
-        src[n] = jnp.where((lane >= 96) & (lane < 99), source[n], 0.0)
+        src[n] = jnp.broadcast_to(source[n], (RANK, 128))
     half = mm(inverse_v, both[RANK:, :] * (1.0 / points_total))
     turned_raw = half[:, 224:256]
     weights_row = transposed(turned_raw)[0:1, :]
@@ -353,20 +353,20 @@
     moment[...] = jnp.broadcast_to(turned_raw[:, LAST : LAST + 1], (RANK, 128))
 
 
-def small_first(parts, core, after, cells_total, points_total):
+def small_first(parts, core, cells_total, points_total):
     def kernel(*refs):
         small_first_kernel(cells_total, points_total, *refs)
 
     return call(
-        kernel, [((2, ROWS_K, 128), f32), ((2, 224, 128), f32), ((3, RANK, 128), f32), ((RANK, 128), f32)], "vvvvvvva",
-        (*parts, core, SELECT, MEANS, after),
+        kernel, [((2, ROWS_K, 128), f32), ((2, 224, 128), f32), ((3, RANK, 128), f32), ((RANK, 128), f32)], "vvvvvvv",
+        (*parts, core, SELECT, MEANS),
     )
 
 
 def evolve_point_kernel(v_ref, speeds, rows, wl, src, values, after, new, out):
     q0 = v_ref[0] * Q1
     lane_w = lanes((RANK, 128))
-    low_lane = ((lane_w >= 64) & (lane_w < 96)) | (lane_w == 97)
+    low_lane = (lane_w >= 64) & (lane_w < 96)
 
     def weights_of(w):
         hi = w.astype(bf16).astype(f32)
@@ -375,18 +375,16 @@
     def piece(kind, n):
         return wl[kind, n * RANK : (n + 1) * RANK, :]
 
-    fixed = [
-        [jnp.concatenate([weights_of(piece(kind, n)) for n in ((5, 3, 6) if h == 0 else (2, 3, 6))], axis=0) for h in range(2)]
-        for kind in range(2)
-    ]
-    tops = []
+    fixed = [jnp.concatenate([weights_of(piece(kind, n)) for n in (3, 6)], axis=0) for kind in range(2)]
+    turning = [[weights_of(piece(kind, n)) for n in (5, 2)] for kind in range(2)]
     aux = []
     for h in range(2):
         gh, gl = split(rows[h, 3:4, :])
         row = sublanes((16, HALF))
         gh, gl = gh.astype(f32), gl.astype(f32)
-        tops.append(jnp.where(row < 2, gh, jnp.where(row == 2, gl, 0.0)).astype(bf16))
         aux.append(jnp.where(row == 0, 1.0, jnp.where(row == 1, gh, jnp.where(row == 2, gl, 0.0))).astype(bf16))
+    inside = HALF // 256 * 256
+    cuts = [(0, inside, (0,)), (inside, 2 * HALF - inside, (0, 1)), (2 * HALF - inside, 2 * HALF, (1,))]
 
     def body(b, carry):
         sums, y, cross, ones_sum = list(carry[:2]), carry[2], carry[3], carry[4]
@@ -395,23 +393,39 @@
         g1 = speeds[2 * NVD + q0 + b]
         u = up + um
         moving = [piece(kind, 0) + up * piece(kind, 1) + um * piece(kind, 4) for kind in range(2)]
-        heads = [weights_of(moving[min(n, 1)] + g1 * src[n]) for n in range(3)]
+        heads = [weights_of(m) for m in moving]
+        first = pl.multiple_of(b * (2 * HALF), 128)
+        states = [values[:, pl.ds(first, HALF)], values[:, pl.ds(first + HALF, HALF)]]
+        raws = [split(state) for state in states]
+        for n in range(SUB):
+            kind = min(n, 1)
+            parts = raws if n == 0 else [split(state) for state in states]
+            operand = jnp.concatenate(
+                [jnp.concatenate([parts[0][k], parts[1][k]], axis=1) for k in (0, 1, 0)], axis=0
+            )
+            source = src[n] * g1
+            mixed = []
+            for low, high, sides in cuts:
+                w = jnp.concatenate([heads[kind], fixed[kind]] + [turning[kind][h] for h in sides], axis=0)[:, :96]
+                mixed.append(dot(w, operand[:, low:high]))
+            rest = HALF - inside
+            middle = mixed[1]
+            ends = [
+                jnp.concatenate([mixed[0], middle[: 4 * RANK, :rest]], axis=1),
+                jnp.concatenate([jnp.concatenate([middle[: 3 * RANK, rest:], middle[4 * RANK :, rest:]], axis=0), mixed[2]], axis=1),
+            ]
+            states = [
+                ends[h][:RANK]
+                + rows[h, 3:4, :] * source[:, 0:1]
+                + rows[h, 1:2, :] * ends[h][RANK : 2 * RANK]
+                + rows[h, 2:3, :] * ends[h][2 * RANK : 3 * RANK]
+                + rows[h, 0:1, :] * ends[h][3 * RANK :]
+                for h in range(2)
+            ]
         for h in range(2):
             start = pl.multiple_of(b * (2 * HALF) + h * HALF, 128)
-            state = values[:, pl.ds(start, HALF)]
-            raw_hi, raw_lo = split(state)
-            hi, lo = raw_hi, raw_lo
-            for n in range(SUB):
-                if n > 0:
-                    hi, lo = split(state)
-                w = jnp.concatenate([heads[n], fixed[min(n, 1)][h]], axis=0)[:, :112]
-                mixed = dot(w, jnp.concatenate([hi, lo, hi, tops[h]], axis=0))
-                state = (
-                    mixed[:RANK]
-                    + rows[h, 0:1, :] * mixed[RANK : 2 * RANK]
-                    + rows[h, 1:2, :] * mixed[2 * RANK : 3 * RANK]
-                    + rows[h, 2:3, :] * mixed[3 * RANK :]
-                )
+            state = states[h]
+            raw_hi, raw_lo = raws[h]
             new[:, pl.ds(start, HALF)] = state
             sh, sl = split(stacked(state, rows, h))
             lh, ll = sh[:RANK], sl[:RANK]
@@ -702,15 +716,15 @@
 
     inner, own = space_sums(values, rates)
     point = point_sums(v, velocity_factor, inner)
-    halo, point = lax.optimization_barrier((halo, point))
-    mine = lax.ppermute(halo, ("space", "vel"), route)
     space, edge = edge_sums(own, below1, inner)
     moved = spread_pairs(space)
+    halo, space = lax.optimization_barrier((halo, space))
+    mine = lax.ppermute(halo, ("space", "vel"), route)
     parts = vel_parts(moved, point)
     mine, parts[0] = lax.optimization_barrier((mine, parts[0]))
     other = lax.ppermute(mine, "vel", pair)
-    filled = fill_planes(v, own, edge, mine.reshape(-1, NZ), other.reshape(-1, NZ), parts[0])
-    wk, wl, src, moment = small_first(parts, core_matrix, filled[0], cells_total, points_total)
+    wk, wl, src, moment = small_first(parts, core_matrix, cells_total, points_total)
+    filled = fill_planes(v, own, edge, mine.reshape(-1, NZ), other.reshape(-1, NZ), moment)
     kinetic, space = evolve_space(wk, moment, filled, rates)
     moved = spread_pairs(space)
     spread, point = evolve_point(v, wl, src, velocity_factor, space)

time: 106 us -> 90.7 us (0.86)
  the two profiles are of different devices: /device:TPU:1 before, /device:TPU:2 now
where the time goes in v4:
time: 90.7 us; the launch traced here: 90.5 us
  Pallas kernels  41.7 us (46%)
  starting transfers between devices  25.5 us (28%)
  waiting for transfers between devices  20 us (22%)
  local copies, waits for them, and re-layouts  2.3 us (3%)
  between operations  0.92 us (1%)
    pallas_call x8, Pallas kernels, call(): pl.pallas_call(kernel, out_shape=[jax.ShapeDtypeStruct(s, d) for s, d in...  41.7 us
    ppermute x6, starting transfers between devices, vel_parts(): parts.append(lax.ppermute(joint, 'vel', route))  11.1 us
    ppermute x6, waiting for transfers between devices, vel_parts(): parts.append(lax.ppermute(joint, 'vel', route))  10.4 us
    ppermute x4, starting transfers between devices, spread_pairs(): moved.append(lax.ppermute(space_part, ('space', 'vel'), route))  8.25 us
    ppermute x4, waiting for transfers between devices, spread_pairs(): moved.append(lax.ppermute(space_part, ('space', 'vel'), route))  5.58 us
    ppermute x2, starting transfers between devices, vel_parts(): joint = joint + lax.ppermute(joint, 'vel', pair)  2.69 us
    ppermute x2, waiting for transfers between devices, vel_parts(): joint = joint + lax.ppermute(joint, 'vel', pair)  2.15 us
  transfers between devices with their start and end apart: 15, of which 10 were waited for; matrix products, arithmetic and copies ran while one was open for 1% of the time, Pallas kernels for 22%

profile of v4, /device:TPU:2, one launch (start us, length us, event | category | flops | bytes accessed | tf_op | source)
XLA Modules:
  0.0 90.5 jit_solution(7423466603978654273)
XLA Ops:
  0.6 0.0 copy-start.1
  0.6 0.0 copy-start.2
  0.7 1.1 %slice.16 = f32[32,1,16,128]{3,2,1,0:T(8,128)S(1)} slice(f32[32,4,16,128]{3,2,1,0:T(8,128)} %param.10), slice={[0:32], [3:4], [0:16], [0:128]} | slice | bytes 524288 | tf_op jit(solution)/shard_map/slice | solution.py:704
  1.7 1.6 %collective-permute-start = (f32[32,1,16,128]{3,2,1,0:T(8,128)S(1)}, f32[32,1,16,128]{3,2,1,0:T(8,128)S(1)}, u32[]{:S(2)}, u32[]{:S(2)}) collective-permute-start(f32[32,1,16,128]{3,2,1,0:T(8,128)S(1)} %slice.16), channel_id=1, source_target_pairs={{0,8},{8,16},{16,24},{24,32},{32,40},{40,48},{48,56},{56,64},{64,7... | collective-permute-start | bytes 786440 | tf_op jit(solution)/shard_map/ppermute | solution.py:704
  3.3 1.2 %slice.13 = f32[32,3,16,128]{3,2,1,0:T(8,128)S(1)} slice(f32[32,4,16,128]{3,2,1,0:T(8,128)} %param.10), slice={[0:32], [0:3], [0:16], [0:128]} | slice | bytes 1572864 | tf_op jit(solution)/shard_map/slice | solution.py:711
  4.5 0.0 copy-done.1
  4.5 0.0 copy-done.2
  4.5 3.4 %shard_map.121 = (f32[32,256]{1,0:T(8,128)S(1)}, f32[32,8192]{1,0:T(8,128)S(1)}) custom-call(f32[2048,128]{1,0:T(8,128)S(1)} %bitcast.9, f32[64,128]{1,0:T(8,128)S(1)} %bitcast.12), custom_call_target="tpu_custom_call" | custom-call | tf_op jit(solution)/shard_map/pallas_call | solution.py:128
  7.9 0.0 copy-start
  7.9 0.0 copy-start.3
  7.9 0.0 copy-start.4
  7.9 0.0 copy-start.7
  7.9 0.0 copy-start.9
  8.0 0.1 pad_maximum_fusion
  8.0 1.8 %collective-permute-done = f32[32,1,16,128]{3,2,1,0:T(8,128)S(1)} collective-permute-done((f32[32,1,16,128]{3,2,1,0:T(8,128)S(1)}, f32[32,1,16,128]{3,2,1,0:T(8,128)S(1)}, u32[]{:S(2)}, u32[]{:S(2)}) %collective-permute-start) | collective-permute-done | bytes 262176 | tf_op jit(solution)/shard_map/ppermute | solution.py:704
  9.8 0.0 copy-start.5
  9.8 0.0 copy-start.6
  9.8 0.0 copy-start.8
  9.8 0.3 shard_map.122
  10.1 1.6 %collective-permute-start.1 = (f32[33,3,16,128]{3,2,1,0:T(8,128)S(1)}, f32[33,3,16,128]{3,2,1,0:T(8,128)S(1)}, u32[]{:S(2)}, u32[]{:S(2)}) collective-permute-start(f32[33,3,16,128]{3,2,1,0:T(8,128)S(1)} %pad_maximum_fusion), channel_id=1, source_target_pairs={{0,8},{1,121},{2,10},{3,123},{4,12},{5,125},{6,14},{7,127},{8,16},... | collective-permute-start | bytes 2433032 | tf_op jit(solution)/shard_map/ppermute | solution.py:722
  11.7 2.6 %collective-permute-start.3 = (f32[32,256]{1,0:T(8,128)S(1)}, f32[32,256]{1,0:T(8,128)S(1)}, u32[]{:S(2)}, u32[]{:S(2)}) collective-permute-start(f32[32,256]{1,0:T(8,128)S(1)} %get-tuple-element.26), channel_id=1, source_target_pairs={{8,0},{25,1},{42,2},{59,3},{76,4},{93,5},{110,6},{127,7},{0,8},{17... | collective-permute-start | bytes 98312 | tf_op jit(solution)/shard_map/ppermute | solution.py:686
  14.3 0.7 collective-permute-start.2
  15.0 0.0 copy-done
  15.0 0.0 copy-done.3
  15.0 0.0 copy-done.4
  15.0 0.0 copy-done.7
  15.0 0.0 copy-done.9
  15.0 4.6 %shard_map.123 = f32[32,256]{1,0:T(8,128)S(1)} custom-call(s32[1]{0:T(128)} %bitcast.4.v_ref, f32[144]{0:T(256)S(1)} %copy-done.9, f32[2,8,1152]{2,1,0:T(8,128)S(1)} %copy-done.4, f32[2,32,1152]{2,1,0:T(8,128)S(1)} %copy-done.3, f32[48,128]{1,0:T(8,128)S(1)} %copy-done.7, f32[32,13824]{1,0:T(8,128)S(1)} %copy-done, f32[32,256]{1,0:T(8,128)S(1)} %get-tuple-element.25.inner.after), custom_call_target="tpu_custom_call" | custom-call | tf_op jit(solution)/shard_map/pallas_call | solution.py:128
  19.6 5.6 %collective-permute-done.3 = f32[32,256]{1,0:T(8,128)S(1)} collective-permute-done((f32[32,256]{1,0:T(8,128)S(1)}, f32[32,256]{1,0:T(8,128)S(1)}, u32[]{:S(2)}, u32[]{:S(2)}) %collective-permute-start.3) | collective-permute-done | bytes 32800 | tf_op jit(solution)/shard_map/ppermute | solution.py:686
  25.2 0.0 collective-permute-done.2
  25.2 0.1 collective-permute-start.4
  25.3 1.2 %collective-permute-done.4 = f32[64,256]{1,0:T(8,128)S(1)} collective-permute-done((f32[64,256]{1,0:T(8,128)S(1)}, f32[64,256]{1,0:T(8,128)S(1)}, u32[]{:S(2)}, u32[]{:S(2)}) %collective-permute-start.4) | collective-permute-done | bytes 65568 | tf_op jit(solution)/shard_map/ppermute | solution.py:693
  26.5 0.0 collective-permute-done.1
  26.5 0.2 collective-permute-start.8
  26.8 5.1 %collective-permute-start.7 = (f32[64,256]{1,0:T(8,128)S(1)}, f32[64,256]{1,0:T(8,128)S(1)}, u32[]{:S(2)}, u32[]{:S(2)}) collective-permute-start(f32[64,256]{1,0:T(8,128)S(1)} %fusion.refs_0_), channel_id=1, source_target_pairs={{0,6},{1,7},{2,0},{3,1},{4,2},{5,3},{6,4},{7,5},{8,14},{9,15},{10,... | collective-permute-start | bytes 196616 | tf_op jit(solution)/shard_map/ppermute | solution.py:697
  31.9 0.0 collective-permute-start.6
  31.9 1.4 %collective-permute-start.5 = (f32[64,256]{1,0:T(8,128)S(1)}, f32[64,256]{1,0:T(8,128)S(1)}, u32[]{:S(2)}, u32[]{:S(2)}) collective-permute-start(f32[64,256]{1,0:T(8,128)S(1)} %fusion.refs_0_), channel_id=1, source_target_pairs={{0,2},{1,3},{2,4},{3,5},{4,6},{5,7},{6,0},{7,1},{8,10},{9,11},{10,... | collective-permute-start | bytes 196616 | tf_op jit(solution)/shard_map/ppermute | solution.py:697
  33.3 1.9 %collective-permute-done.7.refs_3_ = f32[64,256]{1,0:T(8,128)S(1)} collective-permute-done((f32[64,256]{1,0:T(8,128)S(1)}, f32[64,256]{1,0:T(8,128)S(1)}, u32[]{:S(2)}, u32[]{:S(2)}) %collective-permute-start.7) | collective-permute-done | bytes 65568 | tf_op jit(solution)/shard_map/ppermute | solution.py:697
  35.2 3.0 %collective-permute-done.6.refs_2_ = f32[64,256]{1,0:T(8,128)S(1)} collective-permute-done((f32[64,256]{1,0:T(8,128)S(1)}, f32[64,256]{1,0:T(8,128)S(1)}, u32[]{:S(2)}, u32[]{:S(2)}) %collective-permute-start.6) | collective-permute-done | bytes 65568 | tf_op jit(solution)/shard_map/ppermute | solution.py:697
  38.2 0.4 collective-permute-done.5.refs_1_
  38.6 0.0 copy-done.5
  38.6 0.0 copy-done.6
  38.6 0.0 copy-done.8
  38.6 3.8 %shard_map.124 = (f32[2,240,128]{2,1,0:T(8,128)S(1)}, f32[2,224,128]{2,1,0:T(8,128)S(1)}, f32[3,32,128]{2,1,0:T(8,128)S(1)}, f32[32,128]{1,0:T(8,128)S(1)}) custom-call(f32[64,256]{1,0:T(8,128)S(1)} %fusion.refs_0_, f32[64,256]{1,0:T(8,128)S(1)} %collective-permute-done.5.refs_1_, f32[64,256]{1,0:T(8,128)S(1)} %collective-permute-done.6.refs_2_, ...), custom_call_target="tpu_custom_call" | custom-call | tf_op jit(solution)/shard_map/pallas_call | solution.py:128
  42.4 0.0 collective-permute-done.8
  42.4 0.6 shard_map.125
  43.0 13.7 %shard_map.126 = (f32[32,12288]{1,0:T(8,128)S(1)}, f32[32,256]{1,0:T(8,128)S(1)}) custom-call(f32[2,240,128]{2,1,0:T(8,128)S(1)} %get-tuple-element.29.wk, f32[32,128]{1,0:T(8,128)S(1)} %get-tuple-element.30.after.moment, f32[32,22528]{1,0:T(8,128)S(1)} %get-tuple-element.33.raw, f32[64,128]{1,0:T(8,128)S(1)} %bitcast.13, ...), custom_call_target="tpu_custom_call" | custom-call | tf_op jit(solution)/shard_map/pallas_call | solution.py:128
  56.7 4.3 %collective-permute-start.10 = (f32[32,256]{1,0:T(8,128)S(1)}, f32[32,256]{1,0:T(8,128)S(1)}, u32[]{:S(2)}, u32[]{:S(2)}) collective-permute-start(f32[32,256]{1,0:T(8,128)S(1)} %get-tuple-element.36.after), channel_id=1, source_target_pairs={{8,0},{25,1},{42,2},{59,3},{76,4},{93,5},{110,6},{127,7},{0,8},{17... | collective-permute-start | bytes 98312 | tf_op jit(solution)/shard_map/ppermute | solution.py:686
  61.0 0.7 collective-permute-start.9
  61.7 7.8 %shard_map.127 = (f32[32,13824]{1,0:T(8,128)S(1)}, f32[40,256]{1,0:T(8,128)S(1)}) custom-call(s32[1]{0:T(128)} %bitcast.4.v_ref, f32[144]{0:T(256)S(1)} %copy-done.9, f32[2,8,1152]{2,1,0:T(8,128)S(1)} %copy-done.4, f32[2,224,128]{2,1,0:T(8,128)S(1)} %get-tuple-element.37.wl, f32[3,32,128]{2,1,0:T(8,128)S(1)} %get-tuple-element.38.src, ...), custom_call_target="tpu_custom_call" | custom-call | tf_op jit(solution)/shard_map/pallas_call | solution.py:128
  69.5 0.0 collective-permute-done.10
  69.5 0.0 collective-permute-done.9
  69.6 2.6 %collective-permute-start.11 = (f32[72,256]{1,0:T(8,128)S(1)}, f32[72,256]{1,0:T(8,128)S(1)}, u32[]{:S(2)}, u32[]{:S(2)}) collective-permute-start(f32[72,256]{1,0:T(8,128)S(1)} %pad_maximum_fusion.1), channel_id=1, source_target_pairs={{0,1},{1,0},{2,3},{3,2},{4,5},{5,4},{6,7},{7,6},{8,9},{9,8},{10,11... | collective-permute-start | bytes 221192 | tf_op jit(solution)/shard_map/ppermute | solution.py:693
  72.2 0.9 %collective-permute-done.11 = f32[72,256]{1,0:T(8,128)S(1)} collective-permute-done((f32[72,256]{1,0:T(8,128)S(1)}, f32[72,256]{1,0:T(8,128)S(1)}, u32[]{:S(2)}, u32[]{:S(2)}) %collective-permute-start.11) | collective-permute-done | bytes 73760 | tf_op jit(solution)/shard_map/ppermute | solution.py:693
  73.1 2.6 %collective-permute-start.14 = (f32[72,256]{1,0:T(8,128)S(1)}, f32[72,256]{1,0:T(8,128)S(1)}, u32[]{:S(2)}, u32[]{:S(2)}) collective-permute-start(f32[72,256]{1,0:T(8,128)S(1)} %fusion.1.refs_0_), channel_id=1, source_target_pairs={{0,6},{1,7},{2,0},{3,1},{4,2},{5,3},{6,4},{7,5},{8,14},{9,15},{10,... | collective-permute-start | bytes 221192 | tf_op jit(solution)/shard_map/ppermute | solution.py:697
  75.7 0.6 collective-permute-start.13
  76.4 1.3 %collective-permute-start.12 = (f32[72,256]{1,0:T(8,128)S(1)}, f32[72,256]{1,0:T(8,128)S(1)}, u32[]{:S(2)}, u32[]{:S(2)}) collective-permute-start(f32[72,256]{1,0:T(8,128)S(1)} %fusion.1.refs_0_), channel_id=1, source_target_pairs={{0,2},{1,3},{2,4},{3,5},{4,6},{5,7},{6,0},{7,1},{8,10},{9,11},{10,... | collective-permute-start | bytes 221192 | tf_op jit(solution)/shard_map/ppermute | solution.py:697
  77.7 0.7 collective-permute-done.14.refs_3_
  78.4 3.7 %collective-permute-done.13.refs_2_ = f32[72,256]{1,0:T(8,128)S(1)} collective-permute-done((f32[72,256]{1,0:T(8,128)S(1)}, f32[72,256]{1,0:T(8,128)S(1)}, u32[]{:S(2)}, u32[]{:S(2)}) %collective-permute-start.13) | collective-permute-done | bytes 73760 | tf_op jit(solution)/shard_map/ppermute | solution.py:697
  82.1 0.8 collective-permute-done.12.refs_1_
  82.9 7.6 %shard_map.128 = (f32[2048,128]{1,0:T(8,128)}, f32[32,32]{1,0:T(8,128)}, f32[32,13824]{1,0:T(8,128)}) custom-call(f32[72,256]{1,0:T(8,128)S(1)} %fusion.1.refs_0_, f32[72,256]{1,0:T(8,128)S(1)} %collective-permute-done.12.refs_1_, f32[72,256]{1,0:T(8,128)S(1)} %collective-permute-done.13.refs_2_, f32[72,256]{1,0:T(8,128)S(1)} %collective-permute-done.14.refs_3_, ...), custom_call_target="tpu_custom_call" | custom-call | tf_op jit(solution)/shard_map/pallas_call | solution.py:128
  (7 shorter events, 0.1 us)
Async XLA Ops:
  0.6 3.9 %copy-start.1 = (f32[32,4,16,128]{3,2,1,0:T(8,128)S(1)}, f32[32,4,16,128]{3,2,1,0:T(8,128)}, u32[]{:S(2)}) copy-start(f32[32,4,16,128]{3,2,1,0:T(8,128)} %param.10) | copy-start | bytes 3145732
  0.6 3.9 %copy-start.2 = (f32[4,16,128]{2,1,0:T(8,128)S(1)}, f32[4,16,128]{2,1,0:T(8,128)}, u32[]{:S(2)}) copy-start(f32[4,16,128]{2,1,0:T(8,128)} %param.13) | copy-start | bytes 98308
  1.7 8.1 %collective-permute-start = (f32[32,1,16,128]{3,2,1,0:T(8,128)S(1)}, f32[32,1,16,128]{3,2,1,0:T(8,128)S(1)}, u32[]{:S(2)}, u32[]{:S(2)}) collective-permute-start(f32[32,1,16,128]{3,2,1,0:T(8,128)S(1)} %slice.16), channel_id=1, source_target_pairs={{0,8},{8,16},{16,24},{24,32},{32,40},{40,48},{48,56},{56,64},{64,7... | collective-permute-start | bytes 786440 | tf_op jit(solution)/shard_map/ppermute | solution.py:704
  7.9 7.1 %copy-start = (f32[32,13824]{1,0:T(8,128)S(1)}, f32[32,13824]{1,0:T(8,128)}, u32[]{:S(2)}) copy-start(f32[32,13824]{1,0:T(8,128)} %values.3) | copy-start | bytes 5308420
  7.9 7.1 %copy-start.3 = (f32[2,32,1152]{2,1,0:T(8,128)S(1)}, f32[2,32,1152]{2,1,0:T(8,128)}, u32[]{:S(2)}) copy-start(f32[2,32,1152]{2,1,0:T(8,128)} %constant.34.clone.phi) | copy-start | bytes 884740
  7.9 7.1 %copy-start.4 = (f32[2,8,1152]{2,1,0:T(8,128)S(1)}, f32[2,8,1152]{2,1,0:T(8,128)}, u32[]{:S(2)}) copy-start(f32[2,8,1152]{2,1,0:T(8,128)} %constant.33.clone.rows) | copy-start | bytes 221188
  7.9 7.1 %copy-start.7 = (f32[48,128]{1,0:T(8,128)S(1)}, f32[48,128]{1,0:T(8,128)}, u32[]{:S(2)}) copy-start(f32[48,128]{1,0:T(8,128)} %constant.35.clone.scale) | copy-start | bytes 73732
  7.9 7.1 %copy-start.9 = (f32[144]{0:T(256)S(1)}, f32[144]{0:T(256)}, u32[]{:S(2)}) copy-start(f32[144]{0:T(256)} %constant.32.clone.speeds) | copy-start | bytes 1732
  9.8 28.8 %copy-start.5 = (f32[32,896]{1,0:T(8,128)S(1)}, f32[32,896]{1,0:T(8,128)}, u32[]{:S(2)}) copy-start(f32[32,896]{1,0:T(8,128)} %constant.36.clone.refs_5_) | copy-start | bytes 344068
  9.8 28.8 %copy-start.6 = (f32[32,32]{1,0:T(8,128)S(1)}, f32[32,32]{1,0:T(8,128)}, u32[]{:S(2)}) copy-start(f32[32,32]{1,0:T(8,128)} %refs_4_.3) | copy-start | bytes 12292
  9.8 28.8 %copy-start.8 = (f32[8,128]{1,0:T(8,128)S(1)}, f32[8,128]{1,0:T(8,128)}, u32[]{:S(2)}) copy-start(f32[8,128]{1,0:T(8,128)} %constant.37.clone.refs_6_) | copy-start | bytes 12292
  10.1 16.4 %collective-permute-start.1 = (f32[33,3,16,128]{3,2,1,0:T(8,128)S(1)}, f32[33,3,16,128]{3,2,1,0:T(8,128)S(1)}, u32[]{:S(2)}, u32[]{:S(2)}) collective-permute-start(f32[33,3,16,128]{3,2,1,0:T(8,128)S(1)} %pad_maximum_fusion), channel_id=1, source_target_pairs={{0,8},{1,121},{2,10},{3,123},{4,12},{5,125},{6,14},{7,127},{8,16},... | collective-permute-start | bytes 2433032 | tf_op jit(solution)/shard_map/ppermute | solution.py:722
  11.7 13.4 %collective-permute-start.3 = (f32[32,256]{1,0:T(8,128)S(1)}, f32[32,256]{1,0:T(8,128)S(1)}, u32[]{:S(2)}, u32[]{:S(2)}) collective-permute-start(f32[32,256]{1,0:T(8,128)S(1)} %get-tuple-element.26), channel_id=1, source_target_pairs={{8,0},{25,1},{42,2},{59,3},{76,4},{93,5},{110,6},{127,7},{0,8},{17... | collective-permute-start | bytes 98312 | tf_op jit(solution)/shard_map/ppermute | solution.py:686
  14.3 10.8 %collective-permute-start.2 = (f32[32,256]{1,0:T(8,128)S(1)}, f32[32,256]{1,0:T(8,128)S(1)}, u32[]{:S(2)}, u32[]{:S(2)}) collective-permute-start(f32[32,256]{1,0:T(8,128)S(1)} %get-tuple-element.26), channel_id=1, source_target_pairs={{0,0},{17,1},{34,2},{51,3},{68,4},{85,5},{102,6},{119,7},{8,8},{25... | collective-permute-start | bytes 98312 | tf_op jit(solution)/shard_map/ppermute | solution.py:686
  25.2 1.3 %collective-permute-start.4 = (f32[64,256]{1,0:T(8,128)S(1)}, f32[64,256]{1,0:T(8,128)S(1)}, u32[]{:S(2)}, u32[]{:S(2)}) collective-permute-start(f32[64,256]{1,0:T(8,128)S(1)} %pad_maximum_fusion.2), channel_id=1, source_target_pairs={{0,1},{1,0},{2,3},{3,2},{4,5},{5,4},{6,7},{7,6},{8,9},{9,8},{10,11... | collective-permute-start | bytes 196616 | tf_op jit(solution)/shard_map/ppermute | solution.py:693
  26.5 15.9 %collective-permute-start.8 = (f32[33,3,16,128]{3,2,1,0:T(8,128)S(1)}, f32[33,3,16,128]{3,2,1,0:T(8,128)S(1)}, u32[]{:S(2)}, u32[]{:S(2)}) collective-permute-start(f32[33,3,16,128]{3,2,1,0:T(8,128)S(1)} %collective-permute-done.1), channel_id=1, source_target_pairs={{0,1},{1,0},{2,3},{3,2},{4,5},{5,4},{6,7},{7,6},{8,9},{9,8},{10,11... | collective-permute-start | bytes 2433032 | tf_op jit(solution)/shard_map/ppermute | solution.py:725
  26.8 8.4 %collective-permute-start.7 = (f32[64,256]{1,0:T(8,128)S(1)}, f32[64,256]{1,0:T(8,128)S(1)}, u32[]{:S(2)}, u32[]{:S(2)}) collective-permute-start(f32[64,256]{1,0:T(8,128)S(1)} %fusion.refs_0_), channel_id=1, source_target_pairs={{0,6},{1,7},{2,0},{3,1},{4,2},{5,3},{6,4},{7,5},{8,14},{9,15},{10,... | collective-permute-start | bytes 196616 | tf_op jit(solution)/shard_map/ppermute | solution.py:697
  31.9 6.3 %collective-permute-start.6 = (f32[64,256]{1,0:T(8,128)S(1)}, f32[64,256]{1,0:T(8,128)S(1)}, u32[]{:S(2)}, u32[]{:S(2)}) collective-permute-start(f32[64,256]{1,0:T(8,128)S(1)} %fusion.refs_0_), channel_id=1, source_target_pairs={{0,4},{1,5},{2,6},{3,7},{4,0},{5,1},{6,2},{7,3},{8,12},{9,13},{10,... | collective-permute-start | bytes 196616 | tf_op jit(solution)/shard_map/ppermute | solution.py:697
  31.9 6.7 %collective-permute-start.5 = (f32[64,256]{1,0:T(8,128)S(1)}, f32[64,256]{1,0:T(8,128)S(1)}, u32[]{:S(2)}, u32[]{:S(2)}) collective-permute-start(f32[64,256]{1,0:T(8,128)S(1)} %fusion.refs_0_), channel_id=1, source_target_pairs={{0,2},{1,3},{2,4},{3,5},{4,6},{5,7},{6,0},{7,1},{8,10},{9,11},{10,... | collective-permute-start | bytes 196616 | tf_op jit(solution)/shard_map/ppermute | solution.py:697
  56.7 12.8 %collective-permute-start.10 = (f32[32,256]{1,0:T(8,128)S(1)}, f32[32,256]{1,0:T(8,128)S(1)}, u32[]{:S(2)}, u32[]{:S(2)}) collective-permute-start(f32[32,256]{1,0:T(8,128)S(1)} %get-tuple-element.36.after), channel_id=1, source_target_pairs={{8,0},{25,1},{42,2},{59,3},{76,4},{93,5},{110,6},{127,7},{0,8},{17... | collective-permute-start | bytes 98312 | tf_op jit(solution)/shard_map/ppermute | solution.py:686
  61.0 8.5 %collective-permute-start.9 = (f32[32,256]{1,0:T(8,128)S(1)}, f32[32,256]{1,0:T(8,128)S(1)}, u32[]{:S(2)}, u32[]{:S(2)}) collective-permute-start(f32[32,256]{1,0:T(8,128)S(1)} %get-tuple-element.36.after), channel_id=1, source_target_pairs={{0,0},{17,1},{34,2},{51,3},{68,4},{85,5},{102,6},{119,7},{8,8},{25... | collective-permute-start | bytes 98312 | tf_op jit(solution)/shard_map/ppermute | solution.py:686
  69.6 3.5 %collective-permute-start.11 = (f32[72,256]{1,0:T(8,128)S(1)}, f32[72,256]{1,0:T(8,128)S(1)}, u32[]{:S(2)}, u32[]{:S(2)}) collective-permute-start(f32[72,256]{1,0:T(8,128)S(1)} %pad_maximum_fusion.1), channel_id=1, source_target_pairs={{0,1},{1,0},{2,3},{3,2},{4,5},{5,4},{6,7},{7,6},{8,9},{9,8},{10,11... | collective-permute-start | bytes 221192 | tf_op jit(solution)/shard_map/ppermute | solution.py:693
  73.1 5.3 %collective-permute-start.14 = (f32[72,256]{1,0:T(8,128)S(1)}, f32[72,256]{1,0:T(8,128)S(1)}, u32[]{:S(2)}, u32[]{:S(2)}) collective-permute-start(f32[72,256]{1,0:T(8,128)S(1)} %fusion.1.refs_0_), channel_id=1, source_target_pairs={{0,6},{1,7},{2,0},{3,1},{4,2},{5,3},{6,4},{7,5},{8,14},{9,15},{10,... | collective-permute-start | bytes 221192 | tf_op jit(solution)/shard_map/ppermute | solution.py:697
  75.7 6.4 %collective-permute-start.13 = (f32[72,256]{1,0:T(8,128)S(1)}, f32[72,256]{1,0:T(8,128)S(1)}, u32[]{:S(2)}, u32[]{:S(2)}) collective-permute-start(f32[72,256]{1,0:T(8,128)S(1)} %fusion.1.refs_0_), channel_id=1, source_target_pairs={{0,4},{1,5},{2,6},{3,7},{4,0},{5,1},{6,2},{7,3},{8,12},{9,13},{10,... | collective-permute-start | bytes 221192 | tf_op jit(solution)/shard_map/ppermute | solution.py:697
  76.4 6.5 %collective-permute-start.12 = (f32[72,256]{1,0:T(8,128)S(1)}, f32[72,256]{1,0:T(8,128)S(1)}, u32[]{:S(2)}, u32[]{:S(2)}) collective-permute-start(f32[72,256]{1,0:T(8,128)S(1)} %fusion.1.refs_0_), channel_id=1, source_target_pairs={{0,2},{1,3},{2,4},{3,5},{4,6},{5,7},{6,0},{7,1},{8,10},{9,11},{10,... | collective-permute-start | bytes 221192 | tf_op jit(solution)/shard_map/ppermute | solution.py:697

commit v5 on v4

--- a/solution.py
+++ b/solution.py
@@ -110,6 +110,10 @@
     return mm(a, b, dot_t)
 
 
+def aligned(index, size):
+    return index if isinstance(index, int) else pl.multiple_of(index, size)
+
+
 def lanes(shape):
     return lax.broadcasted_iota(jnp.int32, shape, len(shape) - 1)
 
@@ -155,7 +159,7 @@
     )
 
 
-def point_sums_kernel(v_ref, speeds, rows, phi, scale, values, after, out):
+def point_sums_kernel(low, high, v_ref, speeds, rows, phi, scale, values, after, out):
     q0 = v_ref[0] * Q1
     phi_parts = [split(phi[h]) for h in range(2)]
 
@@ -163,7 +167,7 @@
         sums, y, moments = list(carry[:2]), carry[2], carry[3]
         u = speeds[q0 + b] + speeds[NVD + q0 + b]
         for h in range(2):
-            start = pl.multiple_of(b * (2 * HALF) + h * HALF, 128)
+            start = aligned(b * (2 * HALF) + h * HALF, 128)
             sh, sl = split(stacked(values[:, pl.ds(start, HALF)], rows, h))
             lh, ll = sh[:RANK], sl[:RANK]
             ph, plo = phi_parts[h]
@@ -177,16 +181,21 @@
         return sums[0], sums[1], y, moments
 
     zero = jnp.zeros((RANK, 128), f32)
-    first, second, y, moments = lax.fori_loop(0, Q1, body, (zero, zero, zero, jnp.zeros((RANK, RANK), f32)))
+    first, second, y, moments = lax.fori_loop(low, high, body, (zero, zero, zero, jnp.zeros((RANK, RANK), f32)))
     moments = jnp.concatenate([jnp.zeros((RANK, 96), f32), moments], axis=1)
     tile_a, tile_b = point_tiles(first, second, y, v_ref[0] >= 4, moments)
+    if low > 0:
+        tile_a, tile_b = tile_a + after[:, :128], tile_b + after[:, 128:]
     out[:, :128] = tile_a
     out[:, 128:] = tile_b
 
 
-def point_sums(v, values, after):
+def point_sums(v, values, low, high, after):
+    def kernel(*refs):
+        point_sums_kernel(low, high, *refs)
+
     return call(
-        point_sums_kernel, [((RANK, 256), f32)], "ssvvvva",
+        kernel, [((RANK, 256), f32)], "ssvvvvv",
         (v, SPEEDS, ROWS, PHI, PHI_SCALE, values, after), mib=12,
     )[0]
 
@@ -195,7 +204,7 @@
     def load(p, carry):
         for y in range(NY):
             block = values[pl.ds(p * NY + y, RANK, stride=OWN * NY), :]
-            at = pl.multiple_of(p * PLANE + y * NZ, 128)
+            at = aligned(p * PLANE + y * NZ, 128)
             a, b = split(block)
             hi[:, pl.ds(at + PLANE, NZ)] = a
             lo[:, pl.ds(at + PLANE, NZ)] = b
@@ -214,7 +223,7 @@
 
     def body(p, carry):
         t, c = carry
-        at = pl.multiple_of(p * PLANE, 128)
+        at = aligned(p * PLANE, 128)
 
         def stack(main, turned):
             here = main[:, pl.ds(at + PLANE, PLANE)]
@@ -394,7 +403,7 @@
         u = up + um
         moving = [piece(kind, 0) + up * piece(kind, 1) + um * piece(kind, 4) for kind in range(2)]
         heads = [weights_of(m) for m in moving]
-        first = pl.multiple_of(b * (2 * HALF), 128)
+        first = aligned(b * (2 * HALF), 128)
         states = [values[:, pl.ds(first, HALF)], values[:, pl.ds(first + HALF, HALF)]]
         raws = [split(state) for state in states]
         for n in range(SUB):
@@ -423,7 +432,7 @@
                 for h in range(2)
             ]
         for h in range(2):
-            start = pl.multiple_of(b * (2 * HALF) + h * HALF, 128)
+            start = aligned(b * (2 * HALF) + h * HALF, 128)
             state = states[h]
             raw_hi, raw_lo = raws[h]
             new[:, pl.ds(start, HALF)] = state
@@ -474,7 +483,7 @@
 
         def load(p, carry, source=source, place=place):
             for y in range(NY):
-                at = pl.multiple_of((p + place * (LOW + OWN)) * PLANE + y * NZ, 128)
+                at = aligned((p + place * (LOW + OWN)) * PLANE + y * NZ, 128)
                 state[:, pl.ds(at, NZ)] = source[pl.ds(p * NY + y, RANK, stride=HIGH * NY), :]
             return carry
 
@@ -513,12 +522,12 @@
         begin, end = 1 + n, WIDE - 1 - n
 
         def tile(t, j, src=src):
-            cells = src[:, pl.ds(pl.multiple_of(t * PLANE + j * 256, 256), 256)]
+            cells = src[:, pl.ds(aligned(t * PLANE + j * 256, 256), 256)]
             a, b = split(cells)
             return cells, jnp.concatenate([a, b, a], axis=0)
 
         def put(t, y, block, dst=dst, shift=shift):
-            dst[:, pl.ds(pl.multiple_of((t - shift) * PLANE + y * NZ, 128), NZ)] = block
+            dst[:, pl.ds(aligned((t - shift) * PLANE + y * NZ, 128), NZ)] = block
 
         def step(t, carry, w=w, tile=tile, put=put, skip=skip):
             scale = moment[...]
@@ -549,7 +558,8 @@
 
         for j in range(NY // 2):
             passed[:, j * 256 : (j + 1) * 256] = dot(w[skip : skip + RANK], tile(begin - 1, j)[1])
-        lax.fori_loop(begin, end, step, 0)
+        for t in range(begin, end):
+            step(t, 0)
         for j in range(NY // 2):
             mixed = dot(w[skip + RANK : skip + 2 * RANK], tile(end, j)[1])
             for i in range(2):
@@ -560,12 +570,12 @@
         t, c = carry
         turned, relaxed = [], []
         for y in range(NY):
-            block = new[:, pl.ds(pl.multiple_of((p + 2) * PLANE + y * NZ, 128), NZ)]
+            block = new[:, pl.ds(aligned((p + 2) * PLANE + y * NZ, 128), NZ)]
             turned.append(split(roll_lanes(block, 1)))
             relaxed.append(split(block * rates[pl.ds(p * NY + y, 1), :]))
-        here = split(new[:, pl.ds(pl.multiple_of((p + 2) * PLANE, 128), PLANE)])
-        behind = split(new[:, pl.ds(pl.multiple_of((p + 1) * PLANE, 128), PLANE)])
-        old = split(raw[:, pl.ds(pl.multiple_of((p + LOW) * PLANE, 128), PLANE)])
+        here = split(new[:, pl.ds(aligned((p + 2) * PLANE, 128), PLANE)])
+        behind = split(new[:, pl.ds(aligned((p + 1) * PLANE, 128), PLANE)])
+        old = split(raw[:, pl.ds(aligned((p + LOW) * PLANE, 128), PLANE)])
 
         def stack(k):
             wrapped = jnp.concatenate([here[k][:, PLANE - NZ :], here[k][:, : PLANE - NZ]], axis=1)
@@ -577,7 +587,10 @@
         part = part[:RANK] + part[RANK:] + dot_t(here[0], stack(1))
         return t + part[:, :128], c + part[:, 128:]
 
-    t, c = lax.fori_loop(0, OWN, body, (jnp.zeros((RANK, 128), f32), jnp.zeros((RANK, 64), f32)))
+    carry = (jnp.zeros((RANK, 128), f32), jnp.zeros((RANK, 64), f32))
+    for p in range(OWN):
+        carry = body(p, carry)
+    t, c = carry
     out[:, :128] = t
     out[:, 128:] = jnp.concatenate([c, jnp.zeros((RANK, 64), f32)], axis=1)
 
@@ -614,20 +627,18 @@
     def out_space(p, carry):
         for half in range(2):
             size = PLANE // 2
-            at = pl.multiple_of((p + 2) * PLANE + half * size, 128)
+            at = aligned((p + 2) * PLANE + half * size, 128)
             hi, lo = split(kinetic[:, pl.ds(at, size)])
             made = dot(w_space, jnp.concatenate([hi, lo, hi], axis=0))
             for y in range(NY // 2):
                 fresh_space[pl.ds(p * NY + half * (NY // 2) + y, RANK, stride=OWN * NY), :] = made[:, y * NZ : (y + 1) * NZ]
         return carry
 
-    lax.fori_loop(0, OWN, out_space, 0)
-    copies = [pltpu.make_async_copy(fresh_space, space_out, sems.at[0])]
-    copies[0].start()
     third = 2 * Q1 * HALF // 3
+    copies = []
 
     def out_point(i, carry):
-        at = pl.multiple_of(i * 1536, 512)
+        at = aligned(i * 1536, 512)
         hi, lo = split(spread[:, pl.ds(at, 1536)])
         fresh_point[:, pl.ds(at, 1536)] = dot(w_point, jnp.concatenate([hi, lo, hi], axis=0))
         return carry
@@ -637,6 +648,10 @@
         cells = pl.ds(k * third, third)
         copies.append(pltpu.make_async_copy(fresh_point.at[:, cells], point_out.at[:, cells], sems.at[k + 1]))
         copies[-1].start()
+
+    lax.fori_loop(0, OWN, out_space, 0)
+    copies.append(pltpu.make_async_copy(fresh_space, space_out, sems.at[0]))
+    copies[-1].start()
 
     inverse_t = transposed(inverse)
     inverse_vt = transposed(inverse_v)
@@ -715,11 +730,12 @@
     pair = [(w, w ^ 1) for w in range(8)]
 
     inner, own = space_sums(values, rates)
-    point = point_sums(v, velocity_factor, inner)
+    point = point_sums(v, velocity_factor, 0, Q1 // 2, inner)
     space, edge = edge_sums(own, below1, inner)
     moved = spread_pairs(space)
     halo, space = lax.optimization_barrier((halo, space))
     mine = lax.ppermute(halo, ("space", "vel"), route)
+    point = point_sums(v, velocity_factor, Q1 // 2, Q1, point)
     parts = vel_parts(moved, point)
     mine, parts[0] = lax.optimization_barrier((mine, parts[0]))
     other = lax.ppermute(mine, "vel", pair)

time: 90.7 us -> 88 us (0.970)
  Pallas kernels: 41.7 us -> 39.3 us
    pallas_call x8 -> x9, Pallas kernels: 41.7 us -> 39.3 us  [call(): pl.pallas_call(kernel, out_shape=[jax.ShapeDtypeStruct(s, d) for s, d in...]
  transfers between devices with their start and end apart: 15 -> 15, of which waited for: 10 -> 10; matrix products, arithmetic and copies ran while one was open for 1% -> 1% of each run, Pallas kernels for 22% -> 23%
where the time goes in v5:
time: 88 us; the launch traced here: 87.8 us
  Pallas kernels  39.3 us (45%)
  starting transfers between devices  25.6 us (29%)
  waiting for transfers between devices  19.3 us (22%)
  local copies, waits for them, and re-layouts  2.31 us (3%)
  between operations  1.11 us (1%)
    pallas_call x9, Pallas kernels, call(): pl.pallas_call(kernel, out_shape=[jax.ShapeDtypeStruct(s, d) for s, d in...  39.3 us
    ppermute x6, starting transfers between devices, vel_parts(): parts.append(lax.ppermute(joint, 'vel', route))  11.2 us
    ppermute x6, waiting for transfers between devices, vel_parts(): parts.append(lax.ppermute(joint, 'vel', route))  10.4 us
    ppermute x4, starting transfers between devices, spread_pairs(): moved.append(lax.ppermute(space_part, ('space', 'vel'), route))  8.42 us
    ppermute x4, waiting for transfers between devices, spread_pairs(): moved.append(lax.ppermute(space_part, ('space', 'vel'), route))  4.89 us
    ppermute x2, starting transfers between devices, vel_parts(): joint = joint + lax.ppermute(joint, 'vel', pair)  2.68 us
    ppermute x2, waiting for transfers between devices, vel_parts(): joint = joint + lax.ppermute(joint, 'vel', pair)  2.15 us
    ppermute x1, waiting for transfers between devices, per_device(): lax.ppermute(space_factor[:, OWN - 1:], 'space', up).reshape(-1, NZ)  1.8 us
  transfers between devices with their start and end apart: 15, of which 10 were waited for; matrix products, arithmetic and copies ran while one was open for 1% of the time, Pallas kernels for 23%

profile of v5, /device:TPU:2, one launch (start us, length us, event | category | flops | bytes accessed | tf_op | source)
XLA Modules:
  0.0 87.8 jit_solution(13584474687980563602)
XLA Ops:
  0.6 0.0 copy-start.1
  0.6 0.0 copy-start.4
  0.7 1.1 %slice.16 = f32[32,1,16,128]{3,2,1,0:T(8,128)S(1)} slice(f32[32,4,16,128]{3,2,1,0:T(8,128)} %param.10), slice={[0:32], [3:4], [0:16], [0:128]} | slice | bytes 524288 | tf_op jit(solution)/shard_map/slice | solution.py:719
  1.7 1.6 %collective-permute-start = (f32[32,1,16,128]{3,2,1,0:T(8,128)S(1)}, f32[32,1,16,128]{3,2,1,0:T(8,128)S(1)}, u32[]{:S(2)}, u32[]{:S(2)}) collective-permute-start(f32[32,1,16,128]{3,2,1,0:T(8,128)S(1)} %slice.16), channel_id=1, source_target_pairs={{0,8},{8,16},{16,24},{24,32},{32,40},{40,48},{48,56},{56,64},{64,7... | collective-permute-start | bytes 786440 | tf_op jit(solution)/shard_map/ppermute | solution.py:719
  3.3 1.2 %slice.13 = f32[32,3,16,128]{3,2,1,0:T(8,128)S(1)} slice(f32[32,4,16,128]{3,2,1,0:T(8,128)} %param.10), slice={[0:32], [0:3], [0:16], [0:128]} | slice | bytes 1572864 | tf_op jit(solution)/shard_map/slice | solution.py:726
  4.5 0.0 copy-done.1
  4.5 0.0 copy-done.4
  4.5 3.4 %shard_map.121 = (f32[32,256]{1,0:T(8,128)S(1)}, f32[32,8192]{1,0:T(8,128)S(1)}) custom-call(f32[2048,128]{1,0:T(8,128)S(1)} %bitcast.9, f32[64,128]{1,0:T(8,128)S(1)} %bitcast.12), custom_call_target="tpu_custom_call" | custom-call | tf_op jit(solution)/shard_map/pallas_call | solution.py:132
  7.9 0.0 copy-start
  7.9 0.0 copy-start.2
  7.9 0.0 copy-start.3
  7.9 0.0 copy-start.6
  7.9 0.0 copy-start.8
  8.0 0.1 pad_maximum_fusion
  8.0 1.8 %collective-permute-done = f32[32,1,16,128]{3,2,1,0:T(8,128)S(1)} collective-permute-done((f32[32,1,16,128]{3,2,1,0:T(8,128)S(1)}, f32[32,1,16,128]{3,2,1,0:T(8,128)S(1)}, u32[]{:S(2)}, u32[]{:S(2)}) %collective-permute-start) | collective-permute-done | bytes 262176 | tf_op jit(solution)/shard_map/ppermute | solution.py:719
  9.8 0.3 shard_map.122
  10.1 1.6 %collective-permute-start.1 = (f32[33,3,16,128]{3,2,1,0:T(8,128)S(1)}, f32[33,3,16,128]{3,2,1,0:T(8,128)S(1)}, u32[]{:S(2)}, u32[]{:S(2)}) collective-permute-start(f32[33,3,16,128]{3,2,1,0:T(8,128)S(1)} %pad_maximum_fusion), channel_id=1, source_target_pairs={{0,8},{1,121},{2,10},{3,123},{4,12},{5,125},{6,14},{7,127},{8,16},... | collective-permute-start | bytes 2433032 | tf_op jit(solution)/shard_map/ppermute | solution.py:737
  11.7 2.6 %collective-permute-start.3 = (f32[32,256]{1,0:T(8,128)S(1)}, f32[32,256]{1,0:T(8,128)S(1)}, u32[]{:S(2)}, u32[]{:S(2)}) collective-permute-start(f32[32,256]{1,0:T(8,128)S(1)} %get-tuple-element.26), channel_id=1, source_target_pairs={{8,0},{25,1},{42,2},{59,3},{76,4},{93,5},{110,6},{127,7},{0,8},{17... | collective-permute-start | bytes 98312 | tf_op jit(solution)/shard_map/ppermute | solution.py:701
  14.3 0.7 collective-permute-start.2
  15.0 0.0 copy-done
  15.0 0.0 copy-done.2
  15.0 0.0 copy-done.3
  15.0 0.0 copy-done.6
  15.0 0.0 copy-done.8
  15.0 2.6 %shard_map.123.refs_6_ = f32[32,256]{1,0:T(8,128)S(1)} custom-call(s32[1]{0:T(128)} %bitcast.4.refs_0_.v_ref, f32[144]{0:T(256)S(1)} %copy-done.8, f32[2,8,1152]{2,1,0:T(8,128)S(1)} %copy-done.3, f32[2,32,1152]{2,1,0:T(8,128)S(1)} %copy-done.2, f32[48,128]{1,0:T(8,128)S(1)} %copy-done.6, f32[32,13824]{1,0:T(8,128)S(1)} %copy-done, ...), custom_call_target="tpu_custom_call" | custom-call | tf_op jit(solution)/shard_map/pallas_call | solution.py:132
  17.6 0.0 copy-start.5
  17.6 0.0 copy-start.7
  17.6 0.0 copy-start.9
  17.7 2.6 %shard_map.124 = f32[32,256]{1,0:T(8,128)S(1)} custom-call(s32[1]{0:T(128)} %bitcast.4.refs_0_.v_ref, f32[144]{0:T(256)S(1)} %copy-done.8, f32[2,8,1152]{2,1,0:T(8,128)S(1)} %copy-done.3, f32[2,32,1152]{2,1,0:T(8,128)S(1)} %copy-done.2, f32[48,128]{1,0:T(8,128)S(1)} %copy-done.6, f32[32,13824]{1,0:T(8,128)S(1)} %copy-done, f32[32,256]{1,0:T(8,128)S(1)} %shard_map.123.refs_6_), custom_call_target="tpu_custom_call" | custom-call | tf_op jit(solution)/shard_map/pallas_call | solution.py:132
  20.3 4.9 %collective-permute-done.3 = f32[32,256]{1,0:T(8,128)S(1)} collective-permute-done((f32[32,256]{1,0:T(8,128)S(1)}, f32[32,256]{1,0:T(8,128)S(1)}, u32[]{:S(2)}, u32[]{:S(2)}) %collective-permute-start.3) | collective-permute-done | bytes 32800 | tf_op jit(solution)/shard_map/ppermute | solution.py:701
  25.1 0.0 collective-permute-done.2
  25.2 0.1 collective-permute-start.4
  25.3 1.2 %collective-permute-done.4 = f32[64,256]{1,0:T(8,128)S(1)} collective-permute-done((f32[64,256]{1,0:T(8,128)S(1)}, f32[64,256]{1,0:T(8,128)S(1)}, u32[]{:S(2)}, u32[]{:S(2)}) %collective-permute-start.4) | collective-permute-done | bytes 65568 | tf_op jit(solution)/shard_map/ppermute | solution.py:708
  26.5 0.0 collective-permute-done.1
  26.5 0.2 collective-permute-start.8
  26.8 5.1 %collective-permute-start.7 = (f32[64,256]{1,0:T(8,128)S(1)}, f32[64,256]{1,0:T(8,128)S(1)}, u32[]{:S(2)}, u32[]{:S(2)}) collective-permute-start(f32[64,256]{1,0:T(8,128)S(1)} %fusion.refs_0_), channel_id=1, source_target_pairs={{0,6},{1,7},{2,0},{3,1},{4,2},{5,3},{6,4},{7,5},{8,14},{9,15},{10,... | collective-permute-start | bytes 196616 | tf_op jit(solution)/shard_map/ppermute | solution.py:712
  31.9 0.0 collective-permute-start.6
  31.9 1.4 %collective-permute-start.5 = (f32[64,256]{1,0:T(8,128)S(1)}, f32[64,256]{1,0:T(8,128)S(1)}, u32[]{:S(2)}, u32[]{:S(2)}) collective-permute-start(f32[64,256]{1,0:T(8,128)S(1)} %fusion.refs_0_), channel_id=1, source_target_pairs={{0,2},{1,3},{2,4},{3,5},{4,6},{5,7},{6,0},{7,1},{8,10},{9,11},{10,... | collective-permute-start | bytes 196616 | tf_op jit(solution)/shard_map/ppermute | solution.py:712
  33.3 1.9 %collective-permute-done.7.refs_3_ = f32[64,256]{1,0:T(8,128)S(1)} collective-permute-done((f32[64,256]{1,0:T(8,128)S(1)}, f32[64,256]{1,0:T(8,128)S(1)}, u32[]{:S(2)}, u32[]{:S(2)}) %collective-permute-start.7) | collective-permute-done | bytes 65568 | tf_op jit(solution)/shard_map/ppermute | solution.py:712
  35.2 3.0 %collective-permute-done.6.refs_2_ = f32[64,256]{1,0:T(8,128)S(1)} collective-permute-done((f32[64,256]{1,0:T(8,128)S(1)}, f32[64,256]{1,0:T(8,128)S(1)}, u32[]{:S(2)}, u32[]{:S(2)}) %collective-permute-start.6) | collective-permute-done | bytes 65568 | tf_op jit(solution)/shard_map/ppermute | solution.py:712
  38.2 0.4 collective-permute-done.5.refs_1_
  38.6 0.0 copy-done.5
  38.6 0.0 copy-done.7
  38.6 0.0 copy-done.9
  38.6 3.8 %shard_map.125 = (f32[2,240,128]{2,1,0:T(8,128)S(1)}, f32[2,224,128]{2,1,0:T(8,128)S(1)}, f32[3,32,128]{2,1,0:T(8,128)S(1)}, f32[32,128]{1,0:T(8,128)S(1)}) custom-call(f32[64,256]{1,0:T(8,128)S(1)} %fusion.refs_0_, f32[64,256]{1,0:T(8,128)S(1)} %collective-permute-done.5.refs_1_, f32[64,256]{1,0:T(8,128)S(1)} %collective-permute-done.6.refs_2_, ...), custom_call_target="tpu_custom_call" | custom-call | tf_op jit(solution)/shard_map/pallas_call | solution.py:132
  42.4 0.0 collective-permute-done.8
  42.4 0.6 shard_map.126
  43.0 10.5 %shard_map.127 = (f32[32,12288]{1,0:T(8,128)S(1)}, f32[32,256]{1,0:T(8,128)S(1)}) custom-call(f32[2,240,128]{2,1,0:T(8,128)S(1)} %get-tuple-element.29.wk, f32[32,128]{1,0:T(8,128)S(1)} %get-tuple-element.30.after.moment, f32[32,22528]{1,0:T(8,128)S(1)} %get-tuple-element.33.raw, f32[64,128]{1,0:T(8,128)S(1)} %bitcast.13, ...), custom_call_target="tpu_custom_call" | custom-call | tf_op jit(solution)/shard_map/pallas_call | solution.py:132
  53.5 4.3 %collective-permute-start.10 = (f32[32,256]{1,0:T(8,128)S(1)}, f32[32,256]{1,0:T(8,128)S(1)}, u32[]{:S(2)}, u32[]{:S(2)}) collective-permute-start(f32[32,256]{1,0:T(8,128)S(1)} %get-tuple-element.36.after), channel_id=1, source_target_pairs={{8,0},{25,1},{42,2},{59,3},{76,4},{93,5},{110,6},{127,7},{0,8},{17... | collective-permute-start | bytes 98312 | tf_op jit(solution)/shard_map/ppermute | solution.py:701
  57.8 0.9 collective-permute-start.9
  58.7 7.8 %shard_map.128 = (f32[32,13824]{1,0:T(8,128)S(1)}, f32[40,256]{1,0:T(8,128)S(1)}) custom-call(s32[1]{0:T(128)} %bitcast.4.refs_0_.v_ref, f32[144]{0:T(256)S(1)} %copy-done.8, f32[2,8,1152]{2,1,0:T(8,128)S(1)} %copy-done.3, f32[2,224,128]{2,1,0:T(8,128)S(1)} %get-tuple-element.37.wl, f32[3,32,128]{2,1,0:T(8,128)S(1)} %get-tuple-element.38.src, ...), custom_call_target="tpu_custom_call" | custom-call | tf_op jit(solution)/shard_map/pallas_call | solution.py:132
  66.5 0.0 collective-permute-done.10
  66.5 0.0 collective-permute-done.9
  66.5 2.6 %collective-permute-start.11 = (f32[72,256]{1,0:T(8,128)S(1)}, f32[72,256]{1,0:T(8,128)S(1)}, u32[]{:S(2)}, u32[]{:S(2)}) collective-permute-start(f32[72,256]{1,0:T(8,128)S(1)} %pad_maximum_fusion.1), channel_id=1, source_target_pairs={{0,1},{1,0},{2,3},{3,2},{4,5},{5,4},{6,7},{7,6},{8,9},{9,8},{10,11... | collective-permute-start | bytes 221192 | tf_op jit(solution)/shard_map/ppermute | solution.py:708
  69.1 0.9 %collective-permute-done.11 = f32[72,256]{1,0:T(8,128)S(1)} collective-permute-done((f32[72,256]{1,0:T(8,128)S(1)}, f32[72,256]{1,0:T(8,128)S(1)}, u32[]{:S(2)}, u32[]{:S(2)}) %collective-permute-start.11) | collective-permute-done | bytes 73760 | tf_op jit(solution)/shard_map/ppermute | solution.py:708
  70.1 2.6 %collective-permute-start.14 = (f32[72,256]{1,0:T(8,128)S(1)}, f32[72,256]{1,0:T(8,128)S(1)}, u32[]{:S(2)}, u32[]{:S(2)}) collective-permute-start(f32[72,256]{1,0:T(8,128)S(1)} %fusion.1.refs_0_), channel_id=1, source_target_pairs={{0,6},{1,7},{2,0},{3,1},{4,2},{5,3},{6,4},{7,5},{8,14},{9,15},{10,... | collective-permute-start | bytes 221192 | tf_op jit(solution)/shard_map/ppermute | solution.py:712
  72.7 0.7 collective-permute-start.13
  73.4 1.3 %collective-permute-start.12 = (f32[72,256]{1,0:T(8,128)S(1)}, f32[72,256]{1,0:T(8,128)S(1)}, u32[]{:S(2)}, u32[]{:S(2)}) collective-permute-start(f32[72,256]{1,0:T(8,128)S(1)} %fusion.1.refs_0_), channel_id=1, source_target_pairs={{0,2},{1,3},{2,4},{3,5},{4,6},{5,7},{6,0},{7,1},{8,10},{9,11},{10,... | collective-permute-start | bytes 221192 | tf_op jit(solution)/shard_map/ppermute | solution.py:712
  74.7 0.7 collective-permute-done.14.refs_3_
  75.4 3.7 %collective-permute-done.13.refs_2_ = f32[72,256]{1,0:T(8,128)S(1)} collective-permute-done((f32[72,256]{1,0:T(8,128)S(1)}, f32[72,256]{1,0:T(8,128)S(1)}, u32[]{:S(2)}, u32[]{:S(2)}) %collective-permute-start.13) | collective-permute-done | bytes 73760 | tf_op jit(solution)/shard_map/ppermute | solution.py:712
  79.1 0.8 collective-permute-done.12.refs_1_
  79.9 7.7 %shard_map.129 = (f32[2048,128]{1,0:T(8,128)}, f32[32,32]{1,0:T(8,128)}, f32[32,13824]{1,0:T(8,128)}) custom-call(f32[72,256]{1,0:T(8,128)S(1)} %fusion.1.refs_0_, f32[72,256]{1,0:T(8,128)S(1)} %collective-permute-done.12.refs_1_, f32[72,256]{1,0:T(8,128)S(1)} %collective-permute-done.13.refs_2_, f32[72,256]{1,0:T(8,128)S(1)} %collective-permute-done.14.refs_3_, ...), custom_call_target="tpu_custom_call" | custom-call | tf_op jit(solution)/shard_map/pallas_call | solution.py:132
  (7 shorter events, 0.1 us)
Async XLA Ops:
  0.6 3.9 %copy-start.1 = (f32[32,4,16,128]{3,2,1,0:T(8,128)S(1)}, f32[32,4,16,128]{3,2,1,0:T(8,128)}, u32[]{:S(2)}) copy-start(f32[32,4,16,128]{3,2,1,0:T(8,128)} %param.10) | copy-start | bytes 3145732
  0.6 3.9 %copy-start.4 = (f32[4,16,128]{2,1,0:T(8,128)S(1)}, f32[4,16,128]{2,1,0:T(8,128)}, u32[]{:S(2)}) copy-start(f32[4,16,128]{2,1,0:T(8,128)} %param.13) | copy-start | bytes 98308
  1.7 8.1 %collective-permute-start = (f32[32,1,16,128]{3,2,1,0:T(8,128)S(1)}, f32[32,1,16,128]{3,2,1,0:T(8,128)S(1)}, u32[]{:S(2)}, u32[]{:S(2)}) collective-permute-start(f32[32,1,16,128]{3,2,1,0:T(8,128)S(1)} %slice.16), channel_id=1, source_target_pairs={{0,8},{8,16},{16,24},{24,32},{32,40},{40,48},{48,56},{56,64},{64,7... | collective-permute-start | bytes 786440 | tf_op jit(solution)/shard_map/ppermute | solution.py:719
  7.9 7.1 %copy-start = (f32[32,13824]{1,0:T(8,128)S(1)}, f32[32,13824]{1,0:T(8,128)}, u32[]{:S(2)}) copy-start(f32[32,13824]{1,0:T(8,128)} %values.1) | copy-start | bytes 5308420
  7.9 7.1 %copy-start.2 = (f32[2,32,1152]{2,1,0:T(8,128)S(1)}, f32[2,32,1152]{2,1,0:T(8,128)}, u32[]{:S(2)}) copy-start(f32[2,32,1152]{2,1,0:T(8,128)} %constant.34.clone.refs_3_) | copy-start | bytes 884740
  7.9 7.1 %copy-start.3 = (f32[2,8,1152]{2,1,0:T(8,128)S(1)}, f32[2,8,1152]{2,1,0:T(8,128)}, u32[]{:S(2)}) copy-start(f32[2,8,1152]{2,1,0:T(8,128)} %constant.33.clone.refs_2_.rows) | copy-start | bytes 221188
  7.9 7.1 %copy-start.6 = (f32[48,128]{1,0:T(8,128)S(1)}, f32[48,128]{1,0:T(8,128)}, u32[]{:S(2)}) copy-start(f32[48,128]{1,0:T(8,128)} %constant.35.clone.refs_4_) | copy-start | bytes 73732
  7.9 7.1 %copy-start.8 = (f32[144]{0:T(256)S(1)}, f32[144]{0:T(256)}, u32[]{:S(2)}) copy-start(f32[144]{0:T(256)} %constant.32.clone.refs_1_.speeds) | copy-start | bytes 1732
  10.1 16.4 %collective-permute-start.1 = (f32[33,3,16,128]{3,2,1,0:T(8,128)S(1)}, f32[33,3,16,128]{3,2,1,0:T(8,128)S(1)}, u32[]{:S(2)}, u32[]{:S(2)}) collective-permute-start(f32[33,3,16,128]{3,2,1,0:T(8,128)S(1)} %pad_maximum_fusion), channel_id=1, source_target_pairs={{0,8},{1,121},{2,10},{3,123},{4,12},{5,125},{6,14},{7,127},{8,16},... | collective-permute-start | bytes 2433032 | tf_op jit(solution)/shard_map/ppermute | solution.py:737
  11.7 13.4 %collective-permute-start.3 = (f32[32,256]{1,0:T(8,128)S(1)}, f32[32,256]{1,0:T(8,128)S(1)}, u32[]{:S(2)}, u32[]{:S(2)}) collective-permute-start(f32[32,256]{1,0:T(8,128)S(1)} %get-tuple-element.26), channel_id=1, source_target_pairs={{8,0},{25,1},{42,2},{59,3},{76,4},{93,5},{110,6},{127,7},{0,8},{17... | collective-permute-start | bytes 98312 | tf_op jit(solution)/shard_map/ppermute | solution.py:701
  14.3 10.8 %collective-permute-start.2 = (f32[32,256]{1,0:T(8,128)S(1)}, f32[32,256]{1,0:T(8,128)S(1)}, u32[]{:S(2)}, u32[]{:S(2)}) collective-permute-start(f32[32,256]{1,0:T(8,128)S(1)} %get-tuple-element.26), channel_id=1, source_target_pairs={{0,0},{17,1},{34,2},{51,3},{68,4},{85,5},{102,6},{119,7},{8,8},{25... | collective-permute-start | bytes 98312 | tf_op jit(solution)/shard_map/ppermute | solution.py:701
  17.6 21.0 %copy-start.5 = (f32[32,896]{1,0:T(8,128)S(1)}, f32[32,896]{1,0:T(8,128)}, u32[]{:S(2)}) copy-start(f32[32,896]{1,0:T(8,128)} %constant.36.clone.refs_5_) | copy-start | bytes 344068
  17.6 21.0 %copy-start.7 = (f32[32,32]{1,0:T(8,128)S(1)}, f32[32,32]{1,0:T(8,128)}, u32[]{:S(2)}) copy-start(f32[32,32]{1,0:T(8,128)} %refs_4_.5) | copy-start | bytes 12292
  17.6 21.0 %copy-start.9 = (f32[8,128]{1,0:T(8,128)S(1)}, f32[8,128]{1,0:T(8,128)}, u32[]{:S(2)}) copy-start(f32[8,128]{1,0:T(8,128)} %constant.37.clone.refs_6_) | copy-start | bytes 12292
  25.2 1.3 %collective-permute-start.4 = (f32[64,256]{1,0:T(8,128)S(1)}, f32[64,256]{1,0:T(8,128)S(1)}, u32[]{:S(2)}, u32[]{:S(2)}) collective-permute-start(f32[64,256]{1,0:T(8,128)S(1)} %pad_maximum_fusion.2), channel_id=1, source_target_pairs={{0,1},{1,0},{2,3},{3,2},{4,5},{5,4},{6,7},{7,6},{8,9},{9,8},{10,11... | collective-permute-start | bytes 196616 | tf_op jit(solution)/shard_map/ppermute | solution.py:708
  26.5 15.9 %collective-permute-start.8 = (f32[33,3,16,128]{3,2,1,0:T(8,128)S(1)}, f32[33,3,16,128]{3,2,1,0:T(8,128)S(1)}, u32[]{:S(2)}, u32[]{:S(2)}) collective-permute-start(f32[33,3,16,128]{3,2,1,0:T(8,128)S(1)} %collective-permute-done.1), channel_id=1, source_target_pairs={{0,1},{1,0},{2,3},{3,2},{4,5},{5,4},{6,7},{7,6},{8,9},{9,8},{10,11... | collective-permute-start | bytes 2433032 | tf_op jit(solution)/shard_map/ppermute | solution.py:741
  26.8 8.4 %collective-permute-start.7 = (f32[64,256]{1,0:T(8,128)S(1)}, f32[64,256]{1,0:T(8,128)S(1)}, u32[]{:S(2)}, u32[]{:S(2)}) collective-permute-start(f32[64,256]{1,0:T(8,128)S(1)} %fusion.refs_0_), channel_id=1, source_target_pairs={{0,6},{1,7},{2,0},{3,1},{4,2},{5,3},{6,4},{7,5},{8,14},{9,15},{10,... | collective-permute-start | bytes 196616 | tf_op jit(solution)/shard_map/ppermute | solution.py:712
  31.9 6.3 %collective-permute-start.6 = (f32[64,256]{1,0:T(8,128)S(1)}, f32[64,256]{1,0:T(8,128)S(1)}, u32[]{:S(2)}, u32[]{:S(2)}) collective-permute-start(f32[64,256]{1,0:T(8,128)S(1)} %fusion.refs_0_), channel_id=1, source_target_pairs={{0,4},{1,5},{2,6},{3,7},{4,0},{5,1},{6,2},{7,3},{8,12},{9,13},{10,... | collective-permute-start | bytes 196616 | tf_op jit(solution)/shard_map/ppermute | solution.py:712
  31.9 6.7 %collective-permute-start.5 = (f32[64,256]{1,0:T(8,128)S(1)}, f32[64,256]{1,0:T(8,128)S(1)}, u32[]{:S(2)}, u32[]{:S(2)}) collective-permute-start(f32[64,256]{1,0:T(8,128)S(1)} %fusion.refs_0_), channel_id=1, source_target_pairs={{0,2},{1,3},{2,4},{3,5},{4,6},{5,7},{6,0},{7,1},{8,10},{9,11},{10,... | collective-permute-start | bytes 196616 | tf_op jit(solution)/shard_map/ppermute | solution.py:712
  53.5 13.0 %collective-permute-start.10 = (f32[32,256]{1,0:T(8,128)S(1)}, f32[32,256]{1,0:T(8,128)S(1)}, u32[]{:S(2)}, u32[]{:S(2)}) collective-permute-start(f32[32,256]{1,0:T(8,128)S(1)} %get-tuple-element.36.after), channel_id=1, source_target_pairs={{8,0},{25,1},{42,2},{59,3},{76,4},{93,5},{110,6},{127,7},{0,8},{17... | collective-permute-start | bytes 98312 | tf_op jit(solution)/shard_map/ppermute | solution.py:701
  57.8 8.7 %collective-permute-start.9 = (f32[32,256]{1,0:T(8,128)S(1)}, f32[32,256]{1,0:T(8,128)S(1)}, u32[]{:S(2)}, u32[]{:S(2)}) collective-permute-start(f32[32,256]{1,0:T(8,128)S(1)} %get-tuple-element.36.after), channel_id=1, source_target_pairs={{0,0},{17,1},{34,2},{51,3},{68,4},{85,5},{102,6},{119,7},{8,8},{25... | collective-permute-start | bytes 98312 | tf_op jit(solution)/shard_map/ppermute | solution.py:701
  66.5 3.5 %collective-permute-start.11 = (f32[72,256]{1,0:T(8,128)S(1)}, f32[72,256]{1,0:T(8,128)S(1)}, u32[]{:S(2)}, u32[]{:S(2)}) collective-permute-start(f32[72,256]{1,0:T(8,128)S(1)} %pad_maximum_fusion.1), channel_id=1, source_target_pairs={{0,1},{1,0},{2,3},{3,2},{4,5},{5,4},{6,7},{7,6},{8,9},{9,8},{10,11... | collective-permute-start | bytes 221192 | tf_op jit(solution)/shard_map/ppermute | solution.py:708
  70.1 5.3 %collective-permute-start.14 = (f32[72,256]{1,0:T(8,128)S(1)}, f32[72,256]{1,0:T(8,128)S(1)}, u32[]{:S(2)}, u32[]{:S(2)}) collective-permute-start(f32[72,256]{1,0:T(8,128)S(1)} %fusion.1.refs_0_), channel_id=1, source_target_pairs={{0,6},{1,7},{2,0},{3,1},{4,2},{5,3},{6,4},{7,5},{8,14},{9,15},{10,... | collective-permute-start | bytes 221192 | tf_op jit(solution)/shard_map/ppermute | solution.py:712
  72.7 6.4 %collective-permute-start.13 = (f32[72,256]{1,0:T(8,128)S(1)}, f32[72,256]{1,0:T(8,128)S(1)}, u32[]{:S(2)}, u32[]{:S(2)}) collective-permute-start(f32[72,256]{1,0:T(8,128)S(1)} %fusion.1.refs_0_), channel_id=1, source_target_pairs={{0,4},{1,5},{2,6},{3,7},{4,0},{5,1},{6,2},{7,3},{8,12},{9,13},{10,... | collective-permute-start | bytes 221192 | tf_op jit(solution)/shard_map/ppermute | solution.py:712
  73.4 6.5 %collective-permute-start.12 = (f32[72,256]{1,0:T(8,128)S(1)}, f32[72,256]{1,0:T(8,128)S(1)}, u32[]{:S(2)}, u32[]{:S(2)}) collective-permute-start(f32[72,256]{1,0:T(8,128)S(1)} %fusion.1.refs_0_), channel_id=1, source_target_pairs={{0,2},{1,3},{2,4},{3,5},{4,6},{5,7},{6,0},{7,1},{8,10},{9,11},{10,... | collective-permute-start | bytes 221192 | tf_op jit(solution)/shard_map/ppermute | solution.py:712

commit v6 on v5

--- a/solution.py
+++ b/solution.py
@@ -624,39 +624,49 @@
 
     w_space, w_point = wide(inverse), wide(inverse_v)
 
-    def out_space(p, carry):
-        for half in range(2):
-            size = PLANE // 2
-            at = aligned((p + 2) * PLANE + half * size, 128)
-            hi, lo = split(kinetic[:, pl.ds(at, size)])
-            made = dot(w_space, jnp.concatenate([hi, lo, hi], axis=0))
-            for y in range(NY // 2):
-                fresh_space[pl.ds(p * NY + half * (NY // 2) + y, RANK, stride=OWN * NY), :] = made[:, y * NZ : (y + 1) * NZ]
-        return carry
+    def out_space(n):
+        size = PLANE // 2
+        at = 2 * PLANE + n * size
+        hi, lo = split(kinetic[:, at : at + size])
+        made = dot(w_space, jnp.concatenate([hi, lo, hi], axis=0))
+        for y in range(NY // 2):
+            fresh_space[pl.ds(n * (NY // 2) + y, RANK, stride=OWN * NY), :] = made[:, y * NZ : (y + 1) * NZ]
+
+    def out_point(n):
+        cells = slice(n * 1536, (n + 1) * 1536)
+        hi, lo = split(spread[:, cells])
+        fresh_point[:, cells] = dot(w_point, jnp.concatenate([hi, lo, hi], axis=0))
 
     third = 2 * Q1 * HALF // 3
     copies = []
 
-    def out_point(i, carry):
-        at = aligned(i * 1536, 512)
-        hi, lo = split(spread[:, pl.ds(at, 1536)])
-        fresh_point[:, pl.ds(at, 1536)] = dot(w_point, jnp.concatenate([hi, lo, hi], axis=0))
-        return carry
-
-    for k in range(3):
-        lax.fori_loop(3 * k, 3 * k + 3, out_point, 0)
-        cells = pl.ds(k * third, third)
-        copies.append(pltpu.make_async_copy(fresh_point.at[:, cells], point_out.at[:, cells], sems.at[k + 1]))
-        copies[-1].start()
-
-    lax.fori_loop(0, OWN, out_space, 0)
-    copies.append(pltpu.make_async_copy(fresh_space, space_out, sems.at[0]))
-    copies[-1].start()
+    def outputs():
+        for k in range(3):
+            for n in range(3):
+                out_point(3 * k + n)
+                if n == 2:
+                    cells = pl.ds(k * third, third)
+                    copies.append(pltpu.make_async_copy(fresh_point.at[:, cells], point_out.at[:, cells], sems.at[k + 1]))
+                    copies[-1].start()
+                yield
+        for n in range(2 * OWN):
+            out_space(n)
+            if n == 2 * OWN - 1:
+                copies.append(pltpu.make_async_copy(fresh_space, space_out, sems.at[0]))
+                copies[-1].start()
+            yield
+
+    writing = outputs()
+
+    def write(count):
+        for _ in range(count):
+            next(writing, None)
 
     inverse_t = transposed(inverse)
     inverse_vt = transposed(inverse_v)
     turned = mm(inverse, s)
     turned_v = mm(inverse_v, q[:RANK])
+    write(4)
     aux = mm(q[RANK:, 0:32], inverse_vt)
     weights_row = aux[0:1, :]
     moments_row = aux[1:2, :] + aux[2:3, :]
@@ -665,17 +675,22 @@
         left.append(turned[:, 0:32] - turned[:, 32 * (d + 1) : 32 * (d + 2)])
     for d in range(3):
         left.append(mm_t(inverse, gram - s[:, 32 * (d + 1) : 32 * (d + 2)]))
+    half = mm(turned[:, 160:192], core[...])
+    write(3)
     stack = mm(jnp.concatenate(left, axis=0), inverse_t)
     lines = [turned_v[:, 192:224], turned_v[:, 160:192], turned_v[:, 64:96]]
     lines += [-turned_v[:, 128:160], -turned_v[:, 32:64], -turned_v[:, 96:128]]
     flux = mm(jnp.concatenate(lines, axis=0), inverse_vt)
-    current = mm_t(mm(turned[:, 160:192], core[...]), turned_v[:, 224:256])
+    current = mm_t(half, turned_v[:, 224:256])
     for _ in range(SUB):
+        write(2)
         moved = mm(stack, current)
         scaled = moved[:RANK]
         change = -scaled + jnp.sum(scaled * weights_row, axis=1, keepdims=True) * moments_row
         across = jnp.concatenate([moved[(k + 1) * RANK : (k + 2) * RANK] for k in range(6)], axis=1)
+        write(2)
         current = current + (change - mm(across, flux))
+    write(20)
     fresh_core[...] = current
     for copy in copies:
         copy.wait()

time: 88 us -> 85.7 us (0.974)
  Pallas kernels: 39.3 us -> 37 us
    pallas_call x9, Pallas kernels: 39.3 us -> 37 us  [call(): pl.pallas_call(kernel, out_shape=[jax.ShapeDtypeStruct(s, d) for s, d in...]
  transfers between devices with their start and end apart: 15 -> 15, of which waited for: 10 -> 10; matrix products, arithmetic and copies ran while one was open for 1% -> 1% of each run, Pallas kernels for 23% -> 24%
where the time goes in v6:
time: 85.7 us; the launch traced here: 85.5 us
  Pallas kernels  37 us (43%)
  starting transfers between devices  25.6 us (30%)
  waiting for transfers between devices  19.3 us (23%)
  local copies, waits for them, and re-layouts  2.31 us (3%)
  between operations  1.11 us (1%)
    pallas_call x9, Pallas kernels, call(): pl.pallas_call(kernel, out_shape=[jax.ShapeDtypeStruct(s, d) for s, d in...  37 us
    ppermute x6, starting transfers between devices, vel_parts(): parts.append(lax.ppermute(joint, 'vel', route))  11.2 us
    ppermute x6, waiting for transfers between devices, vel_parts(): parts.append(lax.ppermute(joint, 'vel', route))  10.4 us
    ppermute x4, starting transfers between devices, spread_pairs(): moved.append(lax.ppermute(space_part, ('space', 'vel'), route))  8.42 us
    ppermute x4, waiting for transfers between devices, spread_pairs(): moved.append(lax.ppermute(space_part, ('space', 'vel'), route))  4.89 us
    ppermute x2, starting transfers between devices, vel_parts(): joint = joint + lax.ppermute(joint, 'vel', pair)  2.68 us
    ppermute x2, waiting for transfers between devices, vel_parts(): joint = joint + lax.ppermute(joint, 'vel', pair)  2.15 us
    ppermute x1, waiting for transfers between devices, per_device(): lax.ppermute(space_factor[:, OWN - 1:], 'space', up).reshape(-1, NZ)  1.8 us
  transfers between devices with their start and end apart: 15, of which 10 were waited for; matrix products, arithmetic and copies ran while one was open for 1% of the time, Pallas kernels for 24%

profile of v6, /device:TPU:2, one launch (start us, length us, event | category | flops | bytes accessed | tf_op | source)
XLA Modules:
  0.0 85.5 jit_solution(14378369157457839288)
XLA Ops:
  0.6 0.0 copy-start.1
  0.6 0.0 copy-start.4
  0.7 1.1 %slice.16 = f32[32,1,16,128]{3,2,1,0:T(8,128)S(1)} slice(f32[32,4,16,128]{3,2,1,0:T(8,128)} %param.10), slice={[0:32], [3:4], [0:16], [0:128]} | slice | bytes 524288 | tf_op jit(solution)/shard_map/slice | solution.py:734
  1.7 1.6 %collective-permute-start = (f32[32,1,16,128]{3,2,1,0:T(8,128)S(1)}, f32[32,1,16,128]{3,2,1,0:T(8,128)S(1)}, u32[]{:S(2)}, u32[]{:S(2)}) collective-permute-start(f32[32,1,16,128]{3,2,1,0:T(8,128)S(1)} %slice.16), channel_id=1, source_target_pairs={{0,8},{8,16},{16,24},{24,32},{32,40},{40,48},{48,56},{56,64},{64,7... | collective-permute-start | bytes 786440 | tf_op jit(solution)/shard_map/ppermute | solution.py:734
  3.3 1.2 %slice.13 = f32[32,3,16,128]{3,2,1,0:T(8,128)S(1)} slice(f32[32,4,16,128]{3,2,1,0:T(8,128)} %param.10), slice={[0:32], [0:3], [0:16], [0:128]} | slice | bytes 1572864 | tf_op jit(solution)/shard_map/slice | solution.py:741
  4.5 0.0 copy-done.1
  4.5 0.0 copy-done.4
  4.5 3.4 %shard_map.121 = (f32[32,256]{1,0:T(8,128)S(1)}, f32[32,8192]{1,0:T(8,128)S(1)}) custom-call(f32[2048,128]{1,0:T(8,128)S(1)} %bitcast.9, f32[64,128]{1,0:T(8,128)S(1)} %bitcast.12), custom_call_target="tpu_custom_call" | custom-call | tf_op jit(solution)/shard_map/pallas_call | solution.py:132
  7.9 0.0 copy-start
  7.9 0.0 copy-start.2
  7.9 0.0 copy-start.3
  7.9 0.0 copy-start.6
  7.9 0.0 copy-start.8
  8.0 0.1 pad_maximum_fusion
  8.0 1.8 %collective-permute-done = f32[32,1,16,128]{3,2,1,0:T(8,128)S(1)} collective-permute-done((f32[32,1,16,128]{3,2,1,0:T(8,128)S(1)}, f32[32,1,16,128]{3,2,1,0:T(8,128)S(1)}, u32[]{:S(2)}, u32[]{:S(2)}) %collective-permute-start) | collective-permute-done | bytes 262176 | tf_op jit(solution)/shard_map/ppermute | solution.py:734
  9.8 0.3 shard_map.122
  10.1 1.6 %collective-permute-start.1 = (f32[33,3,16,128]{3,2,1,0:T(8,128)S(1)}, f32[33,3,16,128]{3,2,1,0:T(8,128)S(1)}, u32[]{:S(2)}, u32[]{:S(2)}) collective-permute-start(f32[33,3,16,128]{3,2,1,0:T(8,128)S(1)} %pad_maximum_fusion), channel_id=1, source_target_pairs={{0,8},{1,121},{2,10},{3,123},{4,12},{5,125},{6,14},{7,127},{8,16},... | collective-permute-start | bytes 2433032 | tf_op jit(solution)/shard_map/ppermute | solution.py:752
  11.7 2.6 %collective-permute-start.3 = (f32[32,256]{1,0:T(8,128)S(1)}, f32[32,256]{1,0:T(8,128)S(1)}, u32[]{:S(2)}, u32[]{:S(2)}) collective-permute-start(f32[32,256]{1,0:T(8,128)S(1)} %get-tuple-element.26), channel_id=1, source_target_pairs={{8,0},{25,1},{42,2},{59,3},{76,4},{93,5},{110,6},{127,7},{0,8},{17... | collective-permute-start | bytes 98312 | tf_op jit(solution)/shard_map/ppermute | solution.py:716
  14.3 0.7 collective-permute-start.2
  15.0 0.0 copy-done
  15.0 0.0 copy-done.2
  15.0 0.0 copy-done.3
  15.0 0.0 copy-done.6
  15.0 0.0 copy-done.8
  15.0 2.6 %shard_map.123.refs_6_ = f32[32,256]{1,0:T(8,128)S(1)} custom-call(s32[1]{0:T(128)} %bitcast.4.refs_0_.v_ref, f32[144]{0:T(256)S(1)} %copy-done.8, f32[2,8,1152]{2,1,0:T(8,128)S(1)} %copy-done.3, f32[2,32,1152]{2,1,0:T(8,128)S(1)} %copy-done.2, f32[48,128]{1,0:T(8,128)S(1)} %copy-done.6, f32[32,13824]{1,0:T(8,128)S(1)} %copy-done, ...), custom_call_target="tpu_custom_call" | custom-call | tf_op jit(solution)/shard_map/pallas_call | solution.py:132
  17.6 0.0 copy-start.5
  17.6 0.0 copy-start.7
  17.6 0.0 copy-start.9
  17.7 2.6 %shard_map.124 = f32[32,256]{1,0:T(8,128)S(1)} custom-call(s32[1]{0:T(128)} %bitcast.4.refs_0_.v_ref, f32[144]{0:T(256)S(1)} %copy-done.8, f32[2,8,1152]{2,1,0:T(8,128)S(1)} %copy-done.3, f32[2,32,1152]{2,1,0:T(8,128)S(1)} %copy-done.2, f32[48,128]{1,0:T(8,128)S(1)} %copy-done.6, f32[32,13824]{1,0:T(8,128)S(1)} %copy-done, f32[32,256]{1,0:T(8,128)S(1)} %shard_map.123.refs_6_), custom_call_target="tpu_custom_call" | custom-call | tf_op jit(solution)/shard_map/pallas_call | solution.py:132
  20.3 4.9 %collective-permute-done.3 = f32[32,256]{1,0:T(8,128)S(1)} collective-permute-done((f32[32,256]{1,0:T(8,128)S(1)}, f32[32,256]{1,0:T(8,128)S(1)}, u32[]{:S(2)}, u32[]{:S(2)}) %collective-permute-start.3) | collective-permute-done | bytes 32800 | tf_op jit(solution)/shard_map/ppermute | solution.py:716
  25.1 0.0 collective-permute-done.2
  25.2 0.1 collective-permute-start.4
  25.3 1.2 %collective-permute-done.4 = f32[64,256]{1,0:T(8,128)S(1)} collective-permute-done((f32[64,256]{1,0:T(8,128)S(1)}, f32[64,256]{1,0:T(8,128)S(1)}, u32[]{:S(2)}, u32[]{:S(2)}) %collective-permute-start.4) | collective-permute-done | bytes 65568 | tf_op jit(solution)/shard_map/ppermute | solution.py:723
  26.5 0.0 collective-permute-done.1
  26.5 0.2 collective-permute-start.8
  26.8 5.1 %collective-permute-start.7 = (f32[64,256]{1,0:T(8,128)S(1)}, f32[64,256]{1,0:T(8,128)S(1)}, u32[]{:S(2)}, u32[]{:S(2)}) collective-permute-start(f32[64,256]{1,0:T(8,128)S(1)} %fusion.refs_0_), channel_id=1, source_target_pairs={{0,6},{1,7},{2,0},{3,1},{4,2},{5,3},{6,4},{7,5},{8,14},{9,15},{10,... | collective-permute-start | bytes 196616 | tf_op jit(solution)/shard_map/ppermute | solution.py:727
  31.9 0.0 collective-permute-start.6
  31.9 1.4 %collective-permute-start.5 = (f32[64,256]{1,0:T(8,128)S(1)}, f32[64,256]{1,0:T(8,128)S(1)}, u32[]{:S(2)}, u32[]{:S(2)}) collective-permute-start(f32[64,256]{1,0:T(8,128)S(1)} %fusion.refs_0_), channel_id=1, source_target_pairs={{0,2},{1,3},{2,4},{3,5},{4,6},{5,7},{6,0},{7,1},{8,10},{9,11},{10,... | collective-permute-start | bytes 196616 | tf_op jit(solution)/shard_map/ppermute | solution.py:727
  33.3 1.9 %collective-permute-done.7.refs_3_ = f32[64,256]{1,0:T(8,128)S(1)} collective-permute-done((f32[64,256]{1,0:T(8,128)S(1)}, f32[64,256]{1,0:T(8,128)S(1)}, u32[]{:S(2)}, u32[]{:S(2)}) %collective-permute-start.7) | collective-permute-done | bytes 65568 | tf_op jit(solution)/shard_map/ppermute | solution.py:727
  35.2 3.0 %collective-permute-done.6.refs_2_ = f32[64,256]{1,0:T(8,128)S(1)} collective-permute-done((f32[64,256]{1,0:T(8,128)S(1)}, f32[64,256]{1,0:T(8,128)S(1)}, u32[]{:S(2)}, u32[]{:S(2)}) %collective-permute-start.6) | collective-permute-done | bytes 65568 | tf_op jit(solution)/shard_map/ppermute | solution.py:727
  38.2 0.4 collective-permute-done.5.refs_1_
  38.6 0.0 copy-done.5
  38.6 0.0 copy-done.7
  38.6 0.0 copy-done.9
  38.6 3.8 %shard_map.125 = (f32[2,240,128]{2,1,0:T(8,128)S(1)}, f32[2,224,128]{2,1,0:T(8,128)S(1)}, f32[3,32,128]{2,1,0:T(8,128)S(1)}, f32[32,128]{1,0:T(8,128)S(1)}) custom-call(f32[64,256]{1,0:T(8,128)S(1)} %fusion.refs_0_, f32[64,256]{1,0:T(8,128)S(1)} %collective-permute-done.5.refs_1_, f32[64,256]{1,0:T(8,128)S(1)} %collective-permute-done.6.refs_2_, ...), custom_call_target="tpu_custom_call" | custom-call | tf_op jit(solution)/shard_map/pallas_call | solution.py:132
  42.4 0.0 collective-permute-done.8
  42.4 0.6 shard_map.126
  43.0 10.5 %shard_map.127 = (f32[32,12288]{1,0:T(8,128)S(1)}, f32[32,256]{1,0:T(8,128)S(1)}) custom-call(f32[2,240,128]{2,1,0:T(8,128)S(1)} %get-tuple-element.29.wk, f32[32,128]{1,0:T(8,128)S(1)} %get-tuple-element.30.after.moment, f32[32,22528]{1,0:T(8,128)S(1)} %get-tuple-element.33.raw, f32[64,128]{1,0:T(8,128)S(1)} %bitcast.13, ...), custom_call_target="tpu_custom_call" | custom-call | tf_op jit(solution)/shard_map/pallas_call | solution.py:132
  53.5 4.3 %collective-permute-start.10 = (f32[32,256]{1,0:T(8,128)S(1)}, f32[32,256]{1,0:T(8,128)S(1)}, u32[]{:S(2)}, u32[]{:S(2)}) collective-permute-start(f32[32,256]{1,0:T(8,128)S(1)} %get-tuple-element.36.after), channel_id=1, source_target_pairs={{8,0},{25,1},{42,2},{59,3},{76,4},{93,5},{110,6},{127,7},{0,8},{17... | collective-permute-start | bytes 98312 | tf_op jit(solution)/shard_map/ppermute | solution.py:716
  57.8 0.9 %collective-permute-start.9 = (f32[32,256]{1,0:T(8,128)S(1)}, f32[32,256]{1,0:T(8,128)S(1)}, u32[]{:S(2)}, u32[]{:S(2)}) collective-permute-start(f32[32,256]{1,0:T(8,128)S(1)} %get-tuple-element.36.after), channel_id=1, source_target_pairs={{0,0},{17,1},{34,2},{51,3},{68,4},{85,5},{102,6},{119,7},{8,8},{25... | collective-permute-start | bytes 98312 | tf_op jit(solution)/shard_map/ppermute | solution.py:716
  58.7 7.8 %shard_map.128 = (f32[32,13824]{1,0:T(8,128)S(1)}, f32[40,256]{1,0:T(8,128)S(1)}) custom-call(s32[1]{0:T(128)} %bitcast.4.refs_0_.v_ref, f32[144]{0:T(256)S(1)} %copy-done.8, f32[2,8,1152]{2,1,0:T(8,128)S(1)} %copy-done.3, f32[2,224,128]{2,1,0:T(8,128)S(1)} %get-tuple-element.37.wl, f32[3,32,128]{2,1,0:T(8,128)S(1)} %get-tuple-element.38.src, ...), custom_call_target="tpu_custom_call" | custom-call | tf_op jit(solution)/shard_map/pallas_call | solution.py:132
  66.5 0.0 collective-permute-done.10
  66.5 0.0 collective-permute-done.9
  66.5 2.6 %collective-permute-start.11 = (f32[72,256]{1,0:T(8,128)S(1)}, f32[72,256]{1,0:T(8,128)S(1)}, u32[]{:S(2)}, u32[]{:S(2)}) collective-permute-start(f32[72,256]{1,0:T(8,128)S(1)} %pad_maximum_fusion.1), channel_id=1, source_target_pairs={{0,1},{1,0},{2,3},{3,2},{4,5},{5,4},{6,7},{7,6},{8,9},{9,8},{10,11... | collective-permute-start | bytes 221192 | tf_op jit(solution)/shard_map/ppermute | solution.py:723
  69.1 0.9 %collective-permute-done.11 = f32[72,256]{1,0:T(8,128)S(1)} collective-permute-done((f32[72,256]{1,0:T(8,128)S(1)}, f32[72,256]{1,0:T(8,128)S(1)}, u32[]{:S(2)}, u32[]{:S(2)}) %collective-permute-start.11) | collective-permute-done | bytes 73760 | tf_op jit(solution)/shard_map/ppermute | solution.py:723
  70.1 2.6 %collective-permute-start.14 = (f32[72,256]{1,0:T(8,128)S(1)}, f32[72,256]{1,0:T(8,128)S(1)}, u32[]{:S(2)}, u32[]{:S(2)}) collective-permute-start(f32[72,256]{1,0:T(8,128)S(1)} %fusion.1.refs_0_), channel_id=1, source_target_pairs={{0,6},{1,7},{2,0},{3,1},{4,2},{5,3},{6,4},{7,5},{8,14},{9,15},{10,... | collective-permute-start | bytes 221192 | tf_op jit(solution)/shard_map/ppermute | solution.py:727
  72.7 0.7 collective-permute-start.13
  73.4 1.3 %collective-permute-start.12 = (f32[72,256]{1,0:T(8,128)S(1)}, f32[72,256]{1,0:T(8,128)S(1)}, u32[]{:S(2)}, u32[]{:S(2)}) collective-permute-start(f32[72,256]{1,0:T(8,128)S(1)} %fusion.1.refs_0_), channel_id=1, source_target_pairs={{0,2},{1,3},{2,4},{3,5},{4,6},{5,7},{6,0},{7,1},{8,10},{9,11},{10,... | collective-permute-start | bytes 221192 | tf_op jit(solution)/shard_map/ppermute | solution.py:727
  74.7 0.7 collective-permute-done.14.refs_3_
  75.4 3.7 %collective-permute-done.13.refs_2_ = f32[72,256]{1,0:T(8,128)S(1)} collective-permute-done((f32[72,256]{1,0:T(8,128)S(1)}, f32[72,256]{1,0:T(8,128)S(1)}, u32[]{:S(2)}, u32[]{:S(2)}) %collective-permute-start.13) | collective-permute-done | bytes 73760 | tf_op jit(solution)/shard_map/ppermute | solution.py:727
  79.1 0.8 collective-permute-done.12.refs_1_
  79.9 5.5 %shard_map.129 = (f32[2048,128]{1,0:T(8,128)}, f32[32,32]{1,0:T(8,128)}, f32[32,13824]{1,0:T(8,128)}) custom-call(f32[72,256]{1,0:T(8,128)S(1)} %fusion.1.refs_0_, f32[72,256]{1,0:T(8,128)S(1)} %collective-permute-done.12.refs_1_, f32[72,256]{1,0:T(8,128)S(1)} %collective-permute-done.13.refs_2_, f32[72,256]{1,0:T(8,128)S(1)} %collective-permute-done.14.refs_3_, ...), custom_call_target="tpu_custom_call" | custom-call | tf_op jit(solution)/shard_map/pallas_call | solution.py:132
  (7 shorter events, 0.1 us)
Async XLA Ops:
  0.6 3.9 %copy-start.1 = (f32[32,4,16,128]{3,2,1,0:T(8,128)S(1)}, f32[32,4,16,128]{3,2,1,0:T(8,128)}, u32[]{:S(2)}) copy-start(f32[32,4,16,128]{3,2,1,0:T(8,128)} %param.10) | copy-start | bytes 3145732
  0.6 3.9 %copy-start.4 = (f32[4,16,128]{2,1,0:T(8,128)S(1)}, f32[4,16,128]{2,1,0:T(8,128)}, u32[]{:S(2)}) copy-start(f32[4,16,128]{2,1,0:T(8,128)} %param.13) | copy-start | bytes 98308
  1.7 8.1 %collective-permute-start = (f32[32,1,16,128]{3,2,1,0:T(8,128)S(1)}, f32[32,1,16,128]{3,2,1,0:T(8,128)S(1)}, u32[]{:S(2)}, u32[]{:S(2)}) collective-permute-start(f32[32,1,16,128]{3,2,1,0:T(8,128)S(1)} %slice.16), channel_id=1, source_target_pairs={{0,8},{8,16},{16,24},{24,32},{32,40},{40,48},{48,56},{56,64},{64,7... | collective-permute-start | bytes 786440 | tf_op jit(solution)/shard_map/ppermute | solution.py:734
  7.9 7.1 %copy-start = (f32[32,13824]{1,0:T(8,128)S(1)}, f32[32,13824]{1,0:T(8,128)}, u32[]{:S(2)}) copy-start(f32[32,13824]{1,0:T(8,128)} %values.1) | copy-start | bytes 5308420
  7.9 7.1 %copy-start.2 = (f32[2,32,1152]{2,1,0:T(8,128)S(1)}, f32[2,32,1152]{2,1,0:T(8,128)}, u32[]{:S(2)}) copy-start(f32[2,32,1152]{2,1,0:T(8,128)} %constant.34.clone.refs_3_) | copy-start | bytes 884740
  7.9 7.1 %copy-start.3 = (f32[2,8,1152]{2,1,0:T(8,128)S(1)}, f32[2,8,1152]{2,1,0:T(8,128)}, u32[]{:S(2)}) copy-start(f32[2,8,1152]{2,1,0:T(8,128)} %constant.33.clone.refs_2_.rows) | copy-start | bytes 221188
  7.9 7.1 %copy-start.6 = (f32[48,128]{1,0:T(8,128)S(1)}, f32[48,128]{1,0:T(8,128)}, u32[]{:S(2)}) copy-start(f32[48,128]{1,0:T(8,128)} %constant.35.clone.refs_4_) | copy-start | bytes 73732
  7.9 7.1 %copy-start.8 = (f32[144]{0:T(256)S(1)}, f32[144]{0:T(256)}, u32[]{:S(2)}) copy-start(f32[144]{0:T(256)} %constant.32.clone.refs_1_.speeds) | copy-start | bytes 1732
  10.1 16.4 %collective-permute-start.1 = (f32[33,3,16,128]{3,2,1,0:T(8,128)S(1)}, f32[33,3,16,128]{3,2,1,0:T(8,128)S(1)}, u32[]{:S(2)}, u32[]{:S(2)}) collective-permute-start(f32[33,3,16,128]{3,2,1,0:T(8,128)S(1)} %pad_maximum_fusion), channel_id=1, source_target_pairs={{0,8},{1,121},{2,10},{3,123},{4,12},{5,125},{6,14},{7,127},{8,16},... | collective-permute-start | bytes 2433032 | tf_op jit(solution)/shard_map/ppermute | solution.py:752
  11.7 13.4 %collective-permute-start.3 = (f32[32,256]{1,0:T(8,128)S(1)}, f32[32,256]{1,0:T(8,128)S(1)}, u32[]{:S(2)}, u32[]{:S(2)}) collective-permute-start(f32[32,256]{1,0:T(8,128)S(1)} %get-tuple-element.26), channel_id=1, source_target_pairs={{8,0},{25,1},{42,2},{59,3},{76,4},{93,5},{110,6},{127,7},{0,8},{17... | collective-permute-start | bytes 98312 | tf_op jit(solution)/shard_map/ppermute | solution.py:716
  14.3 10.8 %collective-permute-start.2 = (f32[32,256]{1,0:T(8,128)S(1)}, f32[32,256]{1,0:T(8,128)S(1)}, u32[]{:S(2)}, u32[]{:S(2)}) collective-permute-start(f32[32,256]{1,0:T(8,128)S(1)} %get-tuple-element.26), channel_id=1, source_target_pairs={{0,0},{17,1},{34,2},{51,3},{68,4},{85,5},{102,6},{119,7},{8,8},{25... | collective-permute-start | bytes 98312 | tf_op jit(solution)/shard_map/ppermute | solution.py:716
  17.6 21.0 %copy-start.5 = (f32[32,896]{1,0:T(8,128)S(1)}, f32[32,896]{1,0:T(8,128)}, u32[]{:S(2)}) copy-start(f32[32,896]{1,0:T(8,128)} %constant.36.clone.refs_5_) | copy-start | bytes 344068
  17.6 21.0 %copy-start.7 = (f32[32,32]{1,0:T(8,128)S(1)}, f32[32,32]{1,0:T(8,128)}, u32[]{:S(2)}) copy-start(f32[32,32]{1,0:T(8,128)} %refs_4_.5) | copy-start | bytes 12292
  17.6 21.0 %copy-start.9 = (f32[8,128]{1,0:T(8,128)S(1)}, f32[8,128]{1,0:T(8,128)}, u32[]{:S(2)}) copy-start(f32[8,128]{1,0:T(8,128)} %constant.37.clone.refs_6_) | copy-start | bytes 12292
  25.2 1.3 %collective-permute-start.4 = (f32[64,256]{1,0:T(8,128)S(1)}, f32[64,256]{1,0:T(8,128)S(1)}, u32[]{:S(2)}, u32[]{:S(2)}) collective-permute-start(f32[64,256]{1,0:T(8,128)S(1)} %pad_maximum_fusion.2), channel_id=1, source_target_pairs={{0,1},{1,0},{2,3},{3,2},{4,5},{5,4},{6,7},{7,6},{8,9},{9,8},{10,11... | collective-permute-start | bytes 196616 | tf_op jit(solution)/shard_map/ppermute | solution.py:723
  26.5 15.9 %collective-permute-start.8 = (f32[33,3,16,128]{3,2,1,0:T(8,128)S(1)}, f32[33,3,16,128]{3,2,1,0:T(8,128)S(1)}, u32[]{:S(2)}, u32[]{:S(2)}) collective-permute-start(f32[33,3,16,128]{3,2,1,0:T(8,128)S(1)} %collective-permute-done.1), channel_id=1, source_target_pairs={{0,1},{1,0},{2,3},{3,2},{4,5},{5,4},{6,7},{7,6},{8,9},{9,8},{10,11... | collective-permute-start | bytes 2433032 | tf_op jit(solution)/shard_map/ppermute | solution.py:756
  26.8 8.4 %collective-permute-start.7 = (f32[64,256]{1,0:T(8,128)S(1)}, f32[64,256]{1,0:T(8,128)S(1)}, u32[]{:S(2)}, u32[]{:S(2)}) collective-permute-start(f32[64,256]{1,0:T(8,128)S(1)} %fusion.refs_0_), channel_id=1, source_target_pairs={{0,6},{1,7},{2,0},{3,1},{4,2},{5,3},{6,4},{7,5},{8,14},{9,15},{10,... | collective-permute-start | bytes 196616 | tf_op jit(solution)/shard_map/ppermute | solution.py:727
  31.9 6.3 %collective-permute-start.6 = (f32[64,256]{1,0:T(8,128)S(1)}, f32[64,256]{1,0:T(8,128)S(1)}, u32[]{:S(2)}, u32[]{:S(2)}) collective-permute-start(f32[64,256]{1,0:T(8,128)S(1)} %fusion.refs_0_), channel_id=1, source_target_pairs={{0,4},{1,5},{2,6},{3,7},{4,0},{5,1},{6,2},{7,3},{8,12},{9,13},{10,... | collective-permute-start | bytes 196616 | tf_op jit(solution)/shard_map/ppermute | solution.py:727
  31.9 6.7 %collective-permute-start.5 = (f32[64,256]{1,0:T(8,128)S(1)}, f32[64,256]{1,0:T(8,128)S(1)}, u32[]{:S(2)}, u32[]{:S(2)}) collective-permute-start(f32[64,256]{1,0:T(8,128)S(1)} %fusion.refs_0_), channel_id=1, source_target_pairs={{0,2},{1,3},{2,4},{3,5},{4,6},{5,7},{6,0},{7,1},{8,10},{9,11},{10,... | collective-permute-start | bytes 196616 | tf_op jit(solution)/shard_map/ppermute | solution.py:727
  53.5 13.0 %collective-permute-start.10 = (f32[32,256]{1,0:T(8,128)S(1)}, f32[32,256]{1,0:T(8,128)S(1)}, u32[]{:S(2)}, u32[]{:S(2)}) collective-permute-start(f32[32,256]{1,0:T(8,128)S(1)} %get-tuple-element.36.after), channel_id=1, source_target_pairs={{8,0},{25,1},{42,2},{59,3},{76,4},{93,5},{110,6},{127,7},{0,8},{17... | collective-permute-start | bytes 98312 | tf_op jit(solution)/shard_map/ppermute | solution.py:716
  57.8 8.7 %collective-permute-start.9 = (f32[32,256]{1,0:T(8,128)S(1)}, f32[32,256]{1,0:T(8,128)S(1)}, u32[]{:S(2)}, u32[]{:S(2)}) collective-permute-start(f32[32,256]{1,0:T(8,128)S(1)} %get-tuple-element.36.after), channel_id=1, source_target_pairs={{0,0},{17,1},{34,2},{51,3},{68,4},{85,5},{102,6},{119,7},{8,8},{25... | collective-permute-start | bytes 98312 | tf_op jit(solution)/shard_map/ppermute | solution.py:716
  66.5 3.5 %collective-permute-start.11 = (f32[72,256]{1,0:T(8,128)S(1)}, f32[72,256]{1,0:T(8,128)S(1)}, u32[]{:S(2)}, u32[]{:S(2)}) collective-permute-start(f32[72,256]{1,0:T(8,128)S(1)} %pad_maximum_fusion.1), channel_id=1, source_target_pairs={{0,1},{1,0},{2,3},{3,2},{4,5},{5,4},{6,7},{7,6},{8,9},{9,8},{10,11... | collective-permute-start | bytes 221192 | tf_op jit(solution)/shard_map/ppermute | solution.py:723
  70.1 5.3 %collective-permute-start.14 = (f32[72,256]{1,0:T(8,128)S(1)}, f32[72,256]{1,0:T(8,128)S(1)}, u32[]{:S(2)}, u32[]{:S(2)}) collective-permute-start(f32[72,256]{1,0:T(8,128)S(1)} %fusion.1.refs_0_), channel_id=1, source_target_pairs={{0,6},{1,7},{2,0},{3,1},{4,2},{5,3},{6,4},{7,5},{8,14},{9,15},{10,... | collective-permute-start | bytes 221192 | tf_op jit(solution)/shard_map/ppermute | solution.py:727
  72.7 6.4 %collective-permute-start.13 = (f32[72,256]{1,0:T(8,128)S(1)}, f32[72,256]{1,0:T(8,128)S(1)}, u32[]{:S(2)}, u32[]{:S(2)}) collective-permute-start(f32[72,256]{1,0:T(8,128)S(1)} %fusion.1.refs_0_), channel_id=1, source_target_pairs={{0,4},{1,5},{2,6},{3,7},{4,0},{5,1},{6,2},{7,3},{8,12},{9,13},{10,... | collective-permute-start | bytes 221192 | tf_op jit(solution)/shard_map/ppermute | solution.py:727
  73.4 6.5 %collective-permute-start.12 = (f32[72,256]{1,0:T(8,128)S(1)}, f32[72,256]{1,0:T(8,128)S(1)}, u32[]{:S(2)}, u32[]{:S(2)}) collective-permute-start(f32[72,256]{1,0:T(8,128)S(1)} %fusion.1.refs_0_), channel_id=1, source_target_pairs={{0,2},{1,3},{2,4},{3,5},{4,6},{5,7},{6,0},{7,1},{8,10},{9,11},{10,... | collective-permute-start | bytes 221192 | tf_op jit(solution)/shard_map/ppermute | solution.py:727

commit v7 on v6

--- a/solution.py
+++ b/solution.py
@@ -534,20 +534,31 @@
             bases, ups, downs = [], [], []
             for j in range(NY // 2):
                 cells, operand = tile(t, j)
-                mixed = dot(w, operand)
+                cut = skip + 2 * RANK
+                mixed = dot(jnp.concatenate([w[skip + 6 * RANK :], w[:cut]], axis=0), operand)
                 for i in range(2):
                     y = 2 * j + i
                     cell = slice(y * NZ, (y + 1) * NZ)
                     half = slice(i * NZ, (i + 1) * NZ)
-                    part = [mixed[skip + k * RANK : skip + (k + 1) * RANK, half] for k in range(6)]
-                    here = mixed[:RANK, half] if skip else cells[:, half]
-                    density = mixed[skip + 6 * RANK : skip + 6 * RANK + 1, half]
-                    put(t - 1, y, partial[:, cell] + part[1])
+                    up, down = mixed[16 + skip : 16 + skip + RANK, half], mixed[16 + skip + RANK :, half]
+                    here = mixed[16 : 16 + RANK, half] if skip else cells[:, half]
+                    density = mixed[:1, half]
+                    put(t - 1, y, partial[:, cell] + down)
                     rate = rates_all[pl.ds((t - 1) * NY + y, 1), :]
-                    base = here + rate * (scale * density - here) + passed[:, cell]
-                    passed[:, cell] = part[0]
-                    base = base - ((part[0] + part[1]) + (part[2] + part[3]) + (part[4] + part[5]))
-                    bases.append(base + roll_lanes(part[4], 1) + roll_lanes(part[5], -1))
+                    bases.append(here + rate * (scale * density - here) + passed[:, cell] - (up + down))
+                    passed[:, cell] = up
+                mixed = dot(w[cut + 2 * RANK : cut + 4 * RANK], operand)
+                for i in range(2):
+                    y = 2 * j + i
+                    half = slice(i * NZ, (i + 1) * NZ)
+                    up, down = mixed[:RANK, half], mixed[RANK:, half]
+                    bases[y] = bases[y] - (up + down) + roll_lanes(up, 1) + roll_lanes(down, -1)
+                mixed = dot(w[cut : cut + 2 * RANK], operand)
+                for i in range(2):
+                    y = 2 * j + i
+                    half = slice(i * NZ, (i + 1) * NZ)
+                    part = [None, None] + [mixed[k * RANK : (k + 1) * RANK, half] for k in range(2)]
+                    bases[y] = bases[y] - (part[2] + part[3])
                     ups.append(part[2])
                     downs.append(part[3])
                     if y >= 2:
@@ -745,12 +756,12 @@
     pair = [(w, w ^ 1) for w in range(8)]
 
     inner, own = space_sums(values, rates)
-    point = point_sums(v, velocity_factor, 0, Q1 // 2, inner)
+    point = point_sums(v, velocity_factor, 0, 4, inner)
     space, edge = edge_sums(own, below1, inner)
     moved = spread_pairs(space)
     halo, space = lax.optimization_barrier((halo, space))
     mine = lax.ppermute(halo, ("space", "vel"), route)
-    point = point_sums(v, velocity_factor, Q1 // 2, Q1, point)
+    point = point_sums(v, velocity_factor, 4, Q1, point)
     parts = vel_parts(moved, point)
     mine, parts[0] = lax.optimization_barrier((mine, parts[0]))
     other = lax.ppermute(mine, "vel", pair)

time: 85.7 us -> 82.4 us (0.961)
  Pallas kernels: 37 us -> 34 us
    pallas_call x9, Pallas kernels: 37 us -> 34 us  [call(): pl.pallas_call(kernel, out_shape=[jax.ShapeDtypeStruct(s, d) for s, d in...]
  transfers between devices with their start and end apart: 15 -> 15, of which waited for: 10 -> 10; matrix products, arithmetic and copies ran while one was open for 1% -> 2% of each run, Pallas kernels for 24% -> 25%
where the time goes in v7:
time: 82.4 us; the launch traced here: 82.2 us
  Pallas kernels  34 us (41%)
  starting transfers between devices  25.5 us (31%)
  waiting for transfers between devices  19.3 us (23%)
  local copies, waits for them, and re-layouts  2.31 us (3%)
  between operations  1.1 us (1%)
    pallas_call x9, Pallas kernels, call(): pl.pallas_call(kernel, out_shape=[jax.ShapeDtypeStruct(s, d) for s, d in...  34 us
    ppermute x6, starting transfers between devices, vel_parts(): parts.append(lax.ppermute(joint, 'vel', route))  11.2 us
    ppermute x6, waiting for transfers between devices, vel_parts(): parts.append(lax.ppermute(joint, 'vel', route))  10.4 us
    ppermute x4, starting transfers between devices, spread_pairs(): moved.append(lax.ppermute(space_part, ('space', 'vel'), route))  8.25 us
    ppermute x4, waiting for transfers between devices, spread_pairs(): moved.append(lax.ppermute(space_part, ('space', 'vel'), route))  4.89 us
    ppermute x2, starting transfers between devices, vel_parts(): joint = joint + lax.ppermute(joint, 'vel', pair)  2.68 us
    ppermute x2, waiting for transfers between devices, vel_parts(): joint = joint + lax.ppermute(joint, 'vel', pair)  2.15 us
    ppermute x1, waiting for transfers between devices, per_device(): lax.ppermute(space_factor[:, OWN - 1:], 'space', up).reshape(-1, NZ)  1.8 us
  transfers between devices with their start and end apart: 15, of which 10 were waited for; matrix products, arithmetic and copies ran while one was open for 2% of the time, Pallas kernels for 25%

profile of v7, /device:TPU:2, one launch (start us, length us, event | category | flops | bytes accessed | tf_op | source)
XLA Modules:
  0.0 82.2 jit_solution(18251888272060135016)
XLA Ops:
  0.6 0.0 copy-start.1
  0.6 0.0 copy-start.4
  0.7 1.1 %slice.16 = f32[32,1,16,128]{3,2,1,0:T(8,128)S(1)} slice(f32[32,4,16,128]{3,2,1,0:T(8,128)} %param.10), slice={[0:32], [3:4], [0:16], [0:128]} | slice | bytes 524288 | tf_op jit(solution)/shard_map/slice | solution.py:745
  1.7 1.6 %collective-permute-start = (f32[32,1,16,128]{3,2,1,0:T(8,128)S(1)}, f32[32,1,16,128]{3,2,1,0:T(8,128)S(1)}, u32[]{:S(2)}, u32[]{:S(2)}) collective-permute-start(f32[32,1,16,128]{3,2,1,0:T(8,128)S(1)} %slice.16), channel_id=1, source_target_pairs={{0,8},{8,16},{16,24},{24,32},{32,40},{40,48},{48,56},{56,64},{64,7... | collective-permute-start | bytes 786440 | tf_op jit(solution)/shard_map/ppermute | solution.py:745
  3.3 1.2 %slice.13 = f32[32,3,16,128]{3,2,1,0:T(8,128)S(1)} slice(f32[32,4,16,128]{3,2,1,0:T(8,128)} %param.10), slice={[0:32], [0:3], [0:16], [0:128]} | slice | bytes 1572864 | tf_op jit(solution)/shard_map/slice | solution.py:752
  4.5 0.0 copy-done.1
  4.5 0.0 copy-done.4
  4.5 3.4 %shard_map.121 = (f32[32,256]{1,0:T(8,128)S(1)}, f32[32,8192]{1,0:T(8,128)S(1)}) custom-call(f32[2048,128]{1,0:T(8,128)S(1)} %bitcast.9, f32[64,128]{1,0:T(8,128)S(1)} %bitcast.12), custom_call_target="tpu_custom_call" | custom-call | tf_op jit(solution)/shard_map/pallas_call | solution.py:132
  7.9 0.0 copy-start
  7.9 0.0 copy-start.2
  7.9 0.0 copy-start.3
  7.9 0.0 copy-start.6
  7.9 0.0 copy-start.8
  8.0 0.1 pad_maximum_fusion
  8.0 1.8 %collective-permute-done = f32[32,1,16,128]{3,2,1,0:T(8,128)S(1)} collective-permute-done((f32[32,1,16,128]{3,2,1,0:T(8,128)S(1)}, f32[32,1,16,128]{3,2,1,0:T(8,128)S(1)}, u32[]{:S(2)}, u32[]{:S(2)}) %collective-permute-start) | collective-permute-done | bytes 262176 | tf_op jit(solution)/shard_map/ppermute | solution.py:745
  9.8 0.3 shard_map.122
  10.1 1.6 %collective-permute-start.1 = (f32[33,3,16,128]{3,2,1,0:T(8,128)S(1)}, f32[33,3,16,128]{3,2,1,0:T(8,128)S(1)}, u32[]{:S(2)}, u32[]{:S(2)}) collective-permute-start(f32[33,3,16,128]{3,2,1,0:T(8,128)S(1)} %pad_maximum_fusion), channel_id=1, source_target_pairs={{0,8},{1,121},{2,10},{3,123},{4,12},{5,125},{6,14},{7,127},{8,16},... | collective-permute-start | bytes 2433032 | tf_op jit(solution)/shard_map/ppermute | solution.py:763
  11.7 2.6 %collective-permute-start.3 = (f32[32,256]{1,0:T(8,128)S(1)}, f32[32,256]{1,0:T(8,128)S(1)}, u32[]{:S(2)}, u32[]{:S(2)}) collective-permute-start(f32[32,256]{1,0:T(8,128)S(1)} %get-tuple-element.26), channel_id=1, source_target_pairs={{8,0},{25,1},{42,2},{59,3},{76,4},{93,5},{110,6},{127,7},{0,8},{17... | collective-permute-start | bytes 98312 | tf_op jit(solution)/shard_map/ppermute | solution.py:727
  14.3 0.7 collective-permute-start.2
  15.0 0.0 copy-done
  15.0 0.0 copy-done.2
  15.0 0.0 copy-done.3
  15.0 0.0 copy-done.6
  15.0 0.0 copy-done.8
  15.0 3.3 %shard_map.123.refs_6_ = f32[32,256]{1,0:T(8,128)S(1)} custom-call(s32[1]{0:T(128)} %bitcast.4.refs_0_.v_ref, f32[144]{0:T(256)S(1)} %copy-done.8, f32[2,8,1152]{2,1,0:T(8,128)S(1)} %copy-done.3, f32[2,32,1152]{2,1,0:T(8,128)S(1)} %copy-done.2, f32[48,128]{1,0:T(8,128)S(1)} %copy-done.6, f32[32,13824]{1,0:T(8,128)S(1)} %copy-done, ...), custom_call_target="tpu_custom_call" | custom-call | tf_op jit(solution)/shard_map/pallas_call | solution.py:132
  18.3 0.0 copy-start.5
  18.3 0.0 copy-start.7
  18.3 0.0 copy-start.9
  18.3 2.0 %shard_map.124 = f32[32,256]{1,0:T(8,128)S(1)} custom-call(s32[1]{0:T(128)} %bitcast.4.refs_0_.v_ref, f32[144]{0:T(256)S(1)} %copy-done.8, f32[2,8,1152]{2,1,0:T(8,128)S(1)} %copy-done.3, f32[2,32,1152]{2,1,0:T(8,128)S(1)} %copy-done.2, f32[48,128]{1,0:T(8,128)S(1)} %copy-done.6, f32[32,13824]{1,0:T(8,128)S(1)} %copy-done, f32[32,256]{1,0:T(8,128)S(1)} %shard_map.123.refs_6_), custom_call_target="tpu_custom_call" | custom-call | tf_op jit(solution)/shard_map/pallas_call | solution.py:132
  20.3 4.9 %collective-permute-done.3 = f32[32,256]{1,0:T(8,128)S(1)} collective-permute-done((f32[32,256]{1,0:T(8,128)S(1)}, f32[32,256]{1,0:T(8,128)S(1)}, u32[]{:S(2)}, u32[]{:S(2)}) %collective-permute-start.3) | collective-permute-done | bytes 32800 | tf_op jit(solution)/shard_map/ppermute | solution.py:727
  25.1 0.0 collective-permute-done.2
  25.2 0.1 collective-permute-start.4
  25.3 1.2 %collective-permute-done.4 = f32[64,256]{1,0:T(8,128)S(1)} collective-permute-done((f32[64,256]{1,0:T(8,128)S(1)}, f32[64,256]{1,0:T(8,128)S(1)}, u32[]{:S(2)}, u32[]{:S(2)}) %collective-permute-start.4) | collective-permute-done | bytes 65568 | tf_op jit(solution)/shard_map/ppermute | solution.py:734
  26.5 0.0 collective-permute-done.1
  26.5 0.2 collective-permute-start.8
  26.8 5.1 %collective-permute-start.7 = (f32[64,256]{1,0:T(8,128)S(1)}, f32[64,256]{1,0:T(8,128)S(1)}, u32[]{:S(2)}, u32[]{:S(2)}) collective-permute-start(f32[64,256]{1,0:T(8,128)S(1)} %fusion.refs_0_), channel_id=1, source_target_pairs={{0,6},{1,7},{2,0},{3,1},{4,2},{5,3},{6,4},{7,5},{8,14},{9,15},{10,... | collective-permute-start | bytes 196616 | tf_op jit(solution)/shard_map/ppermute | solution.py:738
  31.9 0.0 collective-permute-start.6
  31.9 1.4 %collective-permute-start.5 = (f32[64,256]{1,0:T(8,128)S(1)}, f32[64,256]{1,0:T(8,128)S(1)}, u32[]{:S(2)}, u32[]{:S(2)}) collective-permute-start(f32[64,256]{1,0:T(8,128)S(1)} %fusion.refs_0_), channel_id=1, source_target_pairs={{0,2},{1,3},{2,4},{3,5},{4,6},{5,7},{6,0},{7,1},{8,10},{9,11},{10,... | collective-permute-start | bytes 196616 | tf_op jit(solution)/shard_map/ppermute | solution.py:738
  33.3 1.9 %collective-permute-done.7.refs_3_ = f32[64,256]{1,0:T(8,128)S(1)} collective-permute-done((f32[64,256]{1,0:T(8,128)S(1)}, f32[64,256]{1,0:T(8,128)S(1)}, u32[]{:S(2)}, u32[]{:S(2)}) %collective-permute-start.7) | collective-permute-done | bytes 65568 | tf_op jit(solution)/shard_map/ppermute | solution.py:738
  35.2 3.0 %collective-permute-done.6.refs_2_ = f32[64,256]{1,0:T(8,128)S(1)} collective-permute-done((f32[64,256]{1,0:T(8,128)S(1)}, f32[64,256]{1,0:T(8,128)S(1)}, u32[]{:S(2)}, u32[]{:S(2)}) %collective-permute-start.6) | collective-permute-done | bytes 65568 | tf_op jit(solution)/shard_map/ppermute | solution.py:738
  38.2 0.4 collective-permute-done.5.refs_1_
  38.6 0.0 copy-done.5
  38.6 0.0 copy-done.7
  38.6 0.0 copy-done.9
  38.6 3.8 %shard_map.125 = (f32[2,240,128]{2,1,0:T(8,128)S(1)}, f32[2,224,128]{2,1,0:T(8,128)S(1)}, f32[3,32,128]{2,1,0:T(8,128)S(1)}, f32[32,128]{1,0:T(8,128)S(1)}) custom-call(f32[64,256]{1,0:T(8,128)S(1)} %fusion.refs_0_, f32[64,256]{1,0:T(8,128)S(1)} %collective-permute-done.5.refs_1_, f32[64,256]{1,0:T(8,128)S(1)} %collective-permute-done.6.refs_2_, ...), custom_call_target="tpu_custom_call" | custom-call | tf_op jit(solution)/shard_map/pallas_call | solution.py:132
  42.4 0.0 collective-permute-done.8
  42.4 0.6 shard_map.126
  43.0 7.4 %shard_map.127 = (f32[32,12288]{1,0:T(8,128)S(1)}, f32[32,256]{1,0:T(8,128)S(1)}) custom-call(f32[2,240,128]{2,1,0:T(8,128)S(1)} %get-tuple-element.29.wk, f32[32,128]{1,0:T(8,128)S(1)} %get-tuple-element.30.after.moment, f32[32,22528]{1,0:T(8,128)S(1)} %get-tuple-element.33.raw, f32[64,128]{1,0:T(8,128)S(1)} %bitcast.13, ...), custom_call_target="tpu_custom_call" | custom-call | tf_op jit(solution)/shard_map/pallas_call | solution.py:132
  50.4 4.3 %collective-permute-start.10 = (f32[32,256]{1,0:T(8,128)S(1)}, f32[32,256]{1,0:T(8,128)S(1)}, u32[]{:S(2)}, u32[]{:S(2)}) collective-permute-start(f32[32,256]{1,0:T(8,128)S(1)} %get-tuple-element.36.after), channel_id=1, source_target_pairs={{8,0},{25,1},{42,2},{59,3},{76,4},{93,5},{110,6},{127,7},{0,8},{17... | collective-permute-start | bytes 98312 | tf_op jit(solution)/shard_map/ppermute | solution.py:727
  54.8 0.7 collective-permute-start.9
  55.4 7.8 %shard_map.128 = (f32[32,13824]{1,0:T(8,128)S(1)}, f32[40,256]{1,0:T(8,128)S(1)}) custom-call(s32[1]{0:T(128)} %bitcast.4.refs_0_.v_ref, f32[144]{0:T(256)S(1)} %copy-done.8, f32[2,8,1152]{2,1,0:T(8,128)S(1)} %copy-done.3, f32[2,224,128]{2,1,0:T(8,128)S(1)} %get-tuple-element.37.wl, f32[3,32,128]{2,1,0:T(8,128)S(1)} %get-tuple-element.38.src, ...), custom_call_target="tpu_custom_call" | custom-call | tf_op jit(solution)/shard_map/pallas_call | solution.py:132
  63.2 0.0 collective-permute-done.10
  63.2 0.0 collective-permute-done.9
  63.3 2.6 %collective-permute-start.11 = (f32[72,256]{1,0:T(8,128)S(1)}, f32[72,256]{1,0:T(8,128)S(1)}, u32[]{:S(2)}, u32[]{:S(2)}) collective-permute-start(f32[72,256]{1,0:T(8,128)S(1)} %pad_maximum_fusion.1), channel_id=1, source_target_pairs={{0,1},{1,0},{2,3},{3,2},{4,5},{5,4},{6,7},{7,6},{8,9},{9,8},{10,11... | collective-permute-start | bytes 221192 | tf_op jit(solution)/shard_map/ppermute | solution.py:734
  65.9 0.9 %collective-permute-done.11 = f32[72,256]{1,0:T(8,128)S(1)} collective-permute-done((f32[72,256]{1,0:T(8,128)S(1)}, f32[72,256]{1,0:T(8,128)S(1)}, u32[]{:S(2)}, u32[]{:S(2)}) %collective-permute-start.11) | collective-permute-done | bytes 73760 | tf_op jit(solution)/shard_map/ppermute | solution.py:734
  66.8 2.6 %collective-permute-start.14 = (f32[72,256]{1,0:T(8,128)S(1)}, f32[72,256]{1,0:T(8,128)S(1)}, u32[]{:S(2)}, u32[]{:S(2)}) collective-permute-start(f32[72,256]{1,0:T(8,128)S(1)} %fusion.1.refs_0_), channel_id=1, source_target_pairs={{0,6},{1,7},{2,0},{3,1},{4,2},{5,3},{6,4},{7,5},{8,14},{9,15},{10,... | collective-permute-start | bytes 221192 | tf_op jit(solution)/shard_map/ppermute | solution.py:738
  69.5 0.6 collective-permute-start.13
  70.1 1.3 %collective-permute-start.12 = (f32[72,256]{1,0:T(8,128)S(1)}, f32[72,256]{1,0:T(8,128)S(1)}, u32[]{:S(2)}, u32[]{:S(2)}) collective-permute-start(f32[72,256]{1,0:T(8,128)S(1)} %fusion.1.refs_0_), channel_id=1, source_target_pairs={{0,2},{1,3},{2,4},{3,5},{4,6},{5,7},{6,0},{7,1},{8,10},{9,11},{10,... | collective-permute-start | bytes 221192 | tf_op jit(solution)/shard_map/ppermute | solution.py:738
  71.4 0.7 collective-permute-done.14.refs_3_
  72.1 3.7 %collective-permute-done.13.refs_2_ = f32[72,256]{1,0:T(8,128)S(1)} collective-permute-done((f32[72,256]{1,0:T(8,128)S(1)}, f32[72,256]{1,0:T(8,128)S(1)}, u32[]{:S(2)}, u32[]{:S(2)}) %collective-permute-start.13) | collective-permute-done | bytes 73760 | tf_op jit(solution)/shard_map/ppermute | solution.py:738
  75.8 0.8 collective-permute-done.12.refs_1_
  76.6 5.5 %shard_map.129 = (f32[2048,128]{1,0:T(8,128)}, f32[32,32]{1,0:T(8,128)}, f32[32,13824]{1,0:T(8,128)}) custom-call(f32[72,256]{1,0:T(8,128)S(1)} %fusion.1.refs_0_, f32[72,256]{1,0:T(8,128)S(1)} %collective-permute-done.12.refs_1_, f32[72,256]{1,0:T(8,128)S(1)} %collective-permute-done.13.refs_2_, f32[72,256]{1,0:T(8,128)S(1)} %collective-permute-done.14.refs_3_, ...), custom_call_target="tpu_custom_call" | custom-call | tf_op jit(solution)/shard_map/pallas_call | solution.py:132
  (7 shorter events, 0.1 us)
Async XLA Ops:
  0.6 3.9 %copy-start.1 = (f32[32,4,16,128]{3,2,1,0:T(8,128)S(1)}, f32[32,4,16,128]{3,2,1,0:T(8,128)}, u32[]{:S(2)}) copy-start(f32[32,4,16,128]{3,2,1,0:T(8,128)} %param.10) | copy-start | bytes 3145732
  0.6 3.9 %copy-start.4 = (f32[4,16,128]{2,1,0:T(8,128)S(1)}, f32[4,16,128]{2,1,0:T(8,128)}, u32[]{:S(2)}) copy-start(f32[4,16,128]{2,1,0:T(8,128)} %param.13) | copy-start | bytes 98308
  1.7 8.1 %collective-permute-start = (f32[32,1,16,128]{3,2,1,0:T(8,128)S(1)}, f32[32,1,16,128]{3,2,1,0:T(8,128)S(1)}, u32[]{:S(2)}, u32[]{:S(2)}) collective-permute-start(f32[32,1,16,128]{3,2,1,0:T(8,128)S(1)} %slice.16), channel_id=1, source_target_pairs={{0,8},{8,16},{16,24},{24,32},{32,40},{40,48},{48,56},{56,64},{64,7... | collective-permute-start | bytes 786440 | tf_op jit(solution)/shard_map/ppermute | solution.py:745
  7.9 7.1 %copy-start = (f32[32,13824]{1,0:T(8,128)S(1)}, f32[32,13824]{1,0:T(8,128)}, u32[]{:S(2)}) copy-start(f32[32,13824]{1,0:T(8,128)} %values.1) | copy-start | bytes 5308420
  7.9 7.1 %copy-start.2 = (f32[2,32,1152]{2,1,0:T(8,128)S(1)}, f32[2,32,1152]{2,1,0:T(8,128)}, u32[]{:S(2)}) copy-start(f32[2,32,1152]{2,1,0:T(8,128)} %constant.34.clone.refs_3_) | copy-start | bytes 884740
  7.9 7.1 %copy-start.3 = (f32[2,8,1152]{2,1,0:T(8,128)S(1)}, f32[2,8,1152]{2,1,0:T(8,128)}, u32[]{:S(2)}) copy-start(f32[2,8,1152]{2,1,0:T(8,128)} %constant.33.clone.refs_2_.rows) | copy-start | bytes 221188
  7.9 7.1 %copy-start.6 = (f32[48,128]{1,0:T(8,128)S(1)}, f32[48,128]{1,0:T(8,128)}, u32[]{:S(2)}) copy-start(f32[48,128]{1,0:T(8,128)} %constant.35.clone.refs_4_) | copy-start | bytes 73732
  7.9 7.1 %copy-start.8 = (f32[144]{0:T(256)S(1)}, f32[144]{0:T(256)}, u32[]{:S(2)}) copy-start(f32[144]{0:T(256)} %constant.32.clone.refs_1_.speeds) | copy-start | bytes 1732
  10.1 16.4 %collective-permute-start.1 = (f32[33,3,16,128]{3,2,1,0:T(8,128)S(1)}, f32[33,3,16,128]{3,2,1,0:T(8,128)S(1)}, u32[]{:S(2)}, u32[]{:S(2)}) collective-permute-start(f32[33,3,16,128]{3,2,1,0:T(8,128)S(1)} %pad_maximum_fusion), channel_id=1, source_target_pairs={{0,8},{1,121},{2,10},{3,123},{4,12},{5,125},{6,14},{7,127},{8,16},... | collective-permute-start | bytes 2433032 | tf_op jit(solution)/shard_map/ppermute | solution.py:763
  11.7 13.4 %collective-permute-start.3 = (f32[32,256]{1,0:T(8,128)S(1)}, f32[32,256]{1,0:T(8,128)S(1)}, u32[]{:S(2)}, u32[]{:S(2)}) collective-permute-start(f32[32,256]{1,0:T(8,128)S(1)} %get-tuple-element.26), channel_id=1, source_target_pairs={{8,0},{25,1},{42,2},{59,3},{76,4},{93,5},{110,6},{127,7},{0,8},{17... | collective-permute-start | bytes 98312 | tf_op jit(solution)/shard_map/ppermute | solution.py:727
  14.3 10.8 %collective-permute-start.2 = (f32[32,256]{1,0:T(8,128)S(1)}, f32[32,256]{1,0:T(8,128)S(1)}, u32[]{:S(2)}, u32[]{:S(2)}) collective-permute-start(f32[32,256]{1,0:T(8,128)S(1)} %get-tuple-element.26), channel_id=1, source_target_pairs={{0,0},{17,1},{34,2},{51,3},{68,4},{85,5},{102,6},{119,7},{8,8},{25... | collective-permute-start | bytes 98312 | tf_op jit(solution)/shard_map/ppermute | solution.py:727
  18.3 20.3 %copy-start.5 = (f32[32,896]{1,0:T(8,128)S(1)}, f32[32,896]{1,0:T(8,128)}, u32[]{:S(2)}) copy-start(f32[32,896]{1,0:T(8,128)} %constant.36.clone.refs_5_) | copy-start | bytes 344068
  18.3 20.3 %copy-start.7 = (f32[32,32]{1,0:T(8,128)S(1)}, f32[32,32]{1,0:T(8,128)}, u32[]{:S(2)}) copy-start(f32[32,32]{1,0:T(8,128)} %refs_4_.5) | copy-start | bytes 12292
  18.3 20.3 %copy-start.9 = (f32[8,128]{1,0:T(8,128)S(1)}, f32[8,128]{1,0:T(8,128)}, u32[]{:S(2)}) copy-start(f32[8,128]{1,0:T(8,128)} %constant.37.clone.refs_6_) | copy-start | bytes 12292
  25.2 1.3 %collective-permute-start.4 = (f32[64,256]{1,0:T(8,128)S(1)}, f32[64,256]{1,0:T(8,128)S(1)}, u32[]{:S(2)}, u32[]{:S(2)}) collective-permute-start(f32[64,256]{1,0:T(8,128)S(1)} %pad_maximum_fusion.2), channel_id=1, source_target_pairs={{0,1},{1,0},{2,3},{3,2},{4,5},{5,4},{6,7},{7,6},{8,9},{9,8},{10,11... | collective-permute-start | bytes 196616 | tf_op jit(solution)/shard_map/ppermute | solution.py:734
  26.5 15.9 %collective-permute-start.8 = (f32[33,3,16,128]{3,2,1,0:T(8,128)S(1)}, f32[33,3,16,128]{3,2,1,0:T(8,128)S(1)}, u32[]{:S(2)}, u32[]{:S(2)}) collective-permute-start(f32[33,3,16,128]{3,2,1,0:T(8,128)S(1)} %collective-permute-done.1), channel_id=1, source_target_pairs={{0,1},{1,0},{2,3},{3,2},{4,5},{5,4},{6,7},{7,6},{8,9},{9,8},{10,11... | collective-permute-start | bytes 2433032 | tf_op jit(solution)/shard_map/ppermute | solution.py:767
  26.8 8.4 %collective-permute-start.7 = (f32[64,256]{1,0:T(8,128)S(1)}, f32[64,256]{1,0:T(8,128)S(1)}, u32[]{:S(2)}, u32[]{:S(2)}) collective-permute-start(f32[64,256]{1,0:T(8,128)S(1)} %fusion.refs_0_), channel_id=1, source_target_pairs={{0,6},{1,7},{2,0},{3,1},{4,2},{5,3},{6,4},{7,5},{8,14},{9,15},{10,... | collective-permute-start | bytes 196616 | tf_op jit(solution)/shard_map/ppermute | solution.py:738
  31.9 6.3 %collective-permute-start.6 = (f32[64,256]{1,0:T(8,128)S(1)}, f32[64,256]{1,0:T(8,128)S(1)}, u32[]{:S(2)}, u32[]{:S(2)}) collective-permute-start(f32[64,256]{1,0:T(8,128)S(1)} %fusion.refs_0_), channel_id=1, source_target_pairs={{0,4},{1,5},{2,6},{3,7},{4,0},{5,1},{6,2},{7,3},{8,12},{9,13},{10,... | collective-permute-start | bytes 196616 | tf_op jit(solution)/shard_map/ppermute | solution.py:738
  31.9 6.7 %collective-permute-start.5 = (f32[64,256]{1,0:T(8,128)S(1)}, f32[64,256]{1,0:T(8,128)S(1)}, u32[]{:S(2)}, u32[]{:S(2)}) collective-permute-start(f32[64,256]{1,0:T(8,128)S(1)} %fusion.refs_0_), channel_id=1, source_target_pairs={{0,2},{1,3},{2,4},{3,5},{4,6},{5,7},{6,0},{7,1},{8,10},{9,11},{10,... | collective-permute-start | bytes 196616 | tf_op jit(solution)/shard_map/ppermute | solution.py:738
  50.4 12.8 %collective-permute-start.10 = (f32[32,256]{1,0:T(8,128)S(1)}, f32[32,256]{1,0:T(8,128)S(1)}, u32[]{:S(2)}, u32[]{:S(2)}) collective-permute-start(f32[32,256]{1,0:T(8,128)S(1)} %get-tuple-element.36.after), channel_id=1, source_target_pairs={{8,0},{25,1},{42,2},{59,3},{76,4},{93,5},{110,6},{127,7},{0,8},{17... | collective-permute-start | bytes 98312 | tf_op jit(solution)/shard_map/ppermute | solution.py:727
  54.8 8.5 %collective-permute-start.9 = (f32[32,256]{1,0:T(8,128)S(1)}, f32[32,256]{1,0:T(8,128)S(1)}, u32[]{:S(2)}, u32[]{:S(2)}) collective-permute-start(f32[32,256]{1,0:T(8,128)S(1)} %get-tuple-element.36.after), channel_id=1, source_target_pairs={{0,0},{17,1},{34,2},{51,3},{68,4},{85,5},{102,6},{119,7},{8,8},{25... | collective-permute-start | bytes 98312 | tf_op jit(solution)/shard_map/ppermute | solution.py:727
  63.3 3.5 %collective-permute-start.11 = (f32[72,256]{1,0:T(8,128)S(1)}, f32[72,256]{1,0:T(8,128)S(1)}, u32[]{:S(2)}, u32[]{:S(2)}) collective-permute-start(f32[72,256]{1,0:T(8,128)S(1)} %pad_maximum_fusion.1), channel_id=1, source_target_pairs={{0,1},{1,0},{2,3},{3,2},{4,5},{5,4},{6,7},{7,6},{8,9},{9,8},{10,11... | collective-permute-start | bytes 221192 | tf_op jit(solution)/shard_map/ppermute | solution.py:734
  66.8 5.3 %collective-permute-start.14 = (f32[72,256]{1,0:T(8,128)S(1)}, f32[72,256]{1,0:T(8,128)S(1)}, u32[]{:S(2)}, u32[]{:S(2)}) collective-permute-start(f32[72,256]{1,0:T(8,128)S(1)} %fusion.1.refs_0_), channel_id=1, source_target_pairs={{0,6},{1,7},{2,0},{3,1},{4,2},{5,3},{6,4},{7,5},{8,14},{9,15},{10,... | collective-permute-start | bytes 221192 | tf_op jit(solution)/shard_map/ppermute | solution.py:738
  69.5 6.4 %collective-permute-start.13 = (f32[72,256]{1,0:T(8,128)S(1)}, f32[72,256]{1,0:T(8,128)S(1)}, u32[]{:S(2)}, u32[]{:S(2)}) collective-permute-start(f32[72,256]{1,0:T(8,128)S(1)} %fusion.1.refs_0_), channel_id=1, source_target_pairs={{0,4},{1,5},{2,6},{3,7},{4,0},{5,1},{6,2},{7,3},{8,12},{9,13},{10,... | collective-permute-start | bytes 221192 | tf_op jit(solution)/shard_map/ppermute | solution.py:738
  70.1 6.5 %collective-permute-start.12 = (f32[72,256]{1,0:T(8,128)S(1)}, f32[72,256]{1,0:T(8,128)S(1)}, u32[]{:S(2)}, u32[]{:S(2)}) collective-permute-start(f32[72,256]{1,0:T(8,128)S(1)} %fusion.1.refs_0_), channel_id=1, source_target_pairs={{0,2},{1,3},{2,4},{3,5},{4,6},{5,7},{6,0},{7,1},{8,10},{9,11},{10,... | collective-permute-start | bytes 221192 | tf_op jit(solution)/shard_map/ppermute | solution.py:738
